TPU v7x, 512 devices: a whole 4x8x8 slice. The times are simulated.
512 devices in a mesh: dp: 64 (over z, y_hi, core), shard: 8 (over y_lo, x).
Axes of the slice: x: 4, y: 8 (y_hi: 4, y_lo: 2; y = y_hi * 2 + y_lo), z: 8, core: 2. Of those that a mesh axis runs over, the one named last changes fastest.
Arguments:
- tokens: bfloat16 [1024, 6144], P('dp', 'shard'), may hold values from -6 to 6
- cotangent: bfloat16 [1024, 6144], P('dp', 'shard'), may hold values from -6 to 6
- slot_token: int32 [1, 256], replicated, may hold values from 0 to 1023, as said below
- slot_gate: float32 [1, 256], replicated, may hold values from 0.1 to 0.9
- w_gate: bfloat16 [1, 6144, 16384], P(None, 'shard', 'dp'), may hold values from -0.078125 to 0.078125
- w_up: bfloat16 [1, 6144, 16384], P(None, 'shard', 'dp'), may hold values from -0.078125 to 0.078125
- w_down: bfloat16 [1, 16384, 6144], P(None, 'dp', 'shard'), may hold values from -0.046875 to 0.046875
Outputs:
- mixed: bfloat16 [1024, 6144], P('dp', 'shard')
- grad_tokens: bfloat16 [1024, 6144], P('dp', 'shard')
- grad_gate: bfloat16 [1, 6144, 16384], P(None, 'shard', 'dp')
- grad_up: bfloat16 [1, 6144, 16384], P(None, 'shard', 'dp')
- grad_down: bfloat16 [1, 16384, 6144], P(None, 'dp', 'shard')
Inputs may be any that keep to these rules, and one draw needn't show every extreme that they name: `slot_token`: each row lists 256 distinct tokens; a token may sit in several rows.
All inputs are finite; a program needn't handle non-finite values.
Results may differ from a plain program's by a relative error of at most 0.006.
Values may be sent and summed in bfloat16 or wider, within the bound.
No kernel may reach another device: no remote copies, remote signals or barrier semaphores. Data moves between devices by JAX's collectives and lax.ppermute only.
A program may use at most 64 MiB of HBM per device.

v0:
```python
import jax
import jax.numpy as jnp
from jax import lax
from jax.sharding import PartitionSpec as P


def side_by_side(arrays, axis, dim, along):
    widths = [a.shape[along] for a in arrays]
    both = jnp.concatenate(arrays, axis=along)
    whole = lax.all_gather(both, axis, axis=dim, tiled=True)
    return tuple(jnp.split(whole, [sum(widths[:k]) for k in range(1, len(widths))], axis=along))


def from_everyone(shard, axis):
    length = lax.axis_size(axis)
    return lax.all_to_all(
        jnp.broadcast_to(shard[None], (length, *shard.shape)), axis, 0, 0, tiled=True
    )


def taken_together(shard, axis):
    everything = from_everyone(shard, axis)
    return jnp.sum(everything, axis=0)


def together(arrays, axis):
    ravelled, at, gathered = (jnp.concatenate([a.reshape(-1) for a in arrays]), 0, [])
    subtotal = taken_together(ravelled, axis)
    for a in arrays:
        gathered.append(subtotal[at : at + a.size].reshape(a.shape))
        at += a.size
    return tuple(gathered)


def cut_along(shard, dim, length):
    before, after = (shard.shape[:dim], shard.shape[dim + 1 :])
    return jnp.moveaxis(shard.reshape(*before, length, -1, *after), dim, 0)


def sent_and_summed(shard, axis, dim):
    tiles = cut_along(shard, dim, lax.axis_size(axis))
    arrived = lax.all_to_all(tiles, axis, split_axis=0, concat_axis=0, tiled=True)
    return arrived.sum(axis=0)


def laid_out(tiles, dim):
    shape = list(tiles.shape[1:])
    shape[dim] *= tiles.shape[0]
    return jnp.moveaxis(tiles, 0, dim).reshape(shape)


def gathered_copies(shard, axis, dim):
    return laid_out(from_everyone(shard, axis), dim)


def combine(summed, factor):
    return jnp.dot(factor, summed.astype(jnp.float32), precision=lax.Precision.HIGHEST).astype(
        jnp.bfloat16
    )


def on_device(tokens, cotangent, slot_token, slot_gate, w_gate, w_up, w_down):
    whole_x, whole_dy = side_by_side((tokens, cotangent), "dp", 0, 1)
    experts, capacity = slot_token.shape
    slot_rows = slot_token.reshape(-1)
    slot_weights = slot_gate.reshape(-1)
    inputs = jnp.take(whole_x, slot_rows, axis=0).reshape(experts, capacity, -1)
    gate_part = jnp.einsum("ecd,edf->ecf", inputs, w_gate, preferred_element_type=jnp.float32)
    up_part = jnp.einsum("ecd,edf->ecf", inputs, w_up, preferred_element_type=jnp.float32)
    gate_pre, up_pre = together((gate_part, up_part), "shard")
    sigmoid_gate = jax.nn.sigmoid(gate_pre)
    hidden = (gate_pre * sigmoid_gate * up_pre).astype(jnp.bfloat16)
    out_part = jnp.einsum("ecf,efd->ecd", hidden, w_down, preferred_element_type=jnp.float32)
    out_part = out_part.reshape(experts * capacity, -1)
    tok_rows = tokens.shape[0]
    owned_ids = lax.axis_index("dp") * tok_rows + jnp.arange(tok_rows, dtype=jnp.int32)
    matches = slot_rows[None, :] == owned_ids[:, None]
    out_factor = jnp.where(matches, slot_weights[None, :], 0.0)
    back_factor = matches.astype(jnp.float32)
    out_share = sent_and_summed(out_part, "dp", 0).astype(jnp.bfloat16)
    out_slots = gathered_copies(out_share, "dp", 0)
    mixed = combine(out_slots, out_factor)
    dy_slots = jnp.take(whole_dy, slot_rows, axis=0).astype(jnp.float32)
    scaled = (slot_weights[:, None] * dy_slots).astype(jnp.bfloat16).reshape(experts, capacity, -1)
    grad_down = jnp.einsum(
        "ecf,ecd->efd", hidden, scaled, preferred_element_type=jnp.float32
    ).astype(jnp.bfloat16)
    grad_part = jnp.einsum("ecd,efd->ecf", scaled, w_down, preferred_element_type=jnp.float32)
    grad_hidden = taken_together(grad_part, "shard")
    grad_gate_pre = (
        grad_hidden * up_pre * sigmoid_gate * (1.0 + gate_pre * (1.0 - sigmoid_gate))
    ).astype(jnp.bfloat16)
    grad_up_pre = (grad_hidden * gate_pre * sigmoid_gate).astype(jnp.bfloat16)
    grad_gate = jnp.einsum(
        "ecd,ecf->edf", inputs, grad_gate_pre, preferred_element_type=jnp.float32
    ).astype(jnp.bfloat16)
    grad_up = jnp.einsum(
        "ecd,ecf->edf", inputs, grad_up_pre, preferred_element_type=jnp.float32
    ).astype(jnp.bfloat16)
    back_part = jnp.einsum(
        "ecf,edf->ecd", grad_gate_pre, w_gate, preferred_element_type=jnp.float32
    ) + jnp.einsum("ecf,edf->ecd", grad_up_pre, w_up, preferred_element_type=jnp.float32)
    back_part = back_part.reshape(experts * capacity, -1)
    back_share = sent_and_summed(back_part, "dp", 0).astype(jnp.bfloat16)
    back_slots = gathered_copies(back_share, "dp", 0)
    grad_tokens = combine(back_slots, back_factor)
    return (mixed, grad_tokens, grad_gate, grad_up, grad_down)


def solution(mesh):
    return jax.shard_map(
        on_device,
        mesh=mesh,
        in_specs=(
            P("dp", "shard"),
            P("dp", "shard"),
            P(),
            P(),
            P(None, "shard", "dp"),
            P(None, "shard", "dp"),
            P(None, "dp", "shard"),
        ),
        out_specs=(
            P("dp", "shard"),
            P("dp", "shard"),
            P(None, "shard", "dp"),
            P(None, "shard", "dp"),
            P(None, "dp", "shard"),
        ),
        check_vma=False,
    )
```

profile of v0, /device:TPU:1, one launch (start us, length us, event | category | flops | bytes accessed | tf_op | source)
XLA Modules:
  0.0 331.3 jit_solution(4917624733578262814)
XLA Ops:
  7.2 0.0 all-gather.2.cloned.1.call-start
  7.2 1.4 pad_maximum_fusion.1
  8.7 0.7 compare_select_fusion.2
  9.4 0.7 compare_and_fusion
  10.0 93.1 %all-gather.2.cloned.1.call-done = bf16[1024,1536]{1,0:T(8,128)(2,1)} async-done(((bf16[16,1536]{1,0:T(8,128)(2,1)}), bf16[1024,1536]{1,0:T(8,128)(2,1)}) %all-gather.2.cloned.1.call-update) | async-done | bytes 3145744 | tf_op jit(solution)/shard_map/all_gather | solution.py:10
  103.2 2.1 fusion.21
  105.3 1.9 gather_fusion.1
  107.2 1.3 fusion.5
  108.6 1.5 broadcast_in_dim.53
  110.1 4.4 %all-to-all-start.3 = ((f32[8,1,256,256]{3,2,1,0:T(8,128)}), f32[8,1,256,256]{3,2,1,0:T(8,128)}, u32[]{:S(2)}, u32[]{:S(2)}) async-start(f32[8,1,256,256]{3,2,1,0:T(8,128)} %broadcast_in_dim.53), calls=%async_computation.3 | async-start | bytes 4194304 | tf_op jit(solution)/shard_map/all_to_all | solution.py:16
  114.5 1.2 gather_fusion
  115.7 0.3 convolution_bitcast_fusion
  116.0 0.1 copy.24
  116.2 0.3 convolution_bitcast_fusion.1
  116.5 0.1 copy.23
  116.7 24.0 %all-to-all-done.3 = f32[8,1,256,256]{3,2,1,0:T(8,128)} async-done(((f32[8,1,256,256]{3,2,1,0:T(8,128)}), f32[8,1,256,256]{3,2,1,0:T(8,128)}, u32[]{:S(2)}, u32[]{:S(2)}) %all-to-all-start.3) | async-done | bytes 2097184 | tf_op jit(solution)/shard_map/all_to_all | solution.py:16
  140.7 4.1 %broadcast_in_dim.51 = f32[8,1,131072]{2,1,0:T(1,128)} broadcast(f32[131072]{0:T(1024)S(1)} %pad_maximum_fusion), dimensions={2} | broadcast | bytes 4718592 | tf_op jit(solution)/shard_map/broadcast_in_dim | solution.py:17
  144.8 4.6 %all-to-all-start = ((f32[8,1,131072]{2,1,0:T(1,128)}), f32[8,1,131072]{2,1,0:T(1,128)}, u32[]{:S(2)}, u32[]{:S(2)}) async-start(f32[8,1,131072]{2,1,0:T(1,128)} %broadcast_in_dim.51), calls=%async_computation | async-start | bytes 8388608 | tf_op jit(solution)/shard_map/all_to_all | solution.py:16
  149.3 1.8 reduce_sum.38
  151.1 46.9 %all-to-all-done = f32[8,1,131072]{2,1,0:T(1,128)} async-done(((f32[8,1,131072]{2,1,0:T(1,128)}), f32[8,1,131072]{2,1,0:T(1,128)}, u32[]{:S(2)}, u32[]{:S(2)}) %all-to-all-start) | async-done | bytes 4194336 | tf_op jit(solution)/shard_map/all_to_all | solution.py:16
  198.0 5.2 %reduce_sum.36 = f32[131072]{0:T(1024)S(1)} reduce(f32[8,1,131072]{2,1,0:T(1,128)} %all-to-all-done, f32[]{:T(128)} %constant.6.clone.1), dimensions={0,1}, to_apply=%region_0.0 | reduce | flops 917504 | bytes 4718596 | tf_op jit(solution)/shard_map/reduce_sum | solution.py:23
  203.3 0.1 slice.35
  203.4 0.1 slice.37
  203.5 0.2 multiply_convert_fusion.1
  203.7 0.3 fusion.3
  203.9 1.4 copy.19
  205.3 9.2 %all-to-all-start.1 = ((f32[64,4,768]{2,1,0:T(4,128)}), f32[64,4,768]{2,1,0:T(4,128)S(1)}, u32[]{:S(2)}, u32[]{:S(2)}) async-start(f32[64,4,768]{2,1,0:T(4,128)} %copy.19), calls=%async_computation.1 | async-start | bytes 1572864 | tf_op jit(solution)/shard_map/all_to_all | solution.py:42
  214.6 0.3 fusion.9
  214.9 0.3 convolution_add_fusion
  215.2 1.1 reshape_reshape.4
  216.3 20.1 %all-to-all-done.1 = f32[64,4,768]{2,1,0:T(4,128)S(1)} async-done(((f32[64,4,768]{2,1,0:T(4,128)}), f32[64,4,768]{2,1,0:T(4,128)S(1)}, u32[]{:S(2)}, u32[]{:S(2)}) %all-to-all-start.1) | async-done | bytes 786464 | tf_op jit(solution)/shard_map/all_to_all | solution.py:42
  236.4 10.2 %all-to-all-start.4 = ((f32[64,4,768]{2,1,0:T(4,128)}), f32[64,4,768]{2,1,0:T(4,128)S(1)}, u32[]{:S(2)}, u32[]{:S(2)}) async-start(f32[64,4,768]{2,1,0:T(4,128)} %reshape_reshape.4), calls=%async_computation.4 | async-start | bytes 1572864 | tf_op jit(solution)/shard_map/all_to_all | solution.py:42
  246.6 0.2 reduce_sum.37
  246.8 25.8 %all-to-all-done.4 = f32[64,4,768]{2,1,0:T(4,128)S(1)} async-done(((f32[64,4,768]{2,1,0:T(4,128)}), f32[64,4,768]{2,1,0:T(4,128)S(1)}, u32[]{:S(2)}, u32[]{:S(2)}) %all-to-all-start.4) | async-done | bytes 786464 | tf_op jit(solution)/shard_map/all_to_all | solution.py:42
  272.6 0.8 broadcast_in_dim.52
  273.5 8.6 %all-to-all-start.2 = ((bf16[64,4,768]{2,1,0:T(4,128)(2,1)}), bf16[64,4,768]{2,1,0:T(4,128)(2,1)S(1)}, u32[]{:S(2)}, u32[]{:S(2)}) async-start(bf16[64,4,768]{2,1,0:T(4,128)(2,1)} %broadcast_in_dim.52), calls=%async_computation.2 | async-start | bytes 786432 | tf_op jit(solution)/shard_map/all_to_all | solution.py:16
  282.1 0.2 reduce_sum.39
  282.3 17.7 %all-to-all-done.2 = bf16[64,4,768]{2,1,0:T(4,128)(2,1)S(1)} async-done(((bf16[64,4,768]{2,1,0:T(4,128)(2,1)}), bf16[64,4,768]{2,1,0:T(4,128)(2,1)S(1)}, u32[]{:S(2)}, u32[]{:S(2)}) %all-to-all-start.2) | async-done | bytes 393248 | tf_op jit(solution)/shard_map/all_to_all | solution.py:16
  300.0 0.8 broadcast_in_dim.54
  300.8 5.4 %all-to-all-start.5 = ((bf16[64,4,768]{2,1,0:T(4,128)(2,1)}), bf16[64,4,768]{2,1,0:T(4,128)(2,1)S(1)}, u32[]{:S(2)}, u32[]{:S(2)}) async-start(bf16[64,4,768]{2,1,0:T(4,128)(2,1)} %broadcast_in_dim.54), calls=%async_computation.5 | async-start | bytes 786432 | tf_op jit(solution)/shard_map/all_to_all | solution.py:16
  306.2 1.1 fusion
  307.4 1.1 fusion.1
  308.5 1.2 fusion.2
  309.6 0.1 reshape.165
  309.8 0.9 convolution_convert_fusion.4
  310.7 12.9 %all-to-all-done.5 = bf16[64,4,768]{2,1,0:T(4,128)(2,1)S(1)} async-done(((bf16[64,4,768]{2,1,0:T(4,128)(2,1)}), bf16[64,4,768]{2,1,0:T(4,128)(2,1)S(1)}, u32[]{:S(2)}, u32[]{:S(2)}) %all-to-all-start.5) | async-done | bytes 393248 | tf_op jit(solution)/shard_map/all_to_all | solution.py:16
  323.6 0.1 reshape.166
  323.7 0.8 convolution_convert_fusion.3
  (18 shorter events, 0.2 us)
Async XLA Ops:
  7.2 100.1 %copy-start = (bf16[1,256,768]{2,1,0:T(8,128)(2,1)S(1)}, bf16[1,256,768]{2,1,0:T(8,128)(2,1)}, u32[]{:S(2)}) copy-start(bf16[1,256,768]{2,1,0:T(8,128)(2,1)} %param.15) | copy-start | bytes 1179652
  7.2 96.0 %all-gather.2.cloned.1.call-start = ((), (), s32[]{:S(2)}) async-start(), calls=%async_computation.6 | async-start | bytes 3194880 | tf_op jit(solution)/shard_map/all_gather | solution.py:10
  105.3 1.9 copy-start.5
  110.1 30.6 %all-to-all-start.3 = ((f32[8,1,256,256]{3,2,1,0:T(8,128)}), f32[8,1,256,256]{3,2,1,0:T(8,128)}, u32[]{:S(2)}, u32[]{:S(2)}) async-start(f32[8,1,256,256]{3,2,1,0:T(8,128)} %broadcast_in_dim.53), calls=%async_computation.3 | async-start | bytes 4194304 | tf_op jit(solution)/shard_map/all_to_all | solution.py:16
  114.5 1.2 copy-start.1
  114.5 1.7 copy-start.2
  144.8 53.2 %all-to-all-start = ((f32[8,1,131072]{2,1,0:T(1,128)}), f32[8,1,131072]{2,1,0:T(1,128)}, u32[]{:S(2)}, u32[]{:S(2)}) async-start(f32[8,1,131072]{2,1,0:T(1,128)} %broadcast_in_dim.51), calls=%async_computation | async-start | bytes 8388608 | tf_op jit(solution)/shard_map/all_to_all | solution.py:16
  205.3 31.0 %all-to-all-start.1 = ((f32[64,4,768]{2,1,0:T(4,128)}), f32[64,4,768]{2,1,0:T(4,128)S(1)}, u32[]{:S(2)}, u32[]{:S(2)}) async-start(f32[64,4,768]{2,1,0:T(4,128)} %copy.19), calls=%async_computation.1 | async-start | bytes 1572864 | tf_op jit(solution)/shard_map/all_to_all | solution.py:42
  236.4 36.3 %all-to-all-start.4 = ((f32[64,4,768]{2,1,0:T(4,128)}), f32[64,4,768]{2,1,0:T(4,128)S(1)}, u32[]{:S(2)}, u32[]{:S(2)}) async-start(f32[64,4,768]{2,1,0:T(4,128)} %reshape_reshape.4), calls=%async_computation.4 | async-start | bytes 1572864 | tf_op jit(solution)/shard_map/all_to_all | solution.py:42
  273.5 26.5 %all-to-all-start.2 = ((bf16[64,4,768]{2,1,0:T(4,128)(2,1)}), bf16[64,4,768]{2,1,0:T(4,128)(2,1)S(1)}, u32[]{:S(2)}, u32[]{:S(2)}) async-start(bf16[64,4,768]{2,1,0:T(4,128)(2,1)} %broadcast_in_dim.52), calls=%async_computation.2 | async-start | bytes 786432 | tf_op jit(solution)/shard_map/all_to_all | solution.py:16
  282.1 26.4 %copy-start.3 = (bf16[256,768]{1,0:T(8,128)(2,1)S(1)}, bf16[256,768]{1,0:T(8,128)(2,1)}, u32[]{:S(2)}) copy-start(bf16[256,768]{1,0:T(8,128)(2,1)} %gather_fusion.1) | copy-start | bytes 1179652
  300.8 22.7 %all-to-all-start.5 = ((bf16[64,4,768]{2,1,0:T(4,128)(2,1)}), bf16[64,4,768]{2,1,0:T(4,128)(2,1)S(1)}, u32[]{:S(2)}, u32[]{:S(2)}) async-start(bf16[64,4,768]{2,1,0:T(4,128)(2,1)} %broadcast_in_dim.54), calls=%async_computation.5 | async-start | bytes 786432 | tf_op jit(solution)/shard_map/all_to_all | solution.py:16
  306.2 3.6 %copy-start.4 = (s32[1,256]{1,0:T(1,128)S(1)}, s32[1,256]{1,0:T(1,128)}, u32[]{:S(2)}) copy-start(s32[1,256]{1,0:T(1,128)} %param.11) | copy-start | bytes 3076
Sparse Core Ops, SparseCore 0:
  11.9 91.2 all-gather.1
where the time goes:
time: 332 us; the launch traced here: 331 us
  waiting for transfers between devices  241 us (73%)
  starting transfers between devices  42.4 us (13%)
  local copies, waits for them, and re-layouts  15.8 us (5%)
  between operations  14.3 us (4%)
  other arithmetic  10.3 us (3%)
  matrix products  8 us (2%)
    all_to_all x4, waiting for transfers between devices, from_everyone(): lax.all_to_all(jnp.broadcast_to(shard[None], (length, *shard.shape)), axi...  101 us
    all_gather x1, waiting for transfers between devices, side_by_side(): whole = lax.all_gather(both, axis, axis=dim, tiled=True)  93.1 us
    all_to_all x2, waiting for transfers between devices, sent_and_summed(): lax.all_to_all(tiles, axis, split_axis=0, concat_axis=0, tiled=True)  45.9 us
    all_to_all x4, starting transfers between devices, from_everyone(): lax.all_to_all(jnp.broadcast_to(shard[None], (length, *shard.shape)), axi...  22.9 us
    all_to_all x2, starting transfers between devices, sent_and_summed(): lax.all_to_all(tiles, axis, split_axis=0, concat_axis=0, tiled=True)  19.5 us
    broadcast_in_dim x4, local copies, waits for them, and re-layouts, from_everyone(): jnp.broadcast_to(shard[None], (length, *shard.shape))  7.32 us
    reduce_sum x2, other arithmetic, taken_together(): return jnp.sum(everything, axis=0)  6.99 us
  transfers between devices with their start and end apart: 7, of which 7 were waited for; matrix products, arithmetic and copies ran while one was open for 4% of the time, Pallas kernels for 0%

commit v1 on v0

v1 whole, which is shorter than its diff:
```python
import jax
import jax.numpy as jnp
from jax import lax
from jax.sharding import Mesh
from jax.sharding import PartitionSpec as P

BF16 = jnp.bfloat16
F32 = jnp.float32
CHIPS = ("z", "yh")
SHARD = ("yl", "x")
DP = ("z", "yh", "core")
SIZES = {"z": 8, "yh": 4, "core": 2, "yl": 2, "x": 4}


def exchange(rows, axes):
    n = lax.axis_size(axes)
    blocks = rows.reshape(n, rows.shape[0] // n, rows.shape[1])
    return lax.all_to_all(blocks, axes, 0, 0, tiled=True)


def spread(rows, axes):
    n = lax.axis_size(axes)
    blocks = jnp.broadcast_to(rows[None], (n, *rows.shape))
    out = lax.all_to_all(blocks, axes, 0, 0, tiled=True)
    return out.reshape(n * rows.shape[0], rows.shape[1])


def swap_core(rows):
    return lax.ppermute(rows, "core", [(0, 1), (1, 0)])


def dot(a, b, dims):
    return lax.dot_general(a, b, (dims, ((), ())), preferred_element_type=F32)


def on_device(tokens, cotangent, slot_token, slot_gate, w_gate, w_up, w_down):
    w_gate, w_up, w_down = w_gate[0], w_up[0], w_down[0]
    slots = slot_token.reshape(-1)
    gates = slot_gate.reshape(-1)
    n_slots = slots.shape[0]
    n_own = tokens.shape[0]
    chip = lax.axis_index(CHIPS)
    core = lax.axis_index("core")
    first = core == 0
    n_chips = lax.axis_size(CHIPS)

    keep = jnp.where(first, tokens, cotangent)
    recv = swap_core(jnp.where(first, cotangent, tokens))
    chip_rows = jnp.concatenate([keep, recv], axis=0)
    local = jnp.arange(n_own, dtype=jnp.int32)
    base = chip * (2 * n_own)
    own_ids = base + core * n_own + local
    other_ids = base + (1 - core) * n_own + local
    chip_ids = jnp.concatenate([own_ids, other_ids])
    pick = (slots[:, None] == chip_ids[None, :]).astype(BF16)

    sent = dot(pick, chip_rows, ((1,), (0,))).astype(BF16)
    mine = jnp.sum(exchange(sent, CHIPS).astype(F32), axis=0)
    per_chip = n_slots // n_chips
    my_gates = lax.dynamic_slice(gates, (chip * per_chip,), (per_chip,))[:, None]
    mine = jnp.where(first, mine, mine * my_gates).astype(BF16)
    rows = spread(mine, CHIPS)
    both = lax.all_gather(rows, "core", axis=0, tiled=False)
    inputs, scaled = both[0], both[1]

    parts = jnp.concatenate(
        [
            dot(inputs, w_gate, ((1,), (0,))).astype(BF16),
            dot(inputs, w_up, ((1,), (0,))).astype(BF16),
            dot(scaled, w_down, ((1,), (1,))).astype(BF16),
        ],
        axis=1,
    )
    sums = jnp.sum(exchange(parts, SHARD).astype(F32), axis=0)
    n_ff = w_gate.shape[1]
    gate_pre, up_pre, grad_hidden = sums[:, :n_ff], sums[:, n_ff : 2 * n_ff], sums[:, 2 * n_ff :]
    s = jax.nn.sigmoid(gate_pre)
    trio = jnp.concatenate(
        [
            (gate_pre * s * up_pre).astype(BF16),
            (grad_hidden * up_pre * s * (1.0 + gate_pre * (1.0 - s))).astype(BF16),
            (grad_hidden * gate_pre * s).astype(BF16),
        ],
        axis=1,
    )
    trio = spread(trio, SHARD)
    hidden, grad_gate_pre, grad_up_pre = trio[:, :n_ff], trio[:, n_ff : 2 * n_ff], trio[:, 2 * n_ff :]

    out_part = dot(hidden, w_down, ((1,), (0,)))
    back_part = dot(grad_gate_pre, w_gate, ((1,), (1,))) + dot(grad_up_pre, w_up, ((1,), (1,)))
    other = swap_core(jnp.where(first, back_part, out_part).astype(BF16))
    total = jnp.where(first, out_part, back_part) + other.astype(F32)
    slot_sum = jnp.sum(exchange(total.astype(BF16), CHIPS).astype(F32), axis=0).astype(BF16)
    slot_sum = jnp.where(first, (my_gates * slot_sum.astype(F32)).astype(BF16), slot_sum)
    slot_rows = spread(slot_sum, CHIPS)
    chip_out = dot(pick, slot_rows, ((0,), (0,))).astype(BF16)
    kept, handed = chip_out[:n_own], chip_out[n_own:]
    got = swap_core(handed)
    mixed = jnp.where(first, kept, got)
    grad_tokens = jnp.where(first, got, kept)

    grad_down = dot(hidden, scaled, ((0,), (0,))).astype(BF16)
    grad_gate = dot(inputs, grad_gate_pre, ((0,), (0,))).astype(BF16)
    grad_up = dot(inputs, grad_up_pre, ((0,), (0,))).astype(BF16)
    return (mixed, grad_tokens, grad_gate[None], grad_up[None], grad_down[None])


def solution(mesh):
    fine = Mesh(mesh.devices.reshape(tuple(SIZES.values())), tuple(SIZES))
    return jax.shard_map(
        on_device,
        mesh=fine,
        in_specs=(
            P(DP, SHARD),
            P(DP, SHARD),
            P(),
            P(),
            P(None, SHARD, DP),
            P(None, SHARD, DP),
            P(None, DP, SHARD),
        ),
        out_specs=(
            P(DP, SHARD),
            P(DP, SHARD),
            P(None, SHARD, DP),
            P(None, SHARD, DP),
            P(None, DP, SHARD),
        ),
        check_vma=False,
    )
```

time: 332 us -> 145 us (0.44)
  waiting for transfers between devices: 241 us -> 29.1 us
  blocking collectives: 0 us -> 67.4 us
  between operations: 14.3 us -> 0.82 us
  local copies, waits for them, and re-layouts: 15.8 us -> 3.8 us
  other arithmetic: 10.3 us -> 2.04 us
  starting transfers between devices: 42.4 us -> 34.9 us
    all_to_all x6 -> x2, waiting for transfers between devices: 147 us -> 27.1 us  [the longest x1 14.4 us: exchange(): return lax.all_to_all(blocks, axes, 0, 0, tiled=True)]
    all_gather x1 -> x0, waiting for transfers between devices: 93.1 us -> none  [side_by_side(): whole = lax.all_gather(both, axis, axis=dim, tiled=True)]
    all_to_all x0 -> x4, blocking collectives: none -> 62.5 us  [the longest x2 31.8 us: exchange(): return lax.all_to_all(blocks, axes, 0, 0, tiled=True)]
    all_to_all x6 -> x2, starting transfers between devices: 42.4 us -> 16.7 us  [the longest x1 10.3 us: exchange(): return lax.all_to_all(blocks, axes, 0, 0, tiled=True)]
    ppermute x0 -> x3, starting transfers between devices: none -> 18.1 us  [swap_core(): return lax.ppermute(rows, 'core', [(0, 1), (1, 0)])]
    reduce_sum x4 -> x3, other arithmetic: 7.3 us -> 0.19 us  [the longest x1 0.07 us: on_device(): jnp.sum(exchange(total.astype(BF16), CHIPS).astype(F32), axis=0)]
    broadcast_in_dim x4 -> x3, local copies, waits for them, and re-layouts: 7.32 us -> 0.83 us  [spread(): blocks = jnp.broadcast_to(rows[None], (n, *rows.shape))]
    all_gather x0 -> x1, blocking collectives: none -> 4.89 us  [on_device(): both = lax.all_gather(rows, 'core', axis=0, tiled=False)]
  transfers between devices with their start and end apart: 7 -> 5, of which waited for: 7 -> 4; matrix products, arithmetic and copies ran while one was open for 4% -> 2% of each run, Pallas kernels for 0% -> 0%
where the time goes in v1:
time: 145 us; the launch traced here: 144 us
  blocking collectives  67.4 us (46%)
  starting transfers between devices  34.9 us (24%)
  waiting for transfers between devices  29.1 us (20%)
  matrix products  6.3 us (4%)
  local copies, waits for them, and re-layouts  3.8 us (3%)
  other arithmetic  2.04 us (1%)
    all_to_all x2, blocking collectives, exchange(): return lax.all_to_all(blocks, axes, 0, 0, tiled=True)  31.8 us
    all_to_all x2, blocking collectives, spread(): out = lax.all_to_all(blocks, axes, 0, 0, tiled=True)  30.7 us
    ppermute x3, starting transfers between devices, swap_core(): return lax.ppermute(rows, 'core', [(0, 1), (1, 0)])  18.1 us
    all_to_all x1, waiting for transfers between devices, exchange(): return lax.all_to_all(blocks, axes, 0, 0, tiled=True)  14.4 us
    all_to_all x1, waiting for transfers between devices, spread(): out = lax.all_to_all(blocks, axes, 0, 0, tiled=True)  12.7 us
    all_to_all x1, starting transfers between devices, exchange(): return lax.all_to_all(blocks, axes, 0, 0, tiled=True)  10.3 us
    all_to_all x1, starting transfers between devices, spread(): out = lax.all_to_all(blocks, axes, 0, 0, tiled=True)  6.39 us
    dot_general x11, matrix products, dot(): return lax.dot_general(a, b, (dims, ((), ())), preferred_element_type=F32)  6.3 us
  transfers between devices with their start and end apart: 5, of which 4 were waited for; matrix products, arithmetic and copies ran while one was open for 2% of the time, Pallas kernels for 0%

profile of v1, /device:TPU:1, one launch (start us, length us, event | category | flops | bytes accessed | tf_op | source)
XLA Modules:
  0.0 144.3 jit_solution(2298697582286622835)
XLA Ops:
  0.6 0.0 copy-start
  0.7 0.8 broadcast_select_fusion.3
  1.5 8.7 %collective-permute-start = (bf16[16,768]{1,0:T(8,128)(2,1)S(1)}, bf16[16,768]{1,0:T(8,128)(2,1)S(1)}, u32[]{:S(2)}, u32[]{:S(2)}) collective-permute-start(bf16[16,768]{1,0:T(8,128)(2,1)S(1)} %get-tuple-element.11), channel_id=1, source_target_pairs={{0,8},{8,0},{1,9},{9,1},{2,10},{10,2},{3,11},{11,3},{4,12},{12,4},... | collective-permute-start | bytes 73736 | tf_op jit(solution)/shard_map/ppermute | solution.py:29
  10.2 0.1 pad_add_fusion
  10.3 0.7 collective-permute-done
  11.0 0.0 copy-start.3
  11.0 0.7 copy-done.3
  11.7 1.1 fusion
  12.8 10.3 %all-to-all-start = ((bf16[32,8,768]{2,1,0:T(8,128)(2,1)}), bf16[32,8,768]{2,1,0:T(8,128)(2,1)S(1)}, u32[]{:S(2)}, u32[]{:S(2)}) async-start(bf16[32,8,768]{2,1,0:T(8,128)(2,1)} %fusion), calls=%async_computation | async-start | bytes 786432 | tf_op jit(solution)/shard_map/all_to_all | solution.py:18
  23.1 0.0 copy-start.4
  23.1 0.7 copy-done.4
  23.8 0.1 dynamic-slice_bitcast_fusion
  23.9 14.4 %all-to-all-done = bf16[32,8,768]{2,1,0:T(8,128)(2,1)S(1)} async-done(((bf16[32,8,768]{2,1,0:T(8,128)(2,1)}), bf16[32,8,768]{2,1,0:T(8,128)(2,1)S(1)}, u32[]{:S(2)}, u32[]{:S(2)}) %all-to-all-start) | async-done | bytes 393248 | tf_op jit(solution)/shard_map/all_to_all | solution.py:18
  38.3 0.1 convert_reduce_fusion.1
  38.3 0.1 fusion.29
  38.4 20.9 %all_to_all.30 = bf16[32,8,768]{2,1,0:T(8,128)(2,1)S(1)} all-to-all(bf16[32,8,768]{2,1,0:T(8,128)(2,1)S(1)} %broadcast_in_dim.12), channel_id=1, replica_groups=mesh['z'=8,'yh'=4,'core'=2,'yl'=2,'x'=4] {'z','yh'}, dimensions={0} | all-to-all | bytes 786432 | tf_op jit(solution)/shard_map/all_to_all | solution.py:24
  59.3 4.9 %all_gather.3 = bf16[2,256,768]{2,1,0:T(8,128)(2,1)S(1)} all-gather(bf16[1,256,768]{2,1,0:T(8,128)(2,1)S(1)} %bitcast.53), channel_id=1, replica_groups=mesh['z'=8,'yh'=4,'core'=2,'yl'=2,'x'=4] {'core'}, dimensions={0}, use_global_device_ids=true | all-gather | bytes 1179648 | tf_op jit(solution)/shard_map/all_gather | solution.py:63
  64.2 0.0 copy-done
  64.2 0.0 copy-start.2
  64.2 0.3 convolution_convert_fusion.5
  64.6 0.7 copy-done.2
  65.2 0.0 copy-start.1
  65.2 0.3 convolution_convert_fusion.4
  65.5 0.7 copy-done.1
  66.2 0.3 convolution_convert_fusion.6
  66.6 0.2 copy.13
  66.8 11.6 %all_to_all.31 = bf16[8,32,768]{2,1,0:T(8,128)(2,1)S(1)} all-to-all(bf16[8,32,768]{2,1,0:T(8,128)(2,1)S(1)} %bitcast.52), channel_id=1, replica_groups=mesh['z'=8,'yh'=4,'core'=2,'yl'=2,'x'=4] {'yl','x'}, dimensions={0} | all-to-all | bytes 786432 | tf_op jit(solution)/shard_map/all_to_all | solution.py:18
  78.4 0.1 convert_reduce_fusion
  78.5 9.8 %all_to_all.32 = bf16[8,32,768]{2,1,0:T(8,128)(2,1)S(1)} all-to-all(bf16[8,32,768]{2,1,0:T(8,128)(2,1)S(1)} %broadcast_in_dim.13), channel_id=1, replica_groups=mesh['z'=8,'yh'=4,'core'=2,'yl'=2,'x'=4] {'yl','x'}, dimensions={0} | all-to-all | bytes 786432 | tf_op jit(solution)/shard_map/all_to_all | solution.py:24
  88.3 0.3 fusion.6
  88.6 0.3 fusion.11
  88.9 0.3 select_convert_fusion
  89.2 4.7 %collective-permute-start.1 = (bf16[256,768]{1,0:T(8,128)(2,1)S(1)}, bf16[256,768]{1,0:T(8,128)(2,1)S(1)}, u32[]{:S(2)}, u32[]{:S(2)}) collective-permute-start(bf16[256,768]{1,0:T(8,128)(2,1)S(1)} %get-tuple-element.12), channel_id=1, source_target_pairs={{0,8},{8,0},{1,9},{9,1},{2,10},{10,2},{3,11},{11,3},{4,12},{12,4},... | collective-permute-start | bytes 1179656 | tf_op jit(solution)/shard_map/ppermute | solution.py:29
  93.9 1.3 collective-permute-done.1
  95.2 0.1 fusion.4
  95.3 20.2 %all_to_all.33 = bf16[32,8,768]{2,1,0:T(8,128)(2,1)S(1)} all-to-all(bf16[32,8,768]{2,1,0:T(8,128)(2,1)S(1)} %fusion.4), channel_id=1, replica_groups=mesh['z'=8,'yh'=4,'core'=2,'yl'=2,'x'=4] {'z','yh'}, dimensions={0} | all-to-all | bytes 786432 | tf_op jit(solution)/shard_map/all_to_all | solution.py:18
  115.5 0.1 reduce_sum.32
  115.6 0.1 fusion.30
  115.6 0.8 broadcast_in_dim.14
  116.4 6.4 %all-to-all-start.5 = ((bf16[32,8,768]{2,1,0:T(8,128)(2,1)}), bf16[32,8,768]{2,1,0:T(8,128)(2,1)S(1)}, u32[]{:S(2)}, u32[]{:S(2)}) async-start(bf16[32,8,768]{2,1,0:T(8,128)(2,1)} %broadcast_in_dim.14), calls=%async_computation.5 | async-start | bytes 786432 | tf_op jit(solution)/shard_map/all_to_all | solution.py:24
  122.8 1.1 fusion.1
  123.9 1.1 fusion.2
  124.9 12.7 %all-to-all-done.5 = bf16[32,8,768]{2,1,0:T(8,128)(2,1)S(1)} async-done(((bf16[32,8,768]{2,1,0:T(8,128)(2,1)}), bf16[32,8,768]{2,1,0:T(8,128)(2,1)S(1)}, u32[]{:S(2)}, u32[]{:S(2)}) %all-to-all-start.5) | async-done | bytes 393248 | tf_op jit(solution)/shard_map/all_to_all | solution.py:24
  137.6 0.3 convolution_convert_fusion.7
  137.9 4.7 %collective-permute-start.2 = (bf16[16,768]{1,0:T(8,128)(2,1)S(1)}, bf16[16,768]{1,0:T(8,128)(2,1)S(1)}, u32[]{:S(2)}, u32[]{:S(2)}) collective-permute-start(bf16[16,768]{1,0:T(8,128)(2,1)S(1)} %slice.49), channel_id=1, source_target_pairs={{0,8},{8,0},{1,9},{9,1},{2,10},{10,2},{3,11},{11,3},{4,12},{12,4},... | collective-permute-start | bytes 73736 | tf_op jit(solution)/shard_map/ppermute | solution.py:29
  142.7 1.1 fusion.3
  143.7 0.0 collective-permute-done.2
  143.7 0.6 broadcast_select_fusion
  (7 shorter events, 0.1 us)
Async XLA Ops:
  0.6 63.6 %copy-start = (bf16[1,768,256]{2,1,0:T(8,128)(2,1)S(1)}, bf16[1,768,256]{2,1,0:T(8,128)(2,1)}, u32[]{:S(2)}) copy-start(bf16[1,768,256]{2,1,0:T(8,128)(2,1)} %param.12) | copy-start | bytes 1179652
  1.5 9.6 %collective-permute-start = (bf16[16,768]{1,0:T(8,128)(2,1)S(1)}, bf16[16,768]{1,0:T(8,128)(2,1)S(1)}, u32[]{:S(2)}, u32[]{:S(2)}) collective-permute-start(bf16[16,768]{1,0:T(8,128)(2,1)S(1)} %get-tuple-element.11), channel_id=1, source_target_pairs={{0,8},{8,0},{1,9},{9,1},{2,10},{10,2},{3,11},{11,3},{4,12},{12,4},... | collective-permute-start | bytes 73736 | tf_op jit(solution)/shard_map/ppermute | solution.py:29
  11.0 0.7 copy-start.3
  12.8 25.5 %all-to-all-start = ((bf16[32,8,768]{2,1,0:T(8,128)(2,1)}), bf16[32,8,768]{2,1,0:T(8,128)(2,1)S(1)}, u32[]{:S(2)}, u32[]{:S(2)}) async-start(bf16[32,8,768]{2,1,0:T(8,128)(2,1)} %fusion), calls=%async_computation | async-start | bytes 786432 | tf_op jit(solution)/shard_map/all_to_all | solution.py:18
  23.1 0.7 copy-start.4
  64.2 1.0 copy-start.2
  65.2 1.0 copy-start.1
  89.2 6.0 %collective-permute-start.1 = (bf16[256,768]{1,0:T(8,128)(2,1)S(1)}, bf16[256,768]{1,0:T(8,128)(2,1)S(1)}, u32[]{:S(2)}, u32[]{:S(2)}) collective-permute-start(bf16[256,768]{1,0:T(8,128)(2,1)S(1)} %get-tuple-element.12), channel_id=1, source_target_pairs={{0,8},{8,0},{1,9},{9,1},{2,10},{10,2},{3,11},{11,3},{4,12},{12,4},... | collective-permute-start | bytes 1179656 | tf_op jit(solution)/shard_map/ppermute | solution.py:29
  116.4 21.2 %all-to-all-start.5 = ((bf16[32,8,768]{2,1,0:T(8,128)(2,1)}), bf16[32,8,768]{2,1,0:T(8,128)(2,1)S(1)}, u32[]{:S(2)}, u32[]{:S(2)}) async-start(bf16[32,8,768]{2,1,0:T(8,128)(2,1)} %broadcast_in_dim.14), calls=%async_computation.5 | async-start | bytes 786432 | tf_op jit(solution)/shard_map/all_to_all | solution.py:24
  137.9 5.8 %collective-permute-start.2 = (bf16[16,768]{1,0:T(8,128)(2,1)S(1)}, bf16[16,768]{1,0:T(8,128)(2,1)S(1)}, u32[]{:S(2)}, u32[]{:S(2)}) collective-permute-start(bf16[16,768]{1,0:T(8,128)(2,1)S(1)} %slice.49), channel_id=1, source_target_pairs={{0,8},{8,0},{1,9},{9,1},{2,10},{10,2},{3,11},{11,3},{4,12},{12,4},... | collective-permute-start | bytes 73736 | tf_op jit(solution)/shard_map/ppermute | solution.py:29

commit v2 on v1

--- a/solution.py
+++ b/solution.py
@@ -52,12 +52,23 @@
     own_ids = base + core * n_own + local
     other_ids = base + (1 - core) * n_own + local
     chip_ids = jnp.concatenate([own_ids, other_ids])
-    pick = (slots[:, None] == chip_ids[None, :]).astype(BF16)
 
+    rank_here = jnp.sum((slots[:, None] < chip_ids[None, :]).astype(jnp.int32), axis=0)
+    in_slot = jnp.max((slots[:, None] == chip_ids[None, :]).astype(jnp.int32), axis=0)
+    peers = jnp.arange(n_chips, dtype=jnp.int32)
+    lane = jnp.where(in_slot > 0, rank_here % n_chips, -1)
+    pick = (peers[:, None] == lane[None, :]).astype(BF16)
     sent = dot(pick, chip_rows, ((1,), (0,))).astype(BF16)
-    mine = jnp.sum(exchange(sent, CHIPS).astype(F32), axis=0)
+    arrived = lax.all_to_all(sent, CHIPS, 0, 0, tiled=True)
+
     per_chip = n_slots // n_chips
-    my_gates = lax.dynamic_slice(gates, (chip * per_chip,), (per_chip,))[:, None]
+    ranks = jnp.sum((slots[:, None] < slots[None, :]).astype(jnp.int32), axis=0)
+    my_ranks = chip + n_chips * jnp.arange(per_chip, dtype=jnp.int32)
+    match = ranks[None, :] == my_ranks[:, None]
+    my_tokens = jnp.sum(jnp.where(match, slots[None, :], 0), axis=1)
+    my_gates = jnp.sum(jnp.where(match, gates[None, :], 0.0), axis=1)[:, None]
+    place = ((my_tokens // (2 * n_own))[:, None] == peers[None, :]).astype(BF16)
+    mine = dot(place, arrived, ((1,), (0,)))
     mine = jnp.where(first, mine, mine * my_gates).astype(BF16)
     rows = spread(mine, CHIPS)
     both = lax.all_gather(rows, "core", axis=0, tiled=False)
@@ -90,10 +101,12 @@
     back_part = dot(grad_gate_pre, w_gate, ((1,), (1,))) + dot(grad_up_pre, w_up, ((1,), (1,)))
     other = swap_core(jnp.where(first, back_part, out_part).astype(BF16))
     total = jnp.where(first, out_part, back_part) + other.astype(F32)
-    slot_sum = jnp.sum(exchange(total.astype(BF16), CHIPS).astype(F32), axis=0).astype(BF16)
-    slot_sum = jnp.where(first, (my_gates * slot_sum.astype(F32)).astype(BF16), slot_sum)
-    slot_rows = spread(slot_sum, CHIPS)
-    chip_out = dot(pick, slot_rows, ((0,), (0,))).astype(BF16)
+    slot_sum = jnp.sum(exchange(total.astype(BF16), CHIPS).astype(F32), axis=0)
+    slot_sum = lax.reduce_precision(slot_sum, 8, 7)
+    slot_sum = jnp.where(first, my_gates * slot_sum, slot_sum).astype(BF16)
+    back = dot(place, slot_sum, ((0,), (0,))).astype(BF16)
+    returned = lax.all_to_all(back, CHIPS, 0, 0, tiled=True)
+    chip_out = dot(pick, returned, ((0,), (0,))).astype(BF16)
     kept, handed = chip_out[:n_own], chip_out[n_own:]
     got = swap_core(handed)
     mixed = jnp.where(first, kept, got)

time: 145 us -> 137 us (0.945)
  blocking collectives: 67.4 us -> 43.9 us
  waiting for transfers between devices: 29.1 us -> 35.8 us
  starting transfers between devices: 34.9 us -> 40.2 us
  other arithmetic: 2.04 us -> 4.57 us
    all_to_all x2 -> x1, blocking collectives: 31.8 us -> 11.6 us  [exchange(): return lax.all_to_all(blocks, axes, 0, 0, tiled=True)]
    all_to_all x1 -> x2, starting transfers between devices: 6.39 us -> 16.7 us  [the longest x1 10.3 us: on_device(): arrived = lax.all_to_all(sent, CHIPS, 0, 0, tiled=True)]
    all_to_all x1 -> x2, waiting for transfers between devices: 12.7 us -> 20.3 us  [the longest x1 10.3 us: on_device(): arrived = lax.all_to_all(sent, CHIPS, 0, 0, tiled=True)]
    all_to_all x1, starting transfers between devices: 10.3 us -> 5.45 us  [exchange(): return lax.all_to_all(blocks, axes, 0, 0, tiled=True)]
    all_to_all x2, blocking collectives: 30.7 us -> 28.3 us  [spread(): out = lax.all_to_all(blocks, axes, 0, 0, tiled=True)]
    unnamed x10 -> x14, local copies, waits for them, and re-layouts: 2.72 us -> 4.08 us
    dot_general x11 -> x13, matrix products: 6.3 us -> 5.74 us  [dot(): return lax.dot_general(a, b, (dims, ((), ())), preferred_element_type=F32)]
  transfers between devices with their start and end apart: 5 -> 6, of which waited for: 4 -> 4; matrix products, arithmetic and copies ran while one was open for 2% -> 3% of each run, Pallas kernels for 0% -> 0%
where the time goes in v2:
time: 137 us; the launch traced here: 136 us
  blocking collectives  43.9 us (32%)
  starting transfers between devices  40.2 us (29%)
  waiting for transfers between devices  35.8 us (26%)
  matrix products  5.74 us (4%)
  local copies, waits for them, and re-layouts  4.83 us (4%)
  other arithmetic  4.57 us (3%)
    all_to_all x2, blocking collectives, spread(): out = lax.all_to_all(blocks, axes, 0, 0, tiled=True)  28.3 us
    ppermute x3, starting transfers between devices, swap_core(): return lax.ppermute(rows, 'core', [(0, 1), (1, 0)])  18.1 us
    all_to_all x1, waiting for transfers between devices, exchange(): return lax.all_to_all(blocks, axes, 0, 0, tiled=True)  14.1 us
    all_to_all x1, blocking collectives, exchange(): return lax.all_to_all(blocks, axes, 0, 0, tiled=True)  11.6 us
    all_to_all x1, starting transfers between devices, on_device(): arrived = lax.all_to_all(sent, CHIPS, 0, 0, tiled=True)  10.3 us
    all_to_all x1, waiting for transfers between devices, on_device(): arrived = lax.all_to_all(sent, CHIPS, 0, 0, tiled=True)  10.3 us
    all_to_all x1, waiting for transfers between devices, on_device(): returned = lax.all_to_all(back, CHIPS, 0, 0, tiled=True)  10 us
    all_to_all x1, starting transfers between devices, on_device(): returned = lax.all_to_all(back, CHIPS, 0, 0, tiled=True)  6.37 us
  transfers between devices with their start and end apart: 6, of which 4 were waited for; matrix products, arithmetic and copies ran while one was open for 3% of the time, Pallas kernels for 0%

profile of v2, /device:TPU:1, one launch (start us, length us, event | category | flops | bytes accessed | tf_op | source)
XLA Modules:
  0.0 136.0 jit_solution(13497545580567235479)
XLA Ops:
  0.6 0.0 copy-start
  0.7 0.8 broadcast_select_fusion.3
  1.5 8.7 %collective-permute-start = (bf16[16,768]{1,0:T(8,128)(2,1)S(1)}, bf16[16,768]{1,0:T(8,128)(2,1)S(1)}, u32[]{:S(2)}, u32[]{:S(2)}) collective-permute-start(bf16[16,768]{1,0:T(8,128)(2,1)S(1)} %get-tuple-element.13), channel_id=1, source_target_pairs={{0,8},{8,0},{1,9},{9,1},{2,10},{10,2},{3,11},{11,3},{4,12},{12,4},... | collective-permute-start | bytes 73736 | tf_op jit(solution)/shard_map/ppermute | solution.py:29
  10.2 0.7 copy-done.3
  10.9 0.1 convert_reduce_fusion.2
  11.0 0.1 pad_add_fusion
  11.1 0.2 convert_reduce_fusion.3
  11.3 0.2 fusion.37
  11.5 0.1 fusion.4
  11.7 0.5 broadcast.98
  12.2 0.7 reduce
  12.8 0.6 reshape.71
  13.5 10.3 %all-to-all-start = ((bf16[32,2,384]{2,1,0:T(2,128)(2,1)}), bf16[32,2,384]{2,1,0:T(2,128)(2,1)S(1)}, u32[]{:S(2)}, u32[]{:S(2)}) async-start(bf16[32,2,384]{2,1,0:T(2,128)(2,1)} %reshape.71), calls=%async_computation | async-start | bytes 98304 | tf_op jit(solution)/shard_map/all_to_all | solution.py:62
  23.8 0.7 copy-done.4
  24.5 0.2 fusion.38
  24.7 10.3 %all-to-all-done = bf16[32,2,384]{2,1,0:T(2,128)(2,1)S(1)} async-done(((bf16[32,2,384]{2,1,0:T(2,128)(2,1)}), bf16[32,2,384]{2,1,0:T(2,128)(2,1)S(1)}, u32[]{:S(2)}, u32[]{:S(2)}) %all-to-all-start) | async-done | bytes 49184 | tf_op jit(solution)/shard_map/all_to_all | solution.py:62
  35.0 0.2 fusion.30
  35.3 18.5 %all_to_all.44 = bf16[32,8,768]{2,1,0:T(8,128)(2,1)S(1)} all-to-all(bf16[32,8,768]{2,1,0:T(8,128)(2,1)S(1)} %broadcast_in_dim.66), channel_id=1, replica_groups=mesh['z'=8,'yh'=4,'core'=2,'yl'=2,'x'=4] {'z','yh'}, dimensions={0} | all-to-all | bytes 786432 | tf_op jit(solution)/shard_map/all_to_all | solution.py:24
  53.8 4.1 %all_gather.3 = bf16[2,256,768]{2,1,0:T(8,128)(2,1)S(1)} all-gather(bf16[1,256,768]{2,1,0:T(8,128)(2,1)S(1)} %bitcast.61), channel_id=1, replica_groups=mesh['z'=8,'yh'=4,'core'=2,'yl'=2,'x'=4] {'core'}, dimensions={0}, use_global_device_ids=true | all-gather | bytes 1179648 | tf_op jit(solution)/shard_map/all_gather | solution.py:74
  57.8 0.3 convolution_convert_fusion.4
  58.1 0.7 copy-done.2
  58.8 0.3 convolution_convert_fusion.3
  59.1 0.7 copy-done.1
  59.8 0.3 convolution_convert_fusion.5
  60.2 0.2 copy.20
  60.3 11.6 %all_to_all.45 = bf16[8,32,768]{2,1,0:T(8,128)(2,1)S(1)} all-to-all(bf16[8,32,768]{2,1,0:T(8,128)(2,1)S(1)} %bitcast.60), channel_id=1, replica_groups=mesh['z'=8,'yh'=4,'core'=2,'yl'=2,'x'=4] {'yl','x'}, dimensions={0} | all-to-all | bytes 786432 | tf_op jit(solution)/shard_map/all_to_all | solution.py:18
  71.9 0.1 convert_reduce_fusion.1
  72.1 9.8 %all_to_all.46 = bf16[8,32,768]{2,1,0:T(8,128)(2,1)S(1)} all-to-all(bf16[8,32,768]{2,1,0:T(8,128)(2,1)S(1)} %broadcast_in_dim.67), channel_id=1, replica_groups=mesh['z'=8,'yh'=4,'core'=2,'yl'=2,'x'=4] {'yl','x'}, dimensions={0} | all-to-all | bytes 786432 | tf_op jit(solution)/shard_map/all_to_all | solution.py:24
  81.9 0.3 fusion.6
  82.2 0.3 fusion.11
  82.5 0.3 select_convert_fusion
  82.8 4.7 %collective-permute-start.1 = (bf16[256,768]{1,0:T(8,128)(2,1)S(1)}, bf16[256,768]{1,0:T(8,128)(2,1)S(1)}, u32[]{:S(2)}, u32[]{:S(2)}) collective-permute-start(bf16[256,768]{1,0:T(8,128)(2,1)S(1)} %get-tuple-element.14), channel_id=1, source_target_pairs={{0,8},{8,0},{1,9},{9,1},{2,10},{10,2},{3,11},{11,3},{4,12},{12,4},... | collective-permute-start | bytes 1179656 | tf_op jit(solution)/shard_map/ppermute | solution.py:29
  87.4 1.3 collective-permute-done.1
  88.8 0.9 fusion.5
  89.6 5.4 %all-to-all-start.4 = ((bf16[32,8,768]{2,1,0:T(8,128)(2,1)}), bf16[32,8,768]{2,1,0:T(8,128)(2,1)S(1)}, u32[]{:S(2)}, u32[]{:S(2)}) async-start(bf16[32,8,768]{2,1,0:T(8,128)(2,1)} %fusion.5), calls=%async_computation.4 | async-start | bytes 786432 | tf_op jit(solution)/shard_map/all_to_all | solution.py:18
  95.1 1.1 fusion
  96.2 14.1 %all-to-all-done.4 = bf16[32,8,768]{2,1,0:T(8,128)(2,1)S(1)} async-done(((bf16[32,8,768]{2,1,0:T(8,128)(2,1)}), bf16[32,8,768]{2,1,0:T(8,128)(2,1)S(1)}, u32[]{:S(2)}, u32[]{:S(2)}) %all-to-all-start.4) | async-done | bytes 393248 | tf_op jit(solution)/shard_map/all_to_all | solution.py:18
  110.2 0.1 convert_reduce_fusion
  110.3 0.3 fusion.3
  110.6 0.7 reduce.1
  111.2 0.6 reshape.73
  111.9 6.4 %all-to-all-start.5 = ((bf16[32,2,384]{2,1,0:T(2,128)(2,1)}), bf16[32,2,384]{2,1,0:T(2,128)(2,1)S(1)}, u32[]{:S(2)}, u32[]{:S(2)}) async-start(bf16[32,2,384]{2,1,0:T(2,128)(2,1)} %reshape.73), calls=%async_computation.5 | async-start | bytes 98304 | tf_op jit(solution)/shard_map/all_to_all | solution.py:108
  118.3 1.1 fusion.1
  119.3 10.0 %all-to-all-done.5 = bf16[32,2,384]{2,1,0:T(2,128)(2,1)S(1)} async-done(((bf16[32,2,384]{2,1,0:T(2,128)(2,1)}), bf16[32,2,384]{2,1,0:T(2,128)(2,1)S(1)}, u32[]{:S(2)}, u32[]{:S(2)}) %all-to-all-start.5) | async-done | bytes 49184 | tf_op jit(solution)/shard_map/all_to_all | solution.py:108
  129.4 0.2 convolution_convert_fusion.7
  129.6 4.7 %collective-permute-start.2 = (bf16[16,768]{1,0:T(8,128)(2,1)S(1)}, bf16[16,768]{1,0:T(8,128)(2,1)S(1)}, u32[]{:S(2)}, u32[]{:S(2)}) collective-permute-start(bf16[16,768]{1,0:T(8,128)(2,1)S(1)} %slice.49), channel_id=1, source_target_pairs={{0,8},{8,0},{1,9},{9,1},{2,10},{10,2},{3,11},{11,3},{4,12},{12,4},... | collective-permute-start | bytes 73736 | tf_op jit(solution)/shard_map/ppermute | solution.py:29
  134.3 1.1 fusion.2
  135.3 0.6 broadcast_select_fusion
  (19 shorter events, 0.3 us)
Async XLA Ops:
  0.6 57.2 %copy-start = (bf16[1,768,256]{2,1,0:T(8,128)(2,1)S(1)}, bf16[1,768,256]{2,1,0:T(8,128)(2,1)}, u32[]{:S(2)}) copy-start(bf16[1,768,256]{2,1,0:T(8,128)(2,1)} %param.12) | copy-start | bytes 1179652
  1.5 10.1 %collective-permute-start = (bf16[16,768]{1,0:T(8,128)(2,1)S(1)}, bf16[16,768]{1,0:T(8,128)(2,1)S(1)}, u32[]{:S(2)}, u32[]{:S(2)}) collective-permute-start(bf16[16,768]{1,0:T(8,128)(2,1)S(1)} %get-tuple-element.13), channel_id=1, source_target_pairs={{0,8},{8,0},{1,9},{9,1},{2,10},{10,2},{3,11},{11,3},{4,12},{12,4},... | collective-permute-start | bytes 73736 | tf_op jit(solution)/shard_map/ppermute | solution.py:29
  10.2 0.7 copy-start.3
  13.5 21.5 %all-to-all-start = ((bf16[32,2,384]{2,1,0:T(2,128)(2,1)}), bf16[32,2,384]{2,1,0:T(2,128)(2,1)S(1)}, u32[]{:S(2)}, u32[]{:S(2)}) async-start(bf16[32,2,384]{2,1,0:T(2,128)(2,1)} %reshape.71), calls=%async_computation | async-start | bytes 98304 | tf_op jit(solution)/shard_map/all_to_all | solution.py:62
  23.8 0.7 copy-start.4
  57.8 1.0 copy-start.2
  58.8 1.0 copy-start.1
  82.8 6.0 %collective-permute-start.1 = (bf16[256,768]{1,0:T(8,128)(2,1)S(1)}, bf16[256,768]{1,0:T(8,128)(2,1)S(1)}, u32[]{:S(2)}, u32[]{:S(2)}) collective-permute-start(bf16[256,768]{1,0:T(8,128)(2,1)S(1)} %get-tuple-element.14), channel_id=1, source_target_pairs={{0,8},{8,0},{1,9},{9,1},{2,10},{10,2},{3,11},{11,3},{4,12},{12,4},... | collective-permute-start | bytes 1179656 | tf_op jit(solution)/shard_map/ppermute | solution.py:29
  89.6 20.6 %all-to-all-start.4 = ((bf16[32,8,768]{2,1,0:T(8,128)(2,1)}), bf16[32,8,768]{2,1,0:T(8,128)(2,1)S(1)}, u32[]{:S(2)}, u32[]{:S(2)}) async-start(bf16[32,8,768]{2,1,0:T(8,128)(2,1)} %fusion.5), calls=%async_computation.4 | async-start | bytes 786432 | tf_op jit(solution)/shard_map/all_to_all | solution.py:18
  111.9 17.5 %all-to-all-start.5 = ((bf16[32,2,384]{2,1,0:T(2,128)(2,1)}), bf16[32,2,384]{2,1,0:T(2,128)(2,1)S(1)}, u32[]{:S(2)}, u32[]{:S(2)}) async-start(bf16[32,2,384]{2,1,0:T(2,128)(2,1)} %reshape.73), calls=%async_computation.5 | async-start | bytes 98304 | tf_op jit(solution)/shard_map/all_to_all | solution.py:108
  129.6 5.7 %collective-permute-start.2 = (bf16[16,768]{1,0:T(8,128)(2,1)S(1)}, bf16[16,768]{1,0:T(8,128)(2,1)S(1)}, u32[]{:S(2)}, u32[]{:S(2)}) collective-permute-start(bf16[16,768]{1,0:T(8,128)(2,1)S(1)} %slice.49), channel_id=1, source_target_pairs={{0,8},{8,0},{1,9},{9,1},{2,10},{10,2},{3,11},{11,3},{4,12},{12,4},... | collective-permute-start | bytes 73736 | tf_op jit(solution)/shard_map/ppermute | solution.py:29

commit v3 on v2

v3 whole, which is shorter than its diff:
```python
import jax
import jax.numpy as jnp
from jax import lax
from jax.experimental import pallas as pl
from jax.experimental.pallas import tpu as pltpu
from jax.sharding import Mesh
from jax.sharding import PartitionSpec as P

BF16 = jnp.bfloat16
F32 = jnp.float32
CHIPS = ("z", "yh")
SHARD = ("yl", "x")
DP = ("z", "yh", "core")
SIZES = {"z": 8, "yh": 4, "core": 2, "yl": 2, "x": 4}


def exchange(rows, axes):
    n = lax.axis_size(axes)
    blocks = rows.reshape(n, rows.shape[0] // n, rows.shape[1])
    return lax.all_to_all(blocks, axes, 0, 0, tiled=True)


def spread(rows, axes):
    n = lax.axis_size(axes)
    blocks = jnp.broadcast_to(rows[None], (n, *rows.shape))
    out = lax.all_to_all(blocks, axes, 0, 0, tiled=True)
    return out.reshape(n * rows.shape[0], rows.shape[1])


def from_cores(rows):
    return lax.all_gather(rows, "core", axis=0, tiled=False)


def dot(a, b, dims):
    return lax.dot_general(a, b, (dims, ((), ())), preferred_element_type=F32)


def on_vmem(kernel, shape, dtype, *operands):
    return pl.pallas_call(
        kernel,
        out_shape=jax.ShapeDtypeStruct(shape, dtype),
        in_specs=[pl.BlockSpec(memory_space=pltpu.VMEM)] * len(operands),
        out_specs=pl.BlockSpec(memory_space=pltpu.VMEM),
        compiler_params=pltpu.CompilerParams(vmem_limit_bytes=4 << 20),
    )(*operands)


LANES = 128
SEGMENTS = 8


def to_messages(rows, out_ref):
    used = rows.shape[1] // LANES
    for k in range(used):
        out_ref[:, k, :] = rows[:, k * LANES : (k + 1) * LANES]
    if used < SEGMENTS:
        out_ref[:, used:, :] = jnp.zeros((rows.shape[0], SEGMENTS - used, LANES), F32)


def from_messages(ref, used):
    return jnp.concatenate([ref[:, k, :] for k in range(used)], axis=1).astype(BF16)


def send_tokens(pick_ref, pairs_ref, out_ref):
    width = pairs_ref.shape[1] // 2
    first = lax.axis_index("core") == 0
    rows = jnp.where(first, pairs_ref[:, :width].astype(F32), pairs_ref[:, width:].astype(F32))
    to_messages(dot(pick_ref[...], rows.astype(BF16), ((1,), (0,))), out_ref)


def receive_tokens(place_ref, gates_ref, arrived_ref, out_ref):
    rows = from_messages(arrived_ref, out_ref.shape[2] // LANES)
    mine = dot(place_ref[...], rows, ((1,), (0,)))
    first = lax.axis_index("core") == 0
    mine = jnp.where(first, mine, mine * gates_ref[...]).astype(BF16)
    for q in range(out_ref.shape[0]):
        out_ref[q] = mine


def send_slots(place_t_ref, gates_ref, blocks_ref, out_ref):
    total = blocks_ref[0].astype(F32)
    for q in range(1, blocks_ref.shape[0]):
        total = total + blocks_ref[q].astype(F32)
    total = total.astype(BF16).astype(F32)
    first = lax.axis_index("core") == 0
    total = jnp.where(first, total * gates_ref[...], total).astype(BF16)
    to_messages(dot(place_t_ref[...], total, ((1,), (0,))), out_ref)


def receive_slots(pick_t_ref, arrived_ref, out_ref):
    rows = from_messages(arrived_ref, out_ref.shape[1] // LANES)
    out_ref[...] = dot(pick_t_ref[...], rows, ((1,), (0,))).astype(BF16)


def on_device(tokens, cotangent, slot_token, slot_gate, w_gate, w_up, w_down):
    w_gate, w_up, w_down = w_gate[0], w_up[0], w_down[0]
    slots = slot_token.reshape(-1)
    gates = slot_gate.reshape(-1)
    n_slots = slots.shape[0]
    n_own = tokens.shape[0]
    chip = lax.axis_index(CHIPS)
    core = lax.axis_index("core")
    first = core == 0
    n_chips = lax.axis_size(CHIPS)

    width = tokens.shape[1]
    pairs = from_cores(jnp.concatenate([tokens, cotangent], axis=1)).reshape(2 * n_own, -1)
    chip_ids = chip * (2 * n_own) + jnp.arange(2 * n_own, dtype=jnp.int32)

    joined = jnp.concatenate([w_gate.T, w_up.T, w_down], axis=0)
    n_ff = w_gate.shape[1]
    theirs = lax.ppermute(joined, "core", [(0, 1), (1, 0)])
    used = ((jnp.arange(3 * n_ff) >= 2 * n_ff) == first)[:, None]
    weights_0 = jnp.where(used, jnp.where(first, joined, theirs), jnp.zeros((), BF16))
    weights_1 = jnp.where(used, jnp.where(first, theirs, joined), jnp.zeros((), BF16))
    weights_0, weights_1 = lax.optimization_barrier((weights_0, weights_1))

    rank_here = jnp.sum((slots[:, None] < chip_ids[None, :]).astype(jnp.int32), axis=0)
    in_slot = jnp.max((slots[:, None] == chip_ids[None, :]).astype(jnp.int32), axis=0)
    peers = jnp.arange(n_chips, dtype=jnp.int32)
    lane = jnp.where(in_slot > 0, rank_here % n_chips, -1)
    pick = (peers[:, None] == lane[None, :]).astype(BF16)
    blocks = (n_chips, SEGMENTS, LANES)
    sent = on_vmem(send_tokens, blocks, F32, pick, pairs)
    arrived = lax.all_to_all(sent, CHIPS, 0, 0, tiled=True)

    per_chip = n_slots // n_chips
    ranks = jnp.sum((slots[:, None] < slots[None, :]).astype(jnp.int32), axis=0)
    my_ranks = chip + n_chips * jnp.arange(per_chip, dtype=jnp.int32)
    match = ranks[None, :] == my_ranks[:, None]
    my_tokens = jnp.sum(jnp.where(match, slots[None, :], 0), axis=1)
    my_gates = jnp.sum(jnp.where(match, gates[None, :], 0.0), axis=1)[:, None]
    place = ((my_tokens // (2 * n_own))[:, None] == peers[None, :]).astype(BF16)
    copies = on_vmem(receive_tokens, (n_chips, per_chip, width), BF16, place, my_gates, arrived)
    rows = lax.all_to_all(copies, CHIPS, 0, 0, tiled=True).reshape(n_slots, width)
    both = from_cores(rows)
    inputs, scaled = both[0], both[1]

    parts = jnp.concatenate(
        [
            dot(inputs, joined[: 2 * n_ff], ((1,), (1,))).astype(BF16),
            dot(scaled, w_down, ((1,), (1,))).astype(BF16),
        ],
        axis=1,
    )
    sums = jnp.sum(exchange(parts, SHARD).astype(F32), axis=0)
    gate_pre, up_pre, grad_hidden = sums[:, :n_ff], sums[:, n_ff : 2 * n_ff], sums[:, 2 * n_ff :]
    s = jax.nn.sigmoid(gate_pre)
    trio = jnp.concatenate(
        [
            (grad_hidden * up_pre * s * (1.0 + gate_pre * (1.0 - s))).astype(BF16),
            (grad_hidden * gate_pre * s).astype(BF16),
            (gate_pre * s * up_pre).astype(BF16),
        ],
        axis=1,
    )
    trio = spread(trio, SHARD)
    grad_gate_pre, grad_up_pre, hidden = trio[:, :n_ff], trio[:, n_ff : 2 * n_ff], trio[:, 2 * n_ff :]

    trios = from_cores(trio)
    total = dot(trios[0], weights_0, ((1,), (0,))) + dot(trios[1], weights_1, ((1,), (0,)))
    summands = exchange(total.astype(BF16), CHIPS)
    back = on_vmem(send_slots, blocks, F32, place.T, my_gates, summands)
    returned = lax.all_to_all(back, CHIPS, 0, 0, tiled=True)
    chip_out = on_vmem(receive_slots, (2 * n_own, width), BF16, pick.T, returned)
    done = from_cores(chip_out)
    mixed = lax.dynamic_slice_in_dim(done[0], core * n_own, n_own, 0)
    grad_tokens = lax.dynamic_slice_in_dim(done[1], core * n_own, n_own, 0)

    grad_down = dot(hidden, scaled, ((0,), (0,))).astype(BF16)
    grad_gate = dot(inputs, grad_gate_pre, ((0,), (0,))).astype(BF16)
    grad_up = dot(inputs, grad_up_pre, ((0,), (0,))).astype(BF16)
    return (mixed, grad_tokens, grad_gate[None], grad_up[None], grad_down[None])


def solution(mesh):
    fine = Mesh(mesh.devices.reshape(tuple(SIZES.values())), tuple(SIZES))
    return jax.shard_map(
        on_device,
        mesh=fine,
        in_specs=(
            P(DP, SHARD),
            P(DP, SHARD),
            P(),
            P(),
            P(None, SHARD, DP),
            P(None, SHARD, DP),
            P(None, DP, SHARD),
        ),
        out_specs=(
            P(DP, SHARD),
            P(DP, SHARD),
            P(None, SHARD, DP),
            P(None, SHARD, DP),
            P(None, DP, SHARD),
        ),
        check_vma=False,
    )
```

time: 137 us -> 134 us (0.978)
  blocking collectives: 43.9 us -> 22 us
  waiting for transfers between devices: 35.8 us -> 52 us
  Pallas kernels: 0 us -> 2.82 us
  local copies, waits for them, and re-layouts: 4.83 us -> 2.08 us
  other arithmetic: 4.57 us -> 7.27 us
  matrix products: 5.74 us -> 8.29 us
  starting transfers between devices: 40.2 us -> 38.1 us
    all_to_all x3 -> x0, blocking collectives: 39.9 us -> none  [the longest x2 28.3 us: spread(): out = lax.all_to_all(blocks, axes, 0, 0, tiled=True)]
    all_to_all x0 -> x2, waiting for transfers between devices: none -> 19.3 us  [the longest x1 14.5 us: on_device(): lax.all_to_all(copies, CHIPS, 0, 0, tiled=True).reshape(n_slots, width)]
    all_gather x1 -> x4, blocking collectives: 4.05 us -> 22 us  [from_cores(): return lax.all_gather(rows, 'core', axis=0, tiled=False)]
    ppermute x3 -> x1, starting transfers between devices: 18.1 us -> 2.56 us  [on_device(): theirs = lax.ppermute(joined, 'core', [(0, 1), (1, 0)])]
    all_to_all x0 -> x2, starting transfers between devices: none -> 9.18 us  [the longest x1 4.72 us: spread(): out = lax.all_to_all(blocks, axes, 0, 0, tiled=True)]
    all_to_all x1 -> x2, starting transfers between devices: 5.45 us -> 9.18 us  [exchange(): return lax.all_to_all(blocks, axes, 0, 0, tiled=True)]
    unnamed x14 -> x12, local copies, waits for them, and re-layouts: 4.08 us -> 0.59 us
    pallas_call x0 -> x4, Pallas kernels: none -> 2.82 us  [on_vmem(): pl.pallas_call(kernel, out_shape=jax.ShapeDtypeStruct(shape, dtype), in_s...]
  transfers between devices with their start and end apart: 6 -> 7, of which waited for: 4 -> 6; matrix products, arithmetic and copies ran while one was open for 3% -> 9% of each run, Pallas kernels for 0% -> 0%
where the time goes in v3:
time: 134 us; the launch traced here: 133 us
  waiting for transfers between devices  52 us (39%)
  starting transfers between devices  38.1 us (28%)
  blocking collectives  22 us (16%)
  matrix products  8.29 us (6%)
  other arithmetic  7.27 us (5%)
  Pallas kernels  2.82 us (2%)
  local copies, waits for them, and re-layouts  2.08 us (2%)
    all_gather x4, blocking collectives, from_cores(): return lax.all_gather(rows, 'core', axis=0, tiled=False)  22 us
    all_to_all x2, waiting for transfers between devices, exchange(): return lax.all_to_all(blocks, axes, 0, 0, tiled=True)  16.8 us
    all_to_all x1, waiting for transfers between devices, on_device(): lax.all_to_all(copies, CHIPS, 0, 0, tiled=True).reshape(n_slots, width)  14.5 us
    all_to_all x1, starting transfers between devices, on_device(): arrived = lax.all_to_all(sent, CHIPS, 0, 0, tiled=True)  10.5 us
    all_to_all x2, starting transfers between devices, exchange(): return lax.all_to_all(blocks, axes, 0, 0, tiled=True)  9.18 us
    all_to_all x1, waiting for transfers between devices, on_device(): arrived = lax.all_to_all(sent, CHIPS, 0, 0, tiled=True)  8.54 us
    dot_general x7, matrix products, dot(): return lax.dot_general(a, b, (dims, ((), ())), preferred_element_type=F32)  8.29 us
    all_to_all x1, waiting for transfers between devices, on_device(): returned = lax.all_to_all(back, CHIPS, 0, 0, tiled=True)  7.33 us
  transfers between devices with their start and end apart: 7, of which 6 were waited for; matrix products, arithmetic and copies ran while one was open for 9% of the time, Pallas kernels for 0%

profile of v3, /device:TPU:1, one launch (start us, length us, event | category | flops | bytes accessed | tf_op | source)
XLA Modules:
  0.0 133.4 jit_solution(1201165750300523517)
XLA Ops:
  0.7 0.9 convert_reduce_fusion.2
  1.6 0.1 fusion.14
  1.7 0.8 pad_maximum_fusion.2
  2.4 8.3 %all-gather.pairs_ref = bf16[32,1536]{1,0:T(8,128)(2,1)S(1)} all-gather(bf16[16,1536]{1,0:T(8,128)(2,1)S(1)} %pad_maximum_fusion.2), channel_id=2, replica_groups=mesh['z'=8,'yh'=4,'core'=2,'yl'=2,'x'=4] {'core'}, dimensions={0}, use_global_device_ids=true | all-gather | bytes 147456 | tf_op jit(solution)/shard_map/all_gather | solution.py:31
  10.8 0.8 shard_map.110
  11.6 10.5 %all-to-all-start = ((f32[32,8,128]{2,1,0:T(8,128)}), f32[32,8,128]{2,1,0:T(8,128)S(1)}, u32[]{:S(2)}, u32[]{:S(2)}) async-start(f32[32,8,128]{2,1,0:T(8,128)} %shard_map.110), calls=%async_computation | async-start | bytes 262144 | tf_op jit(solution)/shard_map/all_to_all | solution.py:125
  22.1 0.9 convert_reduce_fusion.1
  23.0 0.9 fusion.15
  23.8 0.9 fusion.16
  24.7 0.1 copy.26.gates_ref
  24.8 0.1 fusion.17.place_ref
  24.9 8.5 %all-to-all-done.arrived_ref = f32[32,8,128]{2,1,0:T(8,128)S(1)} async-done(((f32[32,8,128]{2,1,0:T(8,128)}), f32[32,8,128]{2,1,0:T(8,128)S(1)}, u32[]{:S(2)}, u32[]{:S(2)}) %all-to-all-start) | async-done | bytes 131104 | tf_op jit(solution)/shard_map/all_to_all | solution.py:125
  33.4 0.9 shard_map.111
  34.3 4.5 %all-to-all-start.1 = ((bf16[32,8,768]{2,1,0:T(8,128)(2,1)}), bf16[32,8,768]{2,1,0:T(8,128)(2,1)S(1)}, u32[]{:S(2)}, u32[]{:S(2)}) async-start(bf16[32,8,768]{2,1,0:T(8,128)(2,1)} %shard_map.111), calls=%async_computation.1 | async-start | bytes 786432 | tf_op jit(solution)/shard_map/all_to_all | solution.py:135
  38.8 0.2 copy.24
  39.0 0.0 copy-start.2
  39.0 0.2 copy.23
  39.2 14.5 %all-to-all-done.1 = bf16[32,8,768]{2,1,0:T(8,128)(2,1)S(1)} async-done(((bf16[32,8,768]{2,1,0:T(8,128)(2,1)}), bf16[32,8,768]{2,1,0:T(8,128)(2,1)S(1)}, u32[]{:S(2)}, u32[]{:S(2)}) %all-to-all-start.1) | async-done | bytes 393248 | tf_op jit(solution)/shard_map/all_to_all | solution.py:135
  53.7 4.7 %all_gather.20 = bf16[2,256,768]{2,1,0:T(8,128)(2,1)S(1)} all-gather(bf16[1,256,768]{2,1,0:T(8,128)(2,1)S(1)} %bitcast.47), channel_id=1, replica_groups=mesh['z'=8,'yh'=4,'core'=2,'yl'=2,'x'=4] {'core'}, dimensions={0}, use_global_device_ids=true | all-gather | bytes 1179648 | tf_op jit(solution)/shard_map/all_gather | solution.py:31
  58.4 0.3 convolution_convert_fusion.4
  58.7 0.4 convolution_convert_fusion.3
  59.1 0.2 copy-done
  59.3 0.8 pad_maximum_fusion.1
  60.1 4.0 %all-to-all-start.2 = ((bf16[8,32,768]{2,1,0:T(8,128)(2,1)}), bf16[8,32,768]{2,1,0:T(8,128)(2,1)S(1)}, u32[]{:S(2)}, u32[]{:S(2)}) async-start(bf16[8,32,768]{2,1,0:T(8,128)(2,1)} %bitcast.11), calls=%async_computation.2 | async-start | bytes 786432 | tf_op jit(solution)/shard_map/all_to_all | solution.py:20
  64.1 0.1 pad_maximum_fusion
  64.2 2.6 %collective-permute-start = (bf16[768,768]{1,0:T(8,128)(2,1)S(1)}, bf16[768,768]{1,0:T(8,128)(2,1)}, u32[]{:S(2)}, u32[]{:S(2)}) collective-permute-start(bf16[768,768]{1,0:T(8,128)(2,1)S(1)} %pad_maximum_fusion), channel_id=1, source_target_pairs={{0,8},{8,0},{1,9},{9,1},{2,10},{10,2},{3,11},{11,3},{4,12},{12,4},... | collective-permute-start | bytes 3538952 | tf_op jit(solution)/shard_map/ppermute | solution.py:112
  66.7 4.2 %all-to-all-done.2 = bf16[8,32,768]{2,1,0:T(8,128)(2,1)S(1)} async-done(((bf16[8,32,768]{2,1,0:T(8,128)(2,1)}), bf16[8,32,768]{2,1,0:T(8,128)(2,1)S(1)}, u32[]{:S(2)}, u32[]{:S(2)}) %all-to-all-start.2) | async-done | bytes 393248 | tf_op jit(solution)/shard_map/all_to_all | solution.py:20
  71.0 0.1 convert_reduce_fusion
  71.1 0.8 broadcast_in_dim.80
  71.8 4.7 %all-to-all-start.3 = ((bf16[8,32,768]{2,1,0:T(8,128)(2,1)}), bf16[8,32,768]{2,1,0:T(8,128)(2,1)}, u32[]{:S(2)}, u32[]{:S(2)}) async-start(bf16[8,32,768]{2,1,0:T(8,128)(2,1)} %broadcast_in_dim.80), calls=%async_computation.3 | async-start | bytes 786432 | tf_op jit(solution)/shard_map/all_to_all | solution.py:26
  76.6 0.0 collective-permute-done
  76.6 1.9 %select_select_fusion = (bf16[768,768]{1,0:T(8,128)(2,1)S(1)}, bf16[768,768]{1,0:T(8,128)(2,1)S(1)}) fusion(bf16[768,768]{1,0:T(8,128)(2,1)} %collective-permute-done, pred[768]{0:T(1024)(128)(4,1)S(1)} %fusion.18, pred[]{:T(512)S(6)} %eq.102, bf16[256,768]{1,0:T(8,128)(2,1)S(1)} %bitcast.49, bf16[256,768]{1,0:T(8,128)(2,1)S(1)} %bitcast.43, ...), kind=kLoop, calls=%fused_computation.11 | loop fusion | flops 5898240 | bytes 4719361 | tf_op jit(solution)/shard_map/jit(_where)/select_n | solution.py:115
  78.5 4.9 %all-to-all-done.3 = bf16[8,32,768]{2,1,0:T(8,128)(2,1)} async-done(((bf16[8,32,768]{2,1,0:T(8,128)(2,1)}), bf16[8,32,768]{2,1,0:T(8,128)(2,1)}, u32[]{:S(2)}, u32[]{:S(2)}) %all-to-all-start.3) | async-done | bytes 393248 | tf_op jit(solution)/shard_map/all_to_all | solution.py:26
  83.3 5.0 %all_gather.21 = bf16[2,256,768]{2,1,0:T(8,128)(2,1)S(1)} all-gather(bf16[1,256,768]{2,1,0:T(8,128)(2,1)} %bitcast.12), channel_id=1, replica_groups=mesh['z'=8,'yh'=4,'core'=2,'yl'=2,'x'=4] {'core'}, dimensions={0}, use_global_device_ids=true | all-gather | bytes 1179648 | tf_op jit(solution)/shard_map/all_gather | solution.py:31
  88.3 0.5 fusion.8
  88.8 0.0 copy-start.1
  88.8 1.2 fusion.4
  90.1 5.2 %all-to-all-start.4 = ((bf16[32,8,768]{2,1,0:T(8,128)(2,1)}), bf16[32,8,768]{2,1,0:T(8,128)(2,1)S(1)}, u32[]{:S(2)}, u32[]{:S(2)}) async-start(bf16[32,8,768]{2,1,0:T(8,128)(2,1)} %fusion.4), calls=%async_computation.4 | async-start | bytes 786432 | tf_op jit(solution)/shard_map/all_to_all | solution.py:20
  95.2 2.0 %fusion.1 = bf16[1,768,256]{2,1,0:T(8,128)(2,1)} fusion(bf16[2,256,768]{2,1,0:T(8,128)(2,1)S(1)} %copy-done.1, bf16[256,768]{1,0:T(8,128)(2,1)} %bitcast.18), kind=kOutput, calls=%fused_computation.5 | convolution fusion | flops 100859904 | bytes 917504 | tf_op jit(solution)/shard_map/dot_general | solution.py:35
  97.2 12.6 %all-to-all-done.4.blocks_ref = bf16[32,8,768]{2,1,0:T(8,128)(2,1)S(1)} async-done(((bf16[32,8,768]{2,1,0:T(8,128)(2,1)}), bf16[32,8,768]{2,1,0:T(8,128)(2,1)S(1)}, u32[]{:S(2)}, u32[]{:S(2)}) %all-to-all-start.4) | async-done | bytes 393248 | tf_op jit(solution)/shard_map/all_to_all | solution.py:20
  109.8 0.9 shard_map.112
  110.7 6.7 %all-to-all-start.5 = ((f32[32,8,128]{2,1,0:T(8,128)}), f32[32,8,128]{2,1,0:T(8,128)S(1)}, u32[]{:S(2)}, u32[]{:S(2)}) async-start(f32[32,8,128]{2,1,0:T(8,128)} %shard_map.112), calls=%async_computation.5 | async-start | bytes 262144 | tf_op jit(solution)/shard_map/all_to_all | solution.py:164
  117.4 2.0 %fusion.3 = bf16[1,256,768]{2,1,0:T(8,128)(2,1)} fusion(bf16[2,256,768]{2,1,0:T(8,128)(2,1)S(1)} %copy-done.1, bf16[256,768]{1,0:T(8,128)(2,1)} %bitcast.18), kind=kOutput, calls=%fused_computation.7 | convolution fusion | flops 100859904 | bytes 917504 | tf_op jit(solution)/shard_map/dot_general | solution.py:35
  119.4 2.0 %fusion.2 = bf16[1,768,256]{2,1,0:T(8,128)(2,1)} fusion(bf16[2,256,768]{2,1,0:T(8,128)(2,1)S(1)} %copy-done.1, bf16[256,768]{1,0:T(8,128)(2,1)} %bitcast.18), kind=kOutput, calls=%fused_computation.6 | convolution fusion | flops 100859904 | bytes 917504 | tf_op jit(solution)/shard_map/dot_general | solution.py:35
  121.3 7.3 %all-to-all-done.5.arrived_ref = f32[32,8,128]{2,1,0:T(8,128)S(1)} async-done(((f32[32,8,128]{2,1,0:T(8,128)}), f32[32,8,128]{2,1,0:T(8,128)S(1)}, u32[]{:S(2)}, u32[]{:S(2)}) %all-to-all-start.5) | async-done | bytes 131104 | tf_op jit(solution)/shard_map/all_to_all | solution.py:164
  128.7 0.2 shard_map.113
  128.8 3.9 %all-gather.1 = bf16[64,768]{1,0:T(8,128)(2,1)S(1)} all-gather(bf16[32,768]{1,0:T(8,128)(2,1)S(1)} %shard_map.113), channel_id=3, replica_groups=mesh['z'=8,'yh'=4,'core'=2,'yl'=2,'x'=4] {'core'}, dimensions={0}, use_global_device_ids=true | all-gather | bytes 147456 | tf_op jit(solution)/shard_map/all_gather | solution.py:31
  132.8 0.6 constant_dynamic-slice_fusion
  (16 shorter events, 0.1 us)
Async XLA Ops:
  0.6 38.2 %copy-start.3 = (bf16[1,768,256]{2,1,0:T(8,128)(2,1)S(1)}, bf16[1,768,256]{2,1,0:T(8,128)(2,1)}, u32[]{:S(2)}) copy-start(bf16[1,768,256]{2,1,0:T(8,128)(2,1)} %param.12) | copy-start | bytes 1179652
  11.6 27.4 %copy-start.4 = (bf16[1,768,256]{2,1,0:T(8,128)(2,1)S(1)}, bf16[1,768,256]{2,1,0:T(8,128)(2,1)}, u32[]{:S(2)}) copy-start(bf16[1,768,256]{2,1,0:T(8,128)(2,1)} %param.11) | copy-start | bytes 1179652
  11.6 21.8 %all-to-all-start = ((f32[32,8,128]{2,1,0:T(8,128)}), f32[32,8,128]{2,1,0:T(8,128)S(1)}, u32[]{:S(2)}, u32[]{:S(2)}) async-start(f32[32,8,128]{2,1,0:T(8,128)} %shard_map.110), calls=%async_computation | async-start | bytes 262144 | tf_op jit(solution)/shard_map/all_to_all | solution.py:125
  34.3 19.3 %all-to-all-start.1 = ((bf16[32,8,768]{2,1,0:T(8,128)(2,1)}), bf16[32,8,768]{2,1,0:T(8,128)(2,1)S(1)}, u32[]{:S(2)}, u32[]{:S(2)}) async-start(bf16[32,8,768]{2,1,0:T(8,128)(2,1)} %shard_map.111), calls=%async_computation.1 | async-start | bytes 786432 | tf_op jit(solution)/shard_map/all_to_all | solution.py:135
  39.0 19.4 %copy-start.2 = (bf16[1,256,768]{2,1,0:T(8,128)(2,1)S(1)}, bf16[1,256,768]{2,1,0:T(8,128)(2,1)}, u32[]{:S(2)}) copy-start(bf16[1,256,768]{2,1,0:T(8,128)(2,1)} %param.13) | copy-start | bytes 1179652
  58.4 0.9 copy-start
  60.1 10.9 %all-to-all-start.2 = ((bf16[8,32,768]{2,1,0:T(8,128)(2,1)}), bf16[8,32,768]{2,1,0:T(8,128)(2,1)S(1)}, u32[]{:S(2)}, u32[]{:S(2)}) async-start(bf16[8,32,768]{2,1,0:T(8,128)(2,1)} %bitcast.11), calls=%async_computation.2 | async-start | bytes 786432 | tf_op jit(solution)/shard_map/all_to_all | solution.py:20
  64.2 12.4 %collective-permute-start = (bf16[768,768]{1,0:T(8,128)(2,1)S(1)}, bf16[768,768]{1,0:T(8,128)(2,1)}, u32[]{:S(2)}, u32[]{:S(2)}) collective-permute-start(bf16[768,768]{1,0:T(8,128)(2,1)S(1)} %pad_maximum_fusion), channel_id=1, source_target_pairs={{0,8},{8,0},{1,9},{9,1},{2,10},{10,2},{3,11},{11,3},{4,12},{12,4},... | collective-permute-start | bytes 3538952 | tf_op jit(solution)/shard_map/ppermute | solution.py:112
  71.8 11.5 %all-to-all-start.3 = ((bf16[8,32,768]{2,1,0:T(8,128)(2,1)}), bf16[8,32,768]{2,1,0:T(8,128)(2,1)}, u32[]{:S(2)}, u32[]{:S(2)}) async-start(bf16[8,32,768]{2,1,0:T(8,128)(2,1)} %broadcast_in_dim.80), calls=%async_computation.3 | async-start | bytes 786432 | tf_op jit(solution)/shard_map/all_to_all | solution.py:26
  88.8 6.4 %copy-start.1 = (bf16[2,256,768]{2,1,0:T(8,128)(2,1)S(1)}, bf16[2,256,768]{2,1,0:T(8,128)(2,1)}, u32[]{:S(2)}) copy-start(bf16[2,256,768]{2,1,0:T(8,128)(2,1)} %copy-done) | copy-start | bytes 2359300
  90.1 19.7 %all-to-all-start.4 = ((bf16[32,8,768]{2,1,0:T(8,128)(2,1)}), bf16[32,8,768]{2,1,0:T(8,128)(2,1)S(1)}, u32[]{:S(2)}, u32[]{:S(2)}) async-start(bf16[32,8,768]{2,1,0:T(8,128)(2,1)} %fusion.4), calls=%async_computation.4 | async-start | bytes 786432 | tf_op jit(solution)/shard_map/all_to_all | solution.py:20
  110.7 18.0 %all-to-all-start.5 = ((f32[32,8,128]{2,1,0:T(8,128)}), f32[32,8,128]{2,1,0:T(8,128)S(1)}, u32[]{:S(2)}, u32[]{:S(2)}) async-start(f32[32,8,128]{2,1,0:T(8,128)} %shard_map.112), calls=%async_computation.5 | async-start | bytes 262144 | tf_op jit(solution)/shard_map/all_to_all | solution.py:164

commit v4 on v3

v4 whole, which is shorter than its diff:
```python
import functools

import jax
import jax.numpy as jnp
from jax import lax
from jax.experimental import pallas as pl
from jax.experimental.pallas import tpu as pltpu
from jax.sharding import Mesh
from jax.sharding import PartitionSpec as P


BF16 = jnp.bfloat16
F32 = jnp.float32
CHIPS = ("z", "yh")
SHARD = ("yl", "x")
DP = ("z", "yh", "core")
SIZES = {"z": 8, "yh": 4, "core": 2, "yl": 2, "x": 4}


def exchange(rows, axes):
    n = lax.axis_size(axes)
    blocks = rows.reshape(n, rows.shape[0] // n, rows.shape[1])
    return lax.all_to_all(blocks, axes, 0, 0, tiled=True)


def spread(rows, axes):
    n = lax.axis_size(axes)
    blocks = jnp.broadcast_to(rows[None], (n, *rows.shape))
    out = lax.all_to_all(blocks, axes, 0, 0, tiled=True)
    return out.reshape(n * rows.shape[0], rows.shape[1])


def from_cores(rows):
    return lax.all_gather(rows, "core", axis=0, tiled=False)


def dot(a, b, dims):
    return lax.dot_general(a, b, (dims, ((), ())), preferred_element_type=F32)


def on_vmem(kernel, outs, *operands):
    vmem = pl.BlockSpec(memory_space=pltpu.VMEM)
    return pl.pallas_call(
        kernel,
        out_shape=tuple(jax.ShapeDtypeStruct(*o) for o in outs),
        in_specs=[vmem] * len(operands),
        out_specs=(vmem,) * len(outs),
        compiler_params=pltpu.CompilerParams(vmem_limit_bytes=4 << 20),
    )(*operands)


LANES = 128
SEGMENTS = 8


def to_messages(rows, out_ref):
    used = rows.shape[1] // LANES
    for k in range(used):
        out_ref[:, k, :] = rows[:, k * LANES : (k + 1) * LANES]
    if used < SEGMENTS:
        out_ref[:, used:, :] = jnp.zeros((rows.shape[0], SEGMENTS - used, LANES), F32)


def from_messages(ref, used):
    return jnp.concatenate([ref[:, k, :] for k in range(used)], axis=1).astype(BF16)


def send_tokens(slots_ref, pairs_ref, out_ref, pick_ref):
    n_tok, n_chips = pick_ref.shape
    n_slots = slots_ref.shape[1]
    chip = lax.axis_index("z") * lax.axis_size("yh") + lax.axis_index("yh")
    slots = slots_ref[...]

    ids = chip * n_tok + lax.broadcasted_iota(jnp.int32, (n_tok, n_slots), 0)
    row = jnp.broadcast_to(slots, (n_tok, n_slots))
    rank = jnp.sum(jnp.where(row < ids, 1.0, 0.0), axis=1, keepdims=True).astype(jnp.int32)
    held = jnp.sum(jnp.where(row == ids, 1.0, 0.0), axis=1, keepdims=True)
    peer = lax.broadcasted_iota(jnp.int32, (n_tok, n_chips), 1)
    lane = jnp.where(held > 0.0, lax.rem(rank, n_chips), -1)
    pick_ref[...] = jnp.where(peer == lane, 1.0, 0.0).astype(BF16)

    width = pairs_ref.shape[1] // 2
    first = lax.axis_index("core") == 0
    rows = jnp.where(first, pairs_ref[:, :width].astype(F32), pairs_ref[:, width:].astype(F32))
    to_messages(dot(pick_ref[...], rows.astype(BF16), ((0,), (0,))), out_ref)


def find_slots(n_tok, slots_ref, gates_ref, place_ref, my_gates_ref):
    per_chip, n_chips = place_ref.shape
    n_slots = slots_ref.shape[1]
    chip = lax.axis_index("z") * lax.axis_size("yh") + lax.axis_index("yh")
    slots = slots_ref[...]
    wide = jnp.broadcast_to(slots.astype(F32), (LANES, n_slots))
    column = jnp.transpose(wide)[:, :1]
    below = jnp.where(column < slots.astype(F32), 1.0, 0.0)
    ranks = jnp.sum(below, axis=0, keepdims=True).astype(jnp.int32)
    mine = chip + n_chips * lax.broadcasted_iota(jnp.int32, (per_chip, n_slots), 0)
    match = jnp.broadcast_to(ranks, (per_chip, n_slots)) == mine
    token = jnp.sum(jnp.where(match, slots.astype(F32), 0.0), axis=1, keepdims=True).astype(jnp.int32)
    my_gates_ref[...] = jnp.sum(jnp.where(match, gates_ref[...], 0.0), axis=1, keepdims=True)
    source = lax.broadcasted_iota(jnp.int32, (per_chip, n_chips), 1)
    place_ref[...] = jnp.where(lax.div(token, n_tok) == source, 1.0, 0.0).astype(BF16)


def receive_tokens(place_ref, gates_ref, arrived_ref, out_ref):
    rows = from_messages(arrived_ref, out_ref.shape[2] // LANES)
    mine = dot(place_ref[...], rows, ((1,), (0,)))
    first = lax.axis_index("core") == 0
    mine = jnp.where(first, mine, mine * gates_ref[...]).astype(BF16)
    for q in range(out_ref.shape[0]):
        out_ref[q] = mine


def send_slots(place_ref, gates_ref, blocks_ref, out_ref):
    total = blocks_ref[0].astype(F32)
    for q in range(1, blocks_ref.shape[0]):
        total = total + blocks_ref[q].astype(F32)
    total = total.astype(BF16).astype(F32)
    first = lax.axis_index("core") == 0
    total = jnp.where(first, total, total * gates_ref[...]).astype(BF16)
    to_messages(dot(place_ref[...], total, ((0,), (0,))), out_ref)


def receive_slots(pick_ref, arrived_ref, out_ref):
    rows = from_messages(arrived_ref, out_ref.shape[1] // LANES)
    out_ref[...] = dot(pick_ref[...], rows, ((1,), (0,))).astype(BF16)


def on_device(tokens, cotangent, slot_token, slot_gate, w_gate, w_up, w_down):
    w_gate, w_up, w_down = w_gate[0], w_up[0], w_down[0]
    n_ff = w_gate.shape[1]
    n_own, width = tokens.shape
    n_slots = slot_token.size
    core = lax.axis_index("core")
    first = core == 0
    n_chips = lax.axis_size(CHIPS)
    per_chip = n_slots // n_chips
    blocks = (n_chips, SEGMENTS, LANES)

    pairs = from_cores(jnp.concatenate([tokens, cotangent], axis=1)).reshape(2 * n_own, 2 * width)
    slots = slot_token.reshape(1, -1)
    sent, pick = on_vmem(send_tokens, ((blocks, F32), ((2 * n_own, n_chips), BF16)), slots, pairs)
    arrived = lax.all_to_all(sent, CHIPS, 0, 0, tiled=True)
    place, my_gates = on_vmem(
        functools.partial(find_slots, 2 * n_own),
        (((per_chip, n_chips), BF16), ((per_chip, 1), F32)),
        slots,
        slot_gate.reshape(1, -1),
    )
    gate_up = jnp.concatenate([w_gate.T, w_up.T], axis=0)
    blank = jnp.zeros_like(w_down)
    theirs = jnp.where(first, jnp.concatenate([w_down, blank], axis=0), gate_up)
    theirs = lax.ppermute(theirs, "core", [(0, 1), (1, 0)])
    weights = jnp.where(
        first,
        jnp.concatenate([gate_up, theirs], axis=0),
        jnp.concatenate([theirs[:n_ff], w_down, blank, blank], axis=0),
    )
    (copies,) = on_vmem(receive_tokens, (((n_chips, per_chip, width), BF16),), place, my_gates, arrived)
    rows = lax.all_to_all(copies, CHIPS, 0, 0, tiled=True).reshape(n_slots, width)
    weights, rows = lax.optimization_barrier((weights, rows))

    parts = dot(rows, weights, ((1,), (1,))).astype(BF16)
    sums = jnp.sum(exchange(parts, SHARD).astype(F32), axis=0)
    sums = from_cores(sums)
    trios = []
    for k in range(2):
        gate_pre = sums[0, :, 2 * k * n_ff : (2 * k + 1) * n_ff]
        up_pre = sums[0, :, (2 * k + 1) * n_ff : (2 * k + 2) * n_ff]
        grad_hidden = sums[1, :, k * n_ff : (k + 1) * n_ff]
        s = jax.nn.sigmoid(gate_pre)
        trios.append(
            (
                (gate_pre * s * up_pre).astype(BF16),
                (grad_hidden * up_pre * s * (1.0 + gate_pre * (1.0 - s))).astype(BF16),
                (grad_hidden * gate_pre * s).astype(BF16),
            )
        )
    (h0, g0, u0), (h1, g1, u1) = trios
    factors = jnp.concatenate(
        [jnp.where(first, g0, h0), jnp.where(first, u0, h1), g1, u1, jnp.where(first, h0, h1)], axis=1
    )
    factors = spread(factors, SHARD)

    total = dot(factors[:, : 4 * n_ff], weights, ((1,), (0,))).astype(BF16)
    total, rows = lax.optimization_barrier((total, rows))
    summands = exchange(total, CHIPS)
    other_rows = lax.ppermute(rows, "core", [(0, 1), (1, 0)])
    factors, rows, other_rows, summands = lax.optimization_barrier((factors, rows, other_rows, summands))
    (back,) = on_vmem(send_slots, ((blocks, F32),), place, my_gates, summands)
    returned = lax.all_to_all(back, CHIPS, 0, 0, tiled=True)
    (chip_out,) = on_vmem(receive_slots, (((2 * n_own, width), BF16),), pick, returned)
    done = from_cores(chip_out)
    grad_tokens = lax.dynamic_slice_in_dim(done[0], core * n_own, n_own, 0)
    mixed = lax.dynamic_slice_in_dim(done[1], core * n_own, n_own, 0)

    inputs = jnp.where(first, rows, other_rows)
    scaled = jnp.where(first, other_rows, rows)
    hidden = factors[:, 4 * n_ff :]
    grad_pre = lax.dynamic_slice_in_dim(factors, core * 2 * n_ff, 2 * n_ff, 1)
    grad_down = dot(hidden, scaled, ((0,), (0,))).astype(BF16)
    grad_gate = dot(inputs, grad_pre[:, :n_ff], ((0,), (0,))).astype(BF16)
    grad_up = dot(inputs, grad_pre[:, n_ff:], ((0,), (0,))).astype(BF16)
    return (mixed, grad_tokens, grad_gate[None], grad_up[None], grad_down[None])


def solution(mesh):
    fine = Mesh(mesh.devices.reshape(tuple(SIZES.values())), tuple(SIZES))
    return jax.shard_map(
        on_device,
        mesh=fine,
        in_specs=(
            P(DP, SHARD),
            P(DP, SHARD),
            P(),
            P(),
            P(None, SHARD, DP),
            P(None, SHARD, DP),
            P(None, DP, SHARD),
        ),
        out_specs=(
            P(DP, SHARD),
            P(DP, SHARD),
            P(None, SHARD, DP),
            P(None, SHARD, DP),
            P(None, DP, SHARD),
        ),
        check_vma=False,
    )
```

time: 134 us -> 135 us (level)
  blocking collectives: 22 us -> 35.9 us
  waiting for transfers between devices: 52 us -> 43.2 us
  other arithmetic: 7.27 us -> 1.79 us
  matrix products: 8.29 us -> 5.14 us
  starting transfers between devices: 38.1 us -> 40.6 us
    all_to_all x0 -> x2, blocking collectives: none -> 24.4 us  [the longest x1 13.1 us: spread(): out = lax.all_to_all(blocks, axes, 0, 0, tiled=True)]
    all_gather x4 -> x3, blocking collectives: 22 us -> 11.6 us  [from_cores(): return lax.all_gather(rows, 'core', axis=0, tiled=False)]
    ppermute x1 -> x2, starting transfers between devices: 2.56 us -> 12.7 us  [the longest x1 8.75 us: on_device(): theirs = lax.ppermute(theirs, 'core', [(0, 1), (1, 0)])]
    all_to_all x2 -> x1, waiting for transfers between devices: 16.8 us -> 9.34 us  [exchange(): return lax.all_to_all(blocks, axes, 0, 0, tiled=True)]
    all_to_all x1 -> x0, waiting for transfers between devices: 4.86 us -> none  [spread(): out = lax.all_to_all(blocks, axes, 0, 0, tiled=True)]
    all_to_all x1 -> x0, starting transfers between devices: 4.72 us -> none  [spread(): out = lax.all_to_all(blocks, axes, 0, 0, tiled=True)]
    reduce_sum x4 -> x0, other arithmetic: 3.5 us -> none  [the longest x1 0.91 us: on_device(): jnp.sum((slots[:, None] < chip_ids[None, :]).astype(jnp.int32), axis=0)]
    dot_general x7 -> x5, matrix products: 8.29 us -> 5.14 us  [dot(): return lax.dot_general(a, b, (dims, ((), ())), preferred_element_type=F32)]
  transfers between devices with their start and end apart: 7 -> 6, of which waited for: 6 -> 5; matrix products, arithmetic and copies ran while one was open for 9% -> 4% of each run, Pallas kernels for 0% -> 2%
where the time goes in v4:
time: 135 us; the launch traced here: 134 us
  waiting for transfers between devices  43.2 us (32%)
  starting transfers between devices  40.6 us (30%)
  blocking collectives  35.9 us (27%)
  matrix products  5.14 us (4%)
  Pallas kernels  3.28 us (2%)
  local copies, waits for them, and re-layouts  3.14 us (2%)
  other arithmetic  1.79 us (1%)
    all_to_all x1, waiting for transfers between devices, on_device(): lax.all_to_all(copies, CHIPS, 0, 0, tiled=True).reshape(n_slots, width)  13.4 us
    all_to_all x1, blocking collectives, spread(): out = lax.all_to_all(blocks, axes, 0, 0, tiled=True)  13.1 us
    all_gather x3, blocking collectives, from_cores(): return lax.all_gather(rows, 'core', axis=0, tiled=False)  11.6 us
    all_to_all x1, blocking collectives, exchange(): return lax.all_to_all(blocks, axes, 0, 0, tiled=True)  11.3 us
    all_to_all x1, waiting for transfers between devices, on_device(): arrived = lax.all_to_all(sent, CHIPS, 0, 0, tiled=True)  11 us
    all_to_all x1, starting transfers between devices, on_device(): arrived = lax.all_to_all(sent, CHIPS, 0, 0, tiled=True)  10.3 us
    all_to_all x1, waiting for transfers between devices, exchange(): return lax.all_to_all(blocks, axes, 0, 0, tiled=True)  9.34 us
    ppermute x1, starting transfers between devices, on_device(): theirs = lax.ppermute(theirs, 'core', [(0, 1), (1, 0)])  8.75 us
  transfers between devices with their start and end apart: 6, of which 5 were waited for; matrix products, arithmetic and copies ran while one was open for 4% of the time, Pallas kernels for 2%

profile of v4, /device:TPU:1, one launch (start us, length us, event | category | flops | bytes accessed | tf_op | source)
XLA Modules:
  0.0 133.9 jit_solution(1515766094808955842)
XLA Ops:
  0.6 0.0 copy-start.2
  0.6 1.2 copy.12
  1.9 0.0 copy-start.3
  1.9 0.0 copy-start.4
  1.9 0.0 copy-start
  1.9 0.0 copy-start.1
  1.9 1.2 copy.13
  3.1 0.0 copy-done.2
  3.1 0.2 maximum_select_fusion.1
  3.3 8.7 %collective-permute-start = (bf16[512,768]{1,0:T(8,128)(2,1)S(1)}, bf16[512,768]{1,0:T(8,128)(2,1)S(1)}, u32[]{:S(2)}, u32[]{:S(2)}) collective-permute-start(bf16[512,768]{1,0:T(8,128)(2,1)S(1)} %maximum_select_fusion.1), channel_id=1, source_target_pairs={{0,8},{8,0},{1,9},{9,1},{2,10},{10,2},{3,11},{11,3},{4,12},{12,4},... | collective-permute-start | bytes 2359304 | tf_op jit(solution)/shard_map/ppermute | solution.py:153
  12.0 0.0 copy-done.3
  12.1 0.0 copy-done.4
  12.1 1.9 %all-gather.pairs_ref = bf16[32,1536]{1,0:T(8,128)(2,1)S(1)} all-gather(bf16[16,1536]{1,0:T(8,128)(2,1)S(1)} %pad_maximum_fusion), channel_id=2, replica_groups=mesh['z'=8,'yh'=4,'core'=2,'yl'=2,'x'=4] {'core'}, dimensions={0}, use_global_device_ids=true | all-gather | bytes 147456 | tf_op jit(solution)/shard_map/all_gather | solution.py:34
  14.0 0.0 copy-done
  14.0 1.0 shard_map.110
  15.0 10.3 %all-to-all-start = ((f32[32,8,128]{2,1,0:T(8,128)}), f32[32,8,128]{2,1,0:T(8,128)S(1)}, u32[]{:S(2)}, u32[]{:S(2)}) async-start(f32[32,8,128]{2,1,0:T(8,128)} %get-tuple-element.20), calls=%async_computation | async-start | bytes 262144 | tf_op jit(solution)/shard_map/all_to_all | solution.py:143
  25.3 0.0 copy-done.1
  25.3 0.3 shard_map.111
  25.6 11.0 %all-to-all-done.arrived_ref = f32[32,8,128]{2,1,0:T(8,128)S(1)} async-done(((f32[32,8,128]{2,1,0:T(8,128)}), f32[32,8,128]{2,1,0:T(8,128)S(1)}, u32[]{:S(2)}, u32[]{:S(2)}) %all-to-all-start) | async-done | bytes 131104 | tf_op jit(solution)/shard_map/all_to_all | solution.py:143
  36.6 0.9 shard_map.112
  37.6 4.5 %all-to-all-start.1 = ((bf16[32,8,768]{2,1,0:T(8,128)(2,1)}), bf16[32,8,768]{2,1,0:T(8,128)(2,1)S(1)}, u32[]{:S(2)}, u32[]{:S(2)}) async-start(bf16[32,8,768]{2,1,0:T(8,128)(2,1)} %shard_map.112), calls=%async_computation.1 | async-start | bytes 786432 | tf_op jit(solution)/shard_map/all_to_all | solution.py:160
  42.1 0.0 collective-permute-done
  42.1 1.4 %maximum_select_fusion = bf16[1024,768]{1,0:T(8,128)(2,1)S(1)} fusion(bf16[512,768]{1,0:T(8,128)(2,1)S(1)} %collective-permute-done, bf16[256,768]{1,0:T(8,128)(2,1)S(1)} %bitcast.93, bf16[256,768]{1,0:T(8,128)(2,1)S(1)} %bitcast.91, bf16[256,768]{1,0:T(8,128)(2,1)} %bitcast.103, bf16[256,768]{1,0:T(8,128)(2,1)S(1)} %slice.54, pred[]{:T(512)S(6)} %eq.3, ...), kind=kLoop, calls=%fused_computation | loop fusion | flops 10223616 | bytes 3934209 | tf_op jit(solution)/shard_map/jit(_where)/select_n | solution.py:154
  43.6 13.4 %all-to-all-done.1 = bf16[32,8,768]{2,1,0:T(8,128)(2,1)S(1)} async-done(((bf16[32,8,768]{2,1,0:T(8,128)(2,1)}), bf16[32,8,768]{2,1,0:T(8,128)(2,1)S(1)}, u32[]{:S(2)}, u32[]{:S(2)}) %all-to-all-start.1) | async-done | bytes 393248 | tf_op jit(solution)/shard_map/all_to_all | solution.py:160
  56.9 0.6 convolution_convert_fusion
  57.5 11.3 %all_to_all.30 = bf16[8,32,1024]{2,1,0:T(8,128)(2,1)S(1)} all-to-all(bf16[8,32,1024]{2,1,0:T(8,128)(2,1)S(1)} %bitcast.94), channel_id=1, replica_groups=mesh['z'=8,'yh'=4,'core'=2,'yl'=2,'x'=4] {'yl','x'}, dimensions={0} | all-to-all | bytes 1048576 | tf_op jit(solution)/shard_map/all_to_all | solution.py:23
  68.8 0.1 convert_reduce_fusion
  68.9 5.8 %all-gather.1 = f32[64,1024]{1,0:T(8,128)S(1)} all-gather(f32[32,1024]{1,0:T(8,128)S(1)} %convert_reduce_fusion), channel_id=3, replica_groups=mesh['z'=8,'yh'=4,'core'=2,'yl'=2,'x'=4] {'core'}, dimensions={0}, use_global_device_ids=true | all-gather | bytes 393216 | tf_op jit(solution)/shard_map/all_gather | solution.py:34
  74.9 13.1 %all_to_all.31 = bf16[8,32,1280]{2,1,0:T(8,128)(2,1)S(1)} all-to-all(bf16[8,32,1280]{2,1,0:T(8,128)(2,1)S(1)} %broadcast_in_dim.16), channel_id=1, replica_groups=mesh['z'=8,'yh'=4,'core'=2,'yl'=2,'x'=4] {'yl','x'}, dimensions={0} | all-to-all | bytes 1310720 | tf_op jit(solution)/shard_map/all_to_all | solution.py:29
  87.9 1.3 convolution_convert_fusion.4
  89.3 6.3 %all-to-all-start.4 = ((bf16[32,8,768]{2,1,0:T(8,128)(2,1)}), bf16[32,8,768]{2,1,0:T(8,128)(2,1)S(1)}, u32[]{:S(2)}, u32[]{:S(2)}) async-start(bf16[32,8,768]{2,1,0:T(8,128)(2,1)} %bitcast.17), calls=%async_computation.4 | async-start | bytes 786432 | tf_op jit(solution)/shard_map/all_to_all | solution.py:23
  95.6 3.9 %collective-permute-start.1 = (bf16[256,768]{1,0:T(8,128)(2,1)S(1)}, bf16[256,768]{1,0:T(8,128)(2,1)S(1)}, u32[]{:S(2)}, u32[]{:S(2)}) collective-permute-start(bf16[256,768]{1,0:T(8,128)(2,1)S(1)} %bitcast.86), channel_id=1, source_target_pairs={{0,8},{8,0},{1,9},{9,1},{2,10},{10,2},{3,11},{11,3},{4,12},{12,4},... | collective-permute-start | bytes 1179656 | tf_op jit(solution)/shard_map/ppermute | solution.py:188
  99.5 1.3 collective-permute-done.1
  100.8 9.3 %all-to-all-done.4.blocks_ref = bf16[32,8,768]{2,1,0:T(8,128)(2,1)S(1)} async-done(((bf16[32,8,768]{2,1,0:T(8,128)(2,1)}), bf16[32,8,768]{2,1,0:T(8,128)(2,1)S(1)}, u32[]{:S(2)}, u32[]{:S(2)}) %all-to-all-start.4) | async-done | bytes 393248 | tf_op jit(solution)/shard_map/all_to_all | solution.py:23
  110.2 0.9 shard_map.113
  111.1 6.8 %all-to-all-start.5 = ((f32[32,8,128]{2,1,0:T(8,128)}), f32[32,8,128]{2,1,0:T(8,128)S(1)}, u32[]{:S(2)}, u32[]{:S(2)}) async-start(f32[32,8,128]{2,1,0:T(8,128)} %shard_map.113), calls=%async_computation.5 | async-start | bytes 262144 | tf_op jit(solution)/shard_map/all_to_all | solution.py:191
  117.9 1.1 fusion
  119.0 1.1 fusion.1
  120.1 1.1 fusion.2
  121.1 8.1 %all-to-all-done.5.arrived_ref = f32[32,8,128]{2,1,0:T(8,128)S(1)} async-done(((f32[32,8,128]{2,1,0:T(8,128)}), f32[32,8,128]{2,1,0:T(8,128)S(1)}, u32[]{:S(2)}, u32[]{:S(2)}) %all-to-all-start.5) | async-done | bytes 131104 | tf_op jit(solution)/shard_map/all_to_all | solution.py:191
  129.2 0.2 shard_map.114
  129.4 3.9 %all-gather.2 = bf16[64,768]{1,0:T(8,128)(2,1)S(1)} all-gather(bf16[32,768]{1,0:T(8,128)(2,1)S(1)} %shard_map.114), channel_id=4, replica_groups=mesh['z'=8,'yh'=4,'core'=2,'yl'=2,'x'=4] {'core'}, dimensions={0}, use_global_device_ids=true | all-gather | bytes 147456 | tf_op jit(solution)/shard_map/all_gather | solution.py:34
  133.3 0.6 constant_dynamic-slice_fusion
  (11 shorter events, 0.2 us)
Async XLA Ops:
  0.6 2.5 %copy-start.2 = (bf16[1,256,768]{2,1,0:T(8,128)(2,1)S(1)}, bf16[1,256,768]{2,1,0:T(8,128)(2,1)}, u32[]{:S(2)}) copy-start(bf16[1,256,768]{2,1,0:T(8,128)(2,1)} %param.13) | copy-start | bytes 1179652
  1.9 10.2 %copy-start.3 = (bf16[16,768]{1,0:T(8,128)(2,1)S(1)}, bf16[16,768]{1,0:T(8,128)(2,1)}, u32[]{:S(2)}) copy-start(bf16[16,768]{1,0:T(8,128)(2,1)} %param.8) | copy-start | bytes 73732
  1.9 10.2 %copy-start.4 = (bf16[16,768]{1,0:T(8,128)(2,1)S(1)}, bf16[16,768]{1,0:T(8,128)(2,1)}, u32[]{:S(2)}) copy-start(bf16[16,768]{1,0:T(8,128)(2,1)} %param.7) | copy-start | bytes 73732
  1.9 12.1 %copy-start = (s32[1,256]{1,0:T(1,128)S(1)}, s32[1,256]{1,0:T(1,128)}, u32[]{:S(2)}) copy-start(s32[1,256]{1,0:T(1,128)} %slots_ref.3) | copy-start | bytes 3076
  1.9 23.4 %copy-start.1 = (f32[1,256]{1,0:T(1,128)S(1)}, f32[1,256]{1,0:T(1,128)}, u32[]{:S(2)}) copy-start(f32[1,256]{1,0:T(1,128)} %gates_ref.1) | copy-start | bytes 3076
  3.3 38.8 %collective-permute-start = (bf16[512,768]{1,0:T(8,128)(2,1)S(1)}, bf16[512,768]{1,0:T(8,128)(2,1)S(1)}, u32[]{:S(2)}, u32[]{:S(2)}) collective-permute-start(bf16[512,768]{1,0:T(8,128)(2,1)S(1)} %maximum_select_fusion.1), channel_id=1, source_target_pairs={{0,8},{8,0},{1,9},{9,1},{2,10},{10,2},{3,11},{11,3},{4,12},{12,4},... | collective-permute-start | bytes 2359304 | tf_op jit(solution)/shard_map/ppermute | solution.py:153
  15.0 21.7 %all-to-all-start = ((f32[32,8,128]{2,1,0:T(8,128)}), f32[32,8,128]{2,1,0:T(8,128)S(1)}, u32[]{:S(2)}, u32[]{:S(2)}) async-start(f32[32,8,128]{2,1,0:T(8,128)} %get-tuple-element.20), calls=%async_computation | async-start | bytes 262144 | tf_op jit(solution)/shard_map/all_to_all | solution.py:143
  37.6 19.3 %all-to-all-start.1 = ((bf16[32,8,768]{2,1,0:T(8,128)(2,1)}), bf16[32,8,768]{2,1,0:T(8,128)(2,1)S(1)}, u32[]{:S(2)}, u32[]{:S(2)}) async-start(bf16[32,8,768]{2,1,0:T(8,128)(2,1)} %shard_map.112), calls=%async_computation.1 | async-start | bytes 786432 | tf_op jit(solution)/shard_map/all_to_all | solution.py:160
  89.3 20.9 %all-to-all-start.4 = ((bf16[32,8,768]{2,1,0:T(8,128)(2,1)}), bf16[32,8,768]{2,1,0:T(8,128)(2,1)S(1)}, u32[]{:S(2)}, u32[]{:S(2)}) async-start(bf16[32,8,768]{2,1,0:T(8,128)(2,1)} %bitcast.17), calls=%async_computation.4 | async-start | bytes 786432 | tf_op jit(solution)/shard_map/all_to_all | solution.py:23
  95.6 5.2 %collective-permute-start.1 = (bf16[256,768]{1,0:T(8,128)(2,1)S(1)}, bf16[256,768]{1,0:T(8,128)(2,1)S(1)}, u32[]{:S(2)}, u32[]{:S(2)}) collective-permute-start(bf16[256,768]{1,0:T(8,128)(2,1)S(1)} %bitcast.86), channel_id=1, source_target_pairs={{0,8},{8,0},{1,9},{9,1},{2,10},{10,2},{3,11},{11,3},{4,12},{12,4},... | collective-permute-start | bytes 1179656 | tf_op jit(solution)/shard_map/ppermute | solution.py:188
  111.1 18.1 %all-to-all-start.5 = ((f32[32,8,128]{2,1,0:T(8,128)}), f32[32,8,128]{2,1,0:T(8,128)S(1)}, u32[]{:S(2)}, u32[]{:S(2)}) async-start(f32[32,8,128]{2,1,0:T(8,128)} %shard_map.113), calls=%async_computation.5 | async-start | bytes 262144 | tf_op jit(solution)/shard_map/all_to_all | solution.py:191

commit v5 on v4

--- a/solution.py
+++ b/solution.py
@@ -50,6 +50,7 @@
 
 
 LANES = 128
+ID_BASE = 32
 SEGMENTS = 8
 
 
@@ -65,13 +66,15 @@
     return jnp.concatenate([ref[:, k, :] for k in range(used)], axis=1).astype(BF16)
 
 
-def send_tokens(slots_ref, pairs_ref, out_ref, pick_ref):
+def send_tokens(n_slots, pairs_ref, out_ref, pick_ref):
     n_tok, n_chips = pick_ref.shape
-    n_slots = slots_ref.shape[1]
+    n_own = n_tok // 2
+    width = pairs_ref.shape[2] // 2
     chip = lax.axis_index("z") * lax.axis_size("yh") + lax.axis_index("yh")
-    slots = slots_ref[...]
-
-    ids = chip * n_tok + lax.broadcasted_iota(jnp.int32, (n_tok, n_slots), 0)
+    parts = pairs_ref[0, n_own:, :n_slots].astype(F32)
+    slots = parts[0:1] * float(ID_BASE) + parts[1:2]
+
+    ids = (chip * n_tok + lax.broadcasted_iota(jnp.int32, (n_tok, n_slots), 0)).astype(F32)
     row = jnp.broadcast_to(slots, (n_tok, n_slots))
     rank = jnp.sum(jnp.where(row < ids, 1.0, 0.0), axis=1, keepdims=True).astype(jnp.int32)
     held = jnp.sum(jnp.where(row == ids, 1.0, 0.0), axis=1, keepdims=True)
@@ -79,10 +82,13 @@
     lane = jnp.where(held > 0.0, lax.rem(rank, n_chips), -1)
     pick_ref[...] = jnp.where(peer == lane, 1.0, 0.0).astype(BF16)
 
-    width = pairs_ref.shape[1] // 2
     first = lax.axis_index("core") == 0
-    rows = jnp.where(first, pairs_ref[:, :width].astype(F32), pairs_ref[:, width:].astype(F32))
-    to_messages(dot(pick_ref[...], rows.astype(BF16), ((0,), (0,))), out_ref)
+    here = [
+        jnp.where(first, pairs_ref[c, :n_own, :width].astype(F32), pairs_ref[c, :n_own, width:].astype(F32))
+        for c in range(2)
+    ]
+    rows = jnp.concatenate(here, axis=0).astype(BF16)
+    to_messages(dot(pick_ref[...], rows, ((0,), (0,))), out_ref)
 
 
 def find_slots(n_tok, slots_ref, gates_ref, place_ref, my_gates_ref):
@@ -137,9 +143,15 @@
     per_chip = n_slots // n_chips
     blocks = (n_chips, SEGMENTS, LANES)
 
-    pairs = from_cores(jnp.concatenate([tokens, cotangent], axis=1)).reshape(2 * n_own, 2 * width)
     slots = slot_token.reshape(1, -1)
-    sent, pick = on_vmem(send_tokens, ((blocks, F32), ((2 * n_own, n_chips), BF16)), slots, pairs)
+    ids = jnp.concatenate([slots // ID_BASE, slots % ID_BASE], axis=0).astype(BF16)
+    ids = jnp.pad(ids, ((0, n_own - 2), (0, 2 * width - n_slots)))
+    pairs = from_cores(jnp.concatenate([jnp.concatenate([tokens, cotangent], axis=1), ids], axis=0))
+    sent, pick = on_vmem(
+        functools.partial(send_tokens, n_slots),
+        ((blocks, F32), ((2 * n_own, n_chips), BF16)),
+        pairs,
+    )
     arrived = lax.all_to_all(sent, CHIPS, 0, 0, tiled=True)
     place, my_gates = on_vmem(
         functools.partial(find_slots, 2 * n_own),
@@ -147,20 +159,21 @@
         slots,
         slot_gate.reshape(1, -1),
     )
-    gate_up = jnp.concatenate([w_gate.T, w_up.T], axis=0)
-    blank = jnp.zeros_like(w_down)
-    theirs = jnp.where(first, jnp.concatenate([w_down, blank], axis=0), gate_up)
+    down = w_down.T
+    blank = jnp.zeros_like(down)
+    gate_up = jnp.concatenate([w_gate, w_up], axis=1)
+    theirs = jnp.where(first, jnp.concatenate([down, blank], axis=1), gate_up)
     theirs = lax.ppermute(theirs, "core", [(0, 1), (1, 0)])
     weights = jnp.where(
         first,
-        jnp.concatenate([gate_up, theirs], axis=0),
-        jnp.concatenate([theirs[:n_ff], w_down, blank, blank], axis=0),
+        jnp.concatenate([gate_up, theirs], axis=1),
+        jnp.concatenate([theirs[:, :n_ff], down, blank, blank], axis=1),
     )
     (copies,) = on_vmem(receive_tokens, (((n_chips, per_chip, width), BF16),), place, my_gates, arrived)
     rows = lax.all_to_all(copies, CHIPS, 0, 0, tiled=True).reshape(n_slots, width)
     weights, rows = lax.optimization_barrier((weights, rows))
 
-    parts = dot(rows, weights, ((1,), (1,))).astype(BF16)
+    parts = dot(rows, weights, ((1,), (0,))).astype(BF16)
     sums = jnp.sum(exchange(parts, SHARD).astype(F32), axis=0)
     sums = from_cores(sums)
     trios = []
@@ -177,16 +190,14 @@
             )
         )
     (h0, g0, u0), (h1, g1, u1) = trios
-    factors = jnp.concatenate(
-        [jnp.where(first, g0, h0), jnp.where(first, u0, h1), g1, u1, jnp.where(first, h0, h1)], axis=1
-    )
+    factors = jnp.concatenate([jnp.where(first, g0, h0), jnp.where(first, u0, h1), g1, u1], axis=1)
     factors = spread(factors, SHARD)
 
-    total = dot(factors[:, : 4 * n_ff], weights, ((1,), (0,))).astype(BF16)
-    total, rows = lax.optimization_barrier((total, rows))
+    total = dot(factors, weights, ((1,), (1,))).astype(BF16)
+    total, rows, factors = lax.optimization_barrier((total, rows, factors))
     summands = exchange(total, CHIPS)
-    other_rows = lax.ppermute(rows, "core", [(0, 1), (1, 0)])
-    factors, rows, other_rows, summands = lax.optimization_barrier((factors, rows, other_rows, summands))
+    other = lax.ppermute(jnp.concatenate([rows, factors[:, :n_ff]], axis=1), "core", [(0, 1), (1, 0)])
+    factors, rows, other, summands = lax.optimization_barrier((factors, rows, other, summands))
     (back,) = on_vmem(send_slots, ((blocks, F32),), place, my_gates, summands)
     returned = lax.all_to_all(back, CHIPS, 0, 0, tiled=True)
     (chip_out,) = on_vmem(receive_slots, (((2 * n_own, width), BF16),), pick, returned)
@@ -194,9 +205,9 @@
     grad_tokens = lax.dynamic_slice_in_dim(done[0], core * n_own, n_own, 0)
     mixed = lax.dynamic_slice_in_dim(done[1], core * n_own, n_own, 0)
 
-    inputs = jnp.where(first, rows, other_rows)
-    scaled = jnp.where(first, other_rows, rows)
-    hidden = factors[:, 4 * n_ff :]
+    inputs = jnp.where(first, rows, other[:, :width])
+    scaled = jnp.where(first, other[:, :width], rows)
+    hidden = jnp.where(first, other[:, width:], factors[:, n_ff : 2 * n_ff])
     grad_pre = lax.dynamic_slice_in_dim(factors, core * 2 * n_ff, 2 * n_ff, 1)
     grad_down = dot(hidden, scaled, ((0,), (0,))).astype(BF16)
     grad_gate = dot(inputs, grad_pre[:, :n_ff], ((0,), (0,))).astype(BF16)

time: 135 us -> 132 us (0.978)
  waiting for transfers between devices: 43.2 us -> 40.6 us
  starting transfers between devices: 40.6 us -> 43.1 us
  blocking collectives: 35.9 us -> 33.7 us
    all_to_all x1, waiting for transfers between devices: 9.34 us -> 6.66 us  [exchange(): return lax.all_to_all(blocks, axes, 0, 0, tiled=True)]
    all_to_all x1, starting transfers between devices: 6.81 us -> 8.83 us  [on_device(): returned = lax.all_to_all(back, CHIPS, 0, 0, tiled=True)]
    all_to_all x1, blocking collectives: 13.1 us -> 11.1 us  [spread(): out = lax.all_to_all(blocks, axes, 0, 0, tiled=True)]
where the time goes in v5:
time: 132 us
  starting transfers between devices  43.1 us (33%)
  waiting for transfers between devices  40.6 us (31%)
  blocking collectives  33.7 us (26%)
  matrix products  5.16 us (4%)
  Pallas kernels  3.26 us (2%)
  local copies, waits for them, and re-layouts  3.16 us (2%)
  other arithmetic  1.84 us (1%)
    all_to_all x1, waiting for transfers between devices, on_device(): lax.all_to_all(copies, CHIPS, 0, 0, tiled=True).reshape(n_slots, width)  13.4 us
    all_to_all x1, blocking collectives, exchange(): return lax.all_to_all(blocks, axes, 0, 0, tiled=True)  11.3 us
    all_gather x3, blocking collectives, from_cores(): return lax.all_gather(rows, 'core', axis=0, tiled=False)  11.2 us
    all_to_all x1, blocking collectives, spread(): out = lax.all_to_all(blocks, axes, 0, 0, tiled=True)  11.1 us
    all_to_all x1, waiting for transfers between devices, on_device(): arrived = lax.all_to_all(sent, CHIPS, 0, 0, tiled=True)  11 us
    all_to_all x1, starting transfers between devices, on_device(): arrived = lax.all_to_all(sent, CHIPS, 0, 0, tiled=True)  10.3 us
    all_to_all x1, starting transfers between devices, on_device(): returned = lax.all_to_all(back, CHIPS, 0, 0, tiled=True)  8.83 us
    ppermute x1, starting transfers between devices, on_device(): theirs = lax.ppermute(theirs, 'core', [(0, 1), (1, 0)])  8.75 us
  transfers between devices with their start and end apart: 6, of which 5 were waited for; matrix products, arithmetic and copies ran while one was open for 4% of the time, Pallas kernels for 2%

profile of v5, /device:TPU:1, one launch (start us, length us, event | category | flops | bytes accessed | tf_op | source)
XLA Modules:
  0.0 131.7 jit_solution(14336624879169763457)
XLA Ops:
  0.6 0.0 copy-start.2
  0.6 1.2 copy.12
  1.9 0.0 copy-start
  1.9 0.0 copy-start.3
  1.9 0.0 copy-start.4
  1.9 1.2 copy.13
  3.1 0.0 copy-start.1
  3.1 0.0 copy-done.2
  3.1 0.2 maximum_select_fusion.1
  3.3 8.7 %collective-permute-start = (bf16[768,512]{0,1:T(8,128)(2,1)S(1)}, bf16[768,512]{0,1:T(8,128)(2,1)S(1)}, u32[]{:S(2)}, u32[]{:S(2)}) collective-permute-start(bf16[768,512]{0,1:T(8,128)(2,1)S(1)} %maximum_select_fusion.1), channel_id=1, source_target_pairs={{0,8},{8,0},{1,9},{9,1},{2,10},{10,2},{3,11},{11,3},{4,12},{12,4},... | collective-permute-start | bytes 2359304 | tf_op jit(solution)/shard_map/ppermute | solution.py:166
  12.0 0.0 copy-done
  12.1 0.0 copy-done.3
  12.1 0.0 copy-done.4
  12.1 1.9 %all-gather = bf16[64,1536]{1,0:T(8,128)(2,1)S(1)} all-gather(bf16[32,1536]{1,0:T(8,128)(2,1)S(1)} %pad_maximum_fusion.1), channel_id=2, replica_groups=mesh['z'=8,'yh'=4,'core'=2,'yl'=2,'x'=4] {'core'}, dimensions={0}, use_global_device_ids=true | all-gather | bytes 294912 | tf_op jit(solution)/shard_map/all_gather | solution.py:34
  14.1 1.0 shard_map.110
  15.1 10.3 %all-to-all-start = ((f32[32,8,128]{2,1,0:T(8,128)}), f32[32,8,128]{2,1,0:T(8,128)S(1)}, u32[]{:S(2)}, u32[]{:S(2)}) async-start(f32[32,8,128]{2,1,0:T(8,128)} %get-tuple-element.21), calls=%async_computation | async-start | bytes 262144 | tf_op jit(solution)/shard_map/all_to_all | solution.py:155
  25.4 0.0 copy-done.1
  25.4 0.3 shard_map.111
  25.7 11.0 %all-to-all-done.arrived_ref = f32[32,8,128]{2,1,0:T(8,128)S(1)} async-done(((f32[32,8,128]{2,1,0:T(8,128)}), f32[32,8,128]{2,1,0:T(8,128)S(1)}, u32[]{:S(2)}, u32[]{:S(2)}) %all-to-all-start) | async-done | bytes 131104 | tf_op jit(solution)/shard_map/all_to_all | solution.py:155
  36.7 0.9 shard_map.112
  37.7 4.5 %all-to-all-start.1 = ((bf16[32,8,768]{2,1,0:T(8,128)(2,1)}), bf16[32,8,768]{2,1,0:T(8,128)(2,1)S(1)}, u32[]{:S(2)}, u32[]{:S(2)}) async-start(bf16[32,8,768]{2,1,0:T(8,128)(2,1)} %shard_map.112), calls=%async_computation.1 | async-start | bytes 786432 | tf_op jit(solution)/shard_map/all_to_all | solution.py:173
  42.1 0.0 collective-permute-done
  42.2 1.4 %maximum_select_fusion = bf16[768,1024]{0,1:T(8,128)(2,1)S(1)} fusion(bf16[768,512]{0,1:T(8,128)(2,1)S(1)} %collective-permute-done, bf16[768,256]{0,1:T(8,128)(2,1)S(1)} %bitcast.88, bf16[768,256]{0,1:T(8,128)(2,1)S(1)} %bitcast.86, bf16[768,256]{0,1:T(8,128)(2,1)} %bitcast.90, bf16[768,256]{0,1:T(8,128)(2,1)S(1)} %slice.63, pred[]{:T(512)S(6)} %eq.5, ...), kind=kLoop, calls=%fused_computation | loop fusion | flops 10223616 | bytes 3934209 | tf_op jit(solution)/shard_map/jit(_where)/select_n | solution.py:167
  43.6 13.4 %all-to-all-done.1 = bf16[32,8,768]{2,1,0:T(8,128)(2,1)S(1)} async-done(((bf16[32,8,768]{2,1,0:T(8,128)(2,1)}), bf16[32,8,768]{2,1,0:T(8,128)(2,1)S(1)}, u32[]{:S(2)}, u32[]{:S(2)}) %all-to-all-start.1) | async-done | bytes 393248 | tf_op jit(solution)/shard_map/all_to_all | solution.py:173
  57.0 0.6 convolution_convert_fusion
  57.6 11.3 %all_to_all.30 = bf16[8,32,1024]{2,1,0:T(8,128)(2,1)S(1)} all-to-all(bf16[8,32,1024]{2,1,0:T(8,128)(2,1)S(1)} %bitcast.89), channel_id=1, replica_groups=mesh['z'=8,'yh'=4,'core'=2,'yl'=2,'x'=4] {'yl','x'}, dimensions={0} | all-to-all | bytes 1048576 | tf_op jit(solution)/shard_map/all_to_all | solution.py:23
  68.9 0.1 convert_reduce_fusion
  69.0 5.8 %all-gather.1 = f32[64,1024]{1,0:T(8,128)S(1)} all-gather(f32[32,1024]{1,0:T(8,128)S(1)} %convert_reduce_fusion), channel_id=3, replica_groups=mesh['z'=8,'yh'=4,'core'=2,'yl'=2,'x'=4] {'core'}, dimensions={0}, use_global_device_ids=true | all-gather | bytes 393216 | tf_op jit(solution)/shard_map/all_gather | solution.py:34
  74.8 0.1 broadcast_in_dim.16
  74.9 11.1 %all_to_all.31 = bf16[8,32,1024]{2,1,0:T(8,128)(2,1)S(1)} all-to-all(bf16[8,32,1024]{2,1,0:T(8,128)(2,1)S(1)} %broadcast_in_dim.16), channel_id=1, replica_groups=mesh['z'=8,'yh'=4,'core'=2,'yl'=2,'x'=4] {'yl','x'}, dimensions={0} | all-to-all | bytes 1048576 | tf_op jit(solution)/shard_map/all_to_all | solution.py:29
  86.0 1.3 convolution_convert_fusion.4
  87.3 6.3 %all-to-all-start.4 = ((bf16[32,8,768]{2,1,0:T(8,128)(2,1)}), bf16[32,8,768]{2,1,0:T(8,128)(2,1)S(1)}, u32[]{:S(2)}, u32[]{:S(2)}) async-start(bf16[32,8,768]{2,1,0:T(8,128)(2,1)} %bitcast.16), calls=%async_computation.4 | async-start | bytes 786432 | tf_op jit(solution)/shard_map/all_to_all | solution.py:23
  93.6 0.1 pad_maximum_fusion
  93.7 4.5 %collective-permute-start.1 = (bf16[256,1024]{1,0:T(8,128)(2,1)S(1)}, bf16[256,1024]{1,0:T(8,128)(2,1)S(1)}, u32[]{:S(2)}, u32[]{:S(2)}) collective-permute-start(bf16[256,1024]{1,0:T(8,128)(2,1)S(1)} %pad_maximum_fusion), channel_id=1, source_target_pairs={{0,8},{8,0},{1,9},{9,1},{2,10},{10,2},{3,11},{11,3},{4,12},{12,4},... | collective-permute-start | bytes 1572872 | tf_op jit(solution)/shard_map/ppermute | solution.py:199
  98.2 1.5 %collective-permute-done.1 = bf16[256,1024]{1,0:T(8,128)(2,1)S(1)} collective-permute-done((bf16[256,1024]{1,0:T(8,128)(2,1)S(1)}, bf16[256,1024]{1,0:T(8,128)(2,1)S(1)}, u32[]{:S(2)}, u32[]{:S(2)}) %collective-permute-start.1) | collective-permute-done | bytes 524320 | tf_op jit(solution)/shard_map/ppermute | solution.py:199
  99.7 6.7 %all-to-all-done.4.blocks_ref = bf16[32,8,768]{2,1,0:T(8,128)(2,1)S(1)} async-done(((bf16[32,8,768]{2,1,0:T(8,128)(2,1)}), bf16[32,8,768]{2,1,0:T(8,128)(2,1)S(1)}, u32[]{:S(2)}, u32[]{:S(2)}) %all-to-all-start.4) | async-done | bytes 393248 | tf_op jit(solution)/shard_map/all_to_all | solution.py:23
  106.3 0.9 shard_map.113
  107.2 8.8 %all-to-all-start.5 = ((f32[32,8,128]{2,1,0:T(8,128)}), f32[32,8,128]{2,1,0:T(8,128)S(1)}, u32[]{:S(2)}, u32[]{:S(2)}) async-start(f32[32,8,128]{2,1,0:T(8,128)} %shard_map.113), calls=%async_computation.5 | async-start | bytes 262144 | tf_op jit(solution)/shard_map/all_to_all | solution.py:202
  116.1 1.1 fusion
  117.2 1.1 fusion.1
  118.2 1.1 fusion.2
  119.3 8.1 %all-to-all-done.5.arrived_ref = f32[32,8,128]{2,1,0:T(8,128)S(1)} async-done(((f32[32,8,128]{2,1,0:T(8,128)}), f32[32,8,128]{2,1,0:T(8,128)S(1)}, u32[]{:S(2)}, u32[]{:S(2)}) %all-to-all-start.5) | async-done | bytes 131104 | tf_op jit(solution)/shard_map/all_to_all | solution.py:202
  127.4 0.2 shard_map.114
  127.6 3.5 %all-gather.2 = bf16[64,768]{1,0:T(8,128)(2,1)S(1)} all-gather(bf16[32,768]{1,0:T(8,128)(2,1)S(1)} %shard_map.114), channel_id=4, replica_groups=mesh['z'=8,'yh'=4,'core'=2,'yl'=2,'x'=4] {'core'}, dimensions={0}, use_global_device_ids=true | all-gather | bytes 147456 | tf_op jit(solution)/shard_map/all_gather | solution.py:34
  131.1 0.6 constant_dynamic-slice_fusion
  (12 shorter events, 0.2 us)
Async XLA Ops:
  0.6 2.5 %copy-start.2 = (bf16[1,256,768]{2,1,0:T(8,128)(2,1)S(1)}, bf16[1,256,768]{2,1,0:T(8,128)(2,1)}, u32[]{:S(2)}) copy-start(bf16[1,256,768]{2,1,0:T(8,128)(2,1)} %param.13) | copy-start | bytes 1179652
  1.9 10.2 %copy-start = (s32[1,256]{1,0:T(1,128)S(1)}, s32[1,256]{1,0:T(1,128)}, u32[]{:S(2)}) copy-start(s32[1,256]{1,0:T(1,128)} %slots_ref.1) | copy-start | bytes 3076
  1.9 10.2 %copy-start.3 = (bf16[16,768]{1,0:T(8,128)(2,1)S(1)}, bf16[16,768]{1,0:T(8,128)(2,1)}, u32[]{:S(2)}) copy-start(bf16[16,768]{1,0:T(8,128)(2,1)} %param.8) | copy-start | bytes 73732
  1.9 10.2 %copy-start.4 = (bf16[16,768]{1,0:T(8,128)(2,1)S(1)}, bf16[16,768]{1,0:T(8,128)(2,1)}, u32[]{:S(2)}) copy-start(bf16[16,768]{1,0:T(8,128)(2,1)} %param.7) | copy-start | bytes 73732
  3.1 22.3 %copy-start.1 = (f32[1,256]{1,0:T(1,128)S(1)}, f32[1,256]{1,0:T(1,128)}, u32[]{:S(2)}) copy-start(f32[1,256]{1,0:T(1,128)} %gates_ref.1) | copy-start | bytes 3076
  3.3 38.9 %collective-permute-start = (bf16[768,512]{0,1:T(8,128)(2,1)S(1)}, bf16[768,512]{0,1:T(8,128)(2,1)S(1)}, u32[]{:S(2)}, u32[]{:S(2)}) collective-permute-start(bf16[768,512]{0,1:T(8,128)(2,1)S(1)} %maximum_select_fusion.1), channel_id=1, source_target_pairs={{0,8},{8,0},{1,9},{9,1},{2,10},{10,2},{3,11},{11,3},{4,12},{12,4},... | collective-permute-start | bytes 2359304 | tf_op jit(solution)/shard_map/ppermute | solution.py:166
  15.1 21.7 %all-to-all-start = ((f32[32,8,128]{2,1,0:T(8,128)}), f32[32,8,128]{2,1,0:T(8,128)S(1)}, u32[]{:S(2)}, u32[]{:S(2)}) async-start(f32[32,8,128]{2,1,0:T(8,128)} %get-tuple-element.21), calls=%async_computation | async-start | bytes 262144 | tf_op jit(solution)/shard_map/all_to_all | solution.py:155
  37.7 19.3 %all-to-all-start.1 = ((bf16[32,8,768]{2,1,0:T(8,128)(2,1)}), bf16[32,8,768]{2,1,0:T(8,128)(2,1)S(1)}, u32[]{:S(2)}, u32[]{:S(2)}) async-start(bf16[32,8,768]{2,1,0:T(8,128)(2,1)} %shard_map.112), calls=%async_computation.1 | async-start | bytes 786432 | tf_op jit(solution)/shard_map/all_to_all | solution.py:173
  87.3 19.0 %all-to-all-start.4 = ((bf16[32,8,768]{2,1,0:T(8,128)(2,1)}), bf16[32,8,768]{2,1,0:T(8,128)(2,1)S(1)}, u32[]{:S(2)}, u32[]{:S(2)}) async-start(bf16[32,8,768]{2,1,0:T(8,128)(2,1)} %bitcast.16), calls=%async_computation.4 | async-start | bytes 786432 | tf_op jit(solution)/shard_map/all_to_all | solution.py:23
  93.7 6.0 %collective-permute-start.1 = (bf16[256,1024]{1,0:T(8,128)(2,1)S(1)}, bf16[256,1024]{1,0:T(8,128)(2,1)S(1)}, u32[]{:S(2)}, u32[]{:S(2)}) collective-permute-start(bf16[256,1024]{1,0:T(8,128)(2,1)S(1)} %pad_maximum_fusion), channel_id=1, source_target_pairs={{0,8},{8,0},{1,9},{9,1},{2,10},{10,2},{3,11},{11,3},{4,12},{12,4},... | collective-permute-start | bytes 1572872 | tf_op jit(solution)/shard_map/ppermute | solution.py:199
  107.2 20.2 %all-to-all-start.5 = ((f32[32,8,128]{2,1,0:T(8,128)}), f32[32,8,128]{2,1,0:T(8,128)S(1)}, u32[]{:S(2)}, u32[]{:S(2)}) async-start(f32[32,8,128]{2,1,0:T(8,128)} %shard_map.113), calls=%async_computation.5 | async-start | bytes 262144 | tf_op jit(solution)/shard_map/all_to_all | solution.py:202

commit v6 on v5

--- a/solution.py
+++ b/solution.py
@@ -50,7 +50,6 @@
 
 
 LANES = 128
-ID_BASE = 32
 SEGMENTS = 8
 
 
@@ -66,13 +65,13 @@
     return jnp.concatenate([ref[:, k, :] for k in range(used)], axis=1).astype(BF16)
 
 
-def send_tokens(n_slots, pairs_ref, out_ref, pick_ref):
+def send_tokens(slots_ref, pairs_ref, out_ref, pick_ref):
     n_tok, n_chips = pick_ref.shape
     n_own = n_tok // 2
     width = pairs_ref.shape[2] // 2
     chip = lax.axis_index("z") * lax.axis_size("yh") + lax.axis_index("yh")
-    parts = pairs_ref[0, n_own:, :n_slots].astype(F32)
-    slots = parts[0:1] * float(ID_BASE) + parts[1:2]
+    slots = slots_ref[...].astype(F32)
+    n_slots = slots.shape[1]
 
     ids = (chip * n_tok + lax.broadcasted_iota(jnp.int32, (n_tok, n_slots), 0)).astype(F32)
     row = jnp.broadcast_to(slots, (n_tok, n_slots))
@@ -144,14 +143,8 @@
     blocks = (n_chips, SEGMENTS, LANES)
 
     slots = slot_token.reshape(1, -1)
-    ids = jnp.concatenate([slots // ID_BASE, slots % ID_BASE], axis=0).astype(BF16)
-    ids = jnp.pad(ids, ((0, n_own - 2), (0, 2 * width - n_slots)))
-    pairs = from_cores(jnp.concatenate([jnp.concatenate([tokens, cotangent], axis=1), ids], axis=0))
-    sent, pick = on_vmem(
-        functools.partial(send_tokens, n_slots),
-        ((blocks, F32), ((2 * n_own, n_chips), BF16)),
-        pairs,
-    )
+    pairs = from_cores(jnp.concatenate([tokens, cotangent], axis=1))
+    sent, pick = on_vmem(send_tokens, ((blocks, F32), ((2 * n_own, n_chips), BF16)), slots, pairs)
     arrived = lax.all_to_all(sent, CHIPS, 0, 0, tiled=True)
     place, my_gates = on_vmem(
         functools.partial(find_slots, 2 * n_own),
@@ -170,7 +163,8 @@
         jnp.concatenate([theirs[:, :n_ff], down, blank, blank], axis=1),
     )
     (copies,) = on_vmem(receive_tokens, (((n_chips, per_chip, width), BF16),), place, my_gates, arrived)
-    rows = lax.all_to_all(copies, CHIPS, 0, 0, tiled=True).reshape(n_slots, width)
+    rows = lax.all_to_all(copies, CHIPS, 0, 0, tiled=True)
+    rows = rows.reshape(n_slots, width)
     weights, rows = lax.optimization_barrier((weights, rows))
 
     parts = dot(rows, weights, ((1,), (0,))).astype(BF16)
@@ -197,7 +191,7 @@
     total, rows, factors = lax.optimization_barrier((total, rows, factors))
     summands = exchange(total, CHIPS)
     other = lax.ppermute(jnp.concatenate([rows, factors[:, :n_ff]], axis=1), "core", [(0, 1), (1, 0)])
-    factors, rows, other, summands = lax.optimization_barrier((factors, rows, other, summands))
+    factors, rows, other = lax.optimization_barrier((factors, rows, other))
     (back,) = on_vmem(send_slots, ((blocks, F32),), place, my_gates, summands)
     returned = lax.all_to_all(back, CHIPS, 0, 0, tiled=True)
     (chip_out,) = on_vmem(receive_slots, (((2 * n_own, width), BF16),), pick, returned)

time: 132 us -> 132 us (level)
  no operation moved by 1% of the time
where the time goes in v6:
time: 132 us
  starting transfers between devices  43.1 us (33%)
  waiting for transfers between devices  40.6 us (31%)
  blocking collectives  33.7 us (26%)
  matrix products  5.17 us (4%)
  Pallas kernels  3.28 us (2%)
  local copies, waits for them, and re-layouts  3.16 us (2%)
  other arithmetic  1.8 us (1%)
    all_to_all x1, waiting for transfers between devices, on_device(): rows = lax.all_to_all(copies, CHIPS, 0, 0, tiled=True)  13.4 us
    all_to_all x1, blocking collectives, exchange(): return lax.all_to_all(blocks, axes, 0, 0, tiled=True)  11.3 us
    all_gather x3, blocking collectives, from_cores(): return lax.all_gather(rows, 'core', axis=0, tiled=False)  11.3 us
    all_to_all x1, blocking collectives, spread(): out = lax.all_to_all(blocks, axes, 0, 0, tiled=True)  11.1 us
    all_to_all x1, waiting for transfers between devices, on_device(): arrived = lax.all_to_all(sent, CHIPS, 0, 0, tiled=True)  11 us
    all_to_all x1, starting transfers between devices, on_device(): arrived = lax.all_to_all(sent, CHIPS, 0, 0, tiled=True)  10.3 us
    all_to_all x1, waiting for transfers between devices, on_device(): returned = lax.all_to_all(back, CHIPS, 0, 0, tiled=True)  9.14 us
    all_to_all x1, starting transfers between devices, on_device(): returned = lax.all_to_all(back, CHIPS, 0, 0, tiled=True)  8.84 us
  transfers between devices with their start and end apart: 6, of which 5 were waited for; matrix products, arithmetic and copies ran while one was open for 4% of the time, Pallas kernels for 2%

profile of v6, /device:TPU:1, one launch (start us, length us, event | category | flops | bytes accessed | tf_op | source)
XLA Modules:
  0.0 131.8 jit_solution(10161735733561184580)
XLA Ops:
  0.6 0.0 copy-start.2
  0.6 1.2 copy.12
  1.9 0.0 copy-start.3
  1.9 0.0 copy-start.4
  1.9 0.0 copy-start
  1.9 0.0 copy-start.1
  1.9 1.2 copy.13
  3.1 0.0 copy-done.2
  3.1 0.2 maximum_select_fusion.1
  3.3 8.7 %collective-permute-start = (bf16[768,512]{0,1:T(8,128)(2,1)S(1)}, bf16[768,512]{0,1:T(8,128)(2,1)S(1)}, u32[]{:S(2)}, u32[]{:S(2)}) collective-permute-start(bf16[768,512]{0,1:T(8,128)(2,1)S(1)} %maximum_select_fusion.1), channel_id=1, source_target_pairs={{0,8},{8,0},{1,9},{9,1},{2,10},{10,2},{3,11},{11,3},{4,12},{12,4},... | collective-permute-start | bytes 2359304 | tf_op jit(solution)/shard_map/ppermute | solution.py:159
  12.0 0.0 copy-done.3
  12.1 0.0 copy-done.4
  12.1 1.9 %all-gather = bf16[32,1536]{1,0:T(8,128)(2,1)S(1)} all-gather(bf16[16,1536]{1,0:T(8,128)(2,1)S(1)} %pad_maximum_fusion.2), channel_id=2, replica_groups=mesh['z'=8,'yh'=4,'core'=2,'yl'=2,'x'=4] {'core'}, dimensions={0}, use_global_device_ids=true | all-gather | bytes 147456 | tf_op jit(solution)/shard_map/all_gather | solution.py:34
  14.0 0.0 copy-done
  14.0 1.0 shard_map.110
  15.0 10.3 %all-to-all-start = ((f32[32,8,128]{2,1,0:T(8,128)}), f32[32,8,128]{2,1,0:T(8,128)S(1)}, u32[]{:S(2)}, u32[]{:S(2)}) async-start(f32[32,8,128]{2,1,0:T(8,128)} %get-tuple-element.20), calls=%async_computation | async-start | bytes 262144 | tf_op jit(solution)/shard_map/all_to_all | solution.py:148
  25.3 0.0 copy-done.1
  25.3 0.3 shard_map.111
  25.6 11.0 %all-to-all-done.arrived_ref = f32[32,8,128]{2,1,0:T(8,128)S(1)} async-done(((f32[32,8,128]{2,1,0:T(8,128)}), f32[32,8,128]{2,1,0:T(8,128)S(1)}, u32[]{:S(2)}, u32[]{:S(2)}) %all-to-all-start) | async-done | bytes 131104 | tf_op jit(solution)/shard_map/all_to_all | solution.py:148
  36.6 0.9 shard_map.112
  37.6 4.5 %all-to-all-start.1 = ((bf16[32,8,768]{2,1,0:T(8,128)(2,1)}), bf16[32,8,768]{2,1,0:T(8,128)(2,1)S(1)}, u32[]{:S(2)}, u32[]{:S(2)}) async-start(bf16[32,8,768]{2,1,0:T(8,128)(2,1)} %shard_map.112), calls=%async_computation.1 | async-start | bytes 786432 | tf_op jit(solution)/shard_map/all_to_all | solution.py:166
  42.1 0.0 collective-permute-done
  42.1 1.4 %maximum_select_fusion = bf16[768,1024]{0,1:T(8,128)(2,1)S(1)} fusion(bf16[768,512]{0,1:T(8,128)(2,1)S(1)} %collective-permute-done, bf16[768,256]{0,1:T(8,128)(2,1)S(1)} %bitcast.88, bf16[768,256]{0,1:T(8,128)(2,1)S(1)} %bitcast.86, bf16[768,256]{0,1:T(8,128)(2,1)} %bitcast.90, bf16[768,256]{0,1:T(8,128)(2,1)S(1)} %slice.63, pred[]{:T(512)S(6)} %eq.3, ...), kind=kLoop, calls=%fused_computation | loop fusion | flops 10223616 | bytes 3934209 | tf_op jit(solution)/shard_map/jit(_where)/select_n | solution.py:160
  43.6 13.4 %all-to-all-done.1 = bf16[32,8,768]{2,1,0:T(8,128)(2,1)S(1)} async-done(((bf16[32,8,768]{2,1,0:T(8,128)(2,1)}), bf16[32,8,768]{2,1,0:T(8,128)(2,1)S(1)}, u32[]{:S(2)}, u32[]{:S(2)}) %all-to-all-start.1) | async-done | bytes 393248 | tf_op jit(solution)/shard_map/all_to_all | solution.py:166
  56.9 0.6 convolution_convert_fusion
  57.5 11.3 %all_to_all.30 = bf16[8,32,1024]{2,1,0:T(8,128)(2,1)S(1)} all-to-all(bf16[8,32,1024]{2,1,0:T(8,128)(2,1)S(1)} %bitcast.89), channel_id=1, replica_groups=mesh['z'=8,'yh'=4,'core'=2,'yl'=2,'x'=4] {'yl','x'}, dimensions={0} | all-to-all | bytes 1048576 | tf_op jit(solution)/shard_map/all_to_all | solution.py:23
  68.8 0.1 convert_reduce_fusion
  68.9 5.8 %all-gather.1 = f32[64,1024]{1,0:T(8,128)S(1)} all-gather(f32[32,1024]{1,0:T(8,128)S(1)} %convert_reduce_fusion), channel_id=3, replica_groups=mesh['z'=8,'yh'=4,'core'=2,'yl'=2,'x'=4] {'core'}, dimensions={0}, use_global_device_ids=true | all-gather | bytes 393216 | tf_op jit(solution)/shard_map/all_gather | solution.py:34
  74.7 0.1 broadcast_in_dim.16
  74.8 11.1 %all_to_all.31 = bf16[8,32,1024]{2,1,0:T(8,128)(2,1)S(1)} all-to-all(bf16[8,32,1024]{2,1,0:T(8,128)(2,1)S(1)} %broadcast_in_dim.16), channel_id=1, replica_groups=mesh['z'=8,'yh'=4,'core'=2,'yl'=2,'x'=4] {'yl','x'}, dimensions={0} | all-to-all | bytes 1048576 | tf_op jit(solution)/shard_map/all_to_all | solution.py:29
  85.9 1.3 convolution_convert_fusion.4
  87.3 6.3 %all-to-all-start.4 = ((bf16[32,8,768]{2,1,0:T(8,128)(2,1)}), bf16[32,8,768]{2,1,0:T(8,128)(2,1)S(1)}, u32[]{:S(2)}, u32[]{:S(2)}) async-start(bf16[32,8,768]{2,1,0:T(8,128)(2,1)} %bitcast.16), calls=%async_computation.4 | async-start | bytes 786432 | tf_op jit(solution)/shard_map/all_to_all | solution.py:23
  93.6 0.1 pad_maximum_fusion
  93.6 4.5 %collective-permute-start.1 = (bf16[256,1024]{1,0:T(8,128)(2,1)S(1)}, bf16[256,1024]{1,0:T(8,128)(2,1)S(1)}, u32[]{:S(2)}, u32[]{:S(2)}) collective-permute-start(bf16[256,1024]{1,0:T(8,128)(2,1)S(1)} %pad_maximum_fusion), channel_id=1, source_target_pairs={{0,8},{8,0},{1,9},{9,1},{2,10},{10,2},{3,11},{11,3},{4,12},{12,4},... | collective-permute-start | bytes 1572872 | tf_op jit(solution)/shard_map/ppermute | solution.py:193
  98.1 1.5 %collective-permute-done.1 = bf16[256,1024]{1,0:T(8,128)(2,1)S(1)} collective-permute-done((bf16[256,1024]{1,0:T(8,128)(2,1)S(1)}, bf16[256,1024]{1,0:T(8,128)(2,1)S(1)}, u32[]{:S(2)}, u32[]{:S(2)}) %collective-permute-start.1) | collective-permute-done | bytes 524320 | tf_op jit(solution)/shard_map/ppermute | solution.py:193
  99.6 1.1 fusion
  100.7 5.6 %all-to-all-done.4.blocks_ref = bf16[32,8,768]{2,1,0:T(8,128)(2,1)S(1)} async-done(((bf16[32,8,768]{2,1,0:T(8,128)(2,1)}), bf16[32,8,768]{2,1,0:T(8,128)(2,1)S(1)}, u32[]{:S(2)}, u32[]{:S(2)}) %all-to-all-start.4) | async-done | bytes 393248 | tf_op jit(solution)/shard_map/all_to_all | solution.py:23
  106.3 0.9 shard_map.113
  107.2 8.8 %all-to-all-start.5 = ((f32[32,8,128]{2,1,0:T(8,128)}), f32[32,8,128]{2,1,0:T(8,128)S(1)}, u32[]{:S(2)}, u32[]{:S(2)}) async-start(f32[32,8,128]{2,1,0:T(8,128)} %shard_map.113), calls=%async_computation.5 | async-start | bytes 262144 | tf_op jit(solution)/shard_map/all_to_all | solution.py:196
  116.0 1.1 fusion.1
  117.1 1.1 fusion.2
  118.2 9.1 %all-to-all-done.5.arrived_ref = f32[32,8,128]{2,1,0:T(8,128)S(1)} async-done(((f32[32,8,128]{2,1,0:T(8,128)}), f32[32,8,128]{2,1,0:T(8,128)S(1)}, u32[]{:S(2)}, u32[]{:S(2)}) %all-to-all-start.5) | async-done | bytes 131104 | tf_op jit(solution)/shard_map/all_to_all | solution.py:196
  127.3 0.2 shard_map.114
  127.5 3.6 %all-gather.2 = bf16[64,768]{1,0:T(8,128)(2,1)S(1)} all-gather(bf16[32,768]{1,0:T(8,128)(2,1)S(1)} %shard_map.114), channel_id=4, replica_groups=mesh['z'=8,'yh'=4,'core'=2,'yl'=2,'x'=4] {'core'}, dimensions={0}, use_global_device_ids=true | all-gather | bytes 147456 | tf_op jit(solution)/shard_map/all_gather | solution.py:34
  131.1 0.6 constant_dynamic-slice_fusion
  (9 shorter events, 0.1 us)
Async XLA Ops:
  0.6 2.5 %copy-start.2 = (bf16[1,256,768]{2,1,0:T(8,128)(2,1)S(1)}, bf16[1,256,768]{2,1,0:T(8,128)(2,1)}, u32[]{:S(2)}) copy-start(bf16[1,256,768]{2,1,0:T(8,128)(2,1)} %param.13) | copy-start | bytes 1179652
  1.9 10.2 %copy-start.3 = (bf16[16,768]{1,0:T(8,128)(2,1)S(1)}, bf16[16,768]{1,0:T(8,128)(2,1)}, u32[]{:S(2)}) copy-start(bf16[16,768]{1,0:T(8,128)(2,1)} %param.8) | copy-start | bytes 73732
  1.9 10.2 %copy-start.4 = (bf16[16,768]{1,0:T(8,128)(2,1)S(1)}, bf16[16,768]{1,0:T(8,128)(2,1)}, u32[]{:S(2)}) copy-start(bf16[16,768]{1,0:T(8,128)(2,1)} %param.7) | copy-start | bytes 73732
  1.9 12.1 %copy-start = (s32[1,256]{1,0:T(1,128)S(1)}, s32[1,256]{1,0:T(1,128)}, u32[]{:S(2)}) copy-start(s32[1,256]{1,0:T(1,128)} %slots_ref.3) | copy-start | bytes 3076
  1.9 23.4 %copy-start.1 = (f32[1,256]{1,0:T(1,128)S(1)}, f32[1,256]{1,0:T(1,128)}, u32[]{:S(2)}) copy-start(f32[1,256]{1,0:T(1,128)} %gates_ref.1) | copy-start | bytes 3076
  3.3 38.8 %collective-permute-start = (bf16[768,512]{0,1:T(8,128)(2,1)S(1)}, bf16[768,512]{0,1:T(8,128)(2,1)S(1)}, u32[]{:S(2)}, u32[]{:S(2)}) collective-permute-start(bf16[768,512]{0,1:T(8,128)(2,1)S(1)} %maximum_select_fusion.1), channel_id=1, source_target_pairs={{0,8},{8,0},{1,9},{9,1},{2,10},{10,2},{3,11},{11,3},{4,12},{12,4},... | collective-permute-start | bytes 2359304 | tf_op jit(solution)/shard_map/ppermute | solution.py:159
  15.0 21.7 %all-to-all-start = ((f32[32,8,128]{2,1,0:T(8,128)}), f32[32,8,128]{2,1,0:T(8,128)S(1)}, u32[]{:S(2)}, u32[]{:S(2)}) async-start(f32[32,8,128]{2,1,0:T(8,128)} %get-tuple-element.20), calls=%async_computation | async-start | bytes 262144 | tf_op jit(solution)/shard_map/all_to_all | solution.py:148
  37.6 19.3 %all-to-all-start.1 = ((bf16[32,8,768]{2,1,0:T(8,128)(2,1)}), bf16[32,8,768]{2,1,0:T(8,128)(2,1)S(1)}, u32[]{:S(2)}, u32[]{:S(2)}) async-start(bf16[32,8,768]{2,1,0:T(8,128)(2,1)} %shard_map.112), calls=%async_computation.1 | async-start | bytes 786432 | tf_op jit(solution)/shard_map/all_to_all | solution.py:166
  87.3 19.0 %all-to-all-start.4 = ((bf16[32,8,768]{2,1,0:T(8,128)(2,1)}), bf16[32,8,768]{2,1,0:T(8,128)(2,1)S(1)}, u32[]{:S(2)}, u32[]{:S(2)}) async-start(bf16[32,8,768]{2,1,0:T(8,128)(2,1)} %bitcast.16), calls=%async_computation.4 | async-start | bytes 786432 | tf_op jit(solution)/shard_map/all_to_all | solution.py:23
  93.6 6.0 %collective-permute-start.1 = (bf16[256,1024]{1,0:T(8,128)(2,1)S(1)}, bf16[256,1024]{1,0:T(8,128)(2,1)S(1)}, u32[]{:S(2)}, u32[]{:S(2)}) collective-permute-start(bf16[256,1024]{1,0:T(8,128)(2,1)S(1)} %pad_maximum_fusion), channel_id=1, source_target_pairs={{0,8},{8,0},{1,9},{9,1},{2,10},{10,2},{3,11},{11,3},{4,12},{12,4},... | collective-permute-start | bytes 1572872 | tf_op jit(solution)/shard_map/ppermute | solution.py:193
  107.2 20.2 %all-to-all-start.5 = ((f32[32,8,128]{2,1,0:T(8,128)}), f32[32,8,128]{2,1,0:T(8,128)S(1)}, u32[]{:S(2)}, u32[]{:S(2)}) async-start(f32[32,8,128]{2,1,0:T(8,128)} %shard_map.113), calls=%async_computation.5 | async-start | bytes 262144 | tf_op jit(solution)/shard_map/all_to_all | solution.py:196

commit v7 on v6

--- a/solution.py
+++ b/solution.py
@@ -90,7 +90,7 @@
     to_messages(dot(pick_ref[...], rows, ((0,), (0,))), out_ref)
 
 
-def find_slots(n_tok, slots_ref, gates_ref, place_ref, my_gates_ref):
+def find_slots(n_tok, slots_ref, gates_ref, place_ref, back_ref, fetch_ref, my_gates_ref):
     per_chip, n_chips = place_ref.shape
     n_slots = slots_ref.shape[1]
     chip = lax.axis_index("z") * lax.axis_size("yh") + lax.axis_index("yh")
@@ -106,6 +106,19 @@
     source = lax.broadcasted_iota(jnp.int32, (per_chip, n_chips), 1)
     place_ref[...] = jnp.where(lax.div(token, n_tok) == source, 1.0, 0.0).astype(BF16)
 
+    n_own, n_dev = n_tok // 2, back_ref.shape[1]
+    device = lax.broadcasted_iota(jnp.int32, (per_chip, n_dev), 1)
+    back_ref[...] = jnp.where(lax.div(token, n_own) == device, 1.0, 0.0).astype(BF16)
+    line = lax.broadcasted_iota(jnp.int32, (n_tok, n_slots), 0)
+    ids = (2 * chip + lax.axis_index("core")) * n_own + lax.rem(line, n_own)
+    row = jnp.broadcast_to(slots, (n_tok, n_slots))
+    rank = jnp.sum(jnp.where(row < ids, 1.0, 0.0), axis=1, keepdims=True).astype(jnp.int32)
+    held = jnp.sum(jnp.where(row == ids, 1.0, 0.0), axis=1, keepdims=True)
+    role = lax.div(lax.broadcasted_iota(jnp.int32, (n_tok, n_dev), 0), n_own)
+    peer = lax.broadcasted_iota(jnp.int32, (n_tok, n_dev), 1)
+    lane = jnp.where(held > 0.0, 2 * lax.rem(rank, n_chips), -2) + role
+    fetch_ref[...] = jnp.where((peer == lane) & (held > 0.0), 1.0, 0.0).astype(BF16)
+
 
 def receive_tokens(place_ref, gates_ref, arrived_ref, out_ref):
     rows = from_messages(arrived_ref, out_ref.shape[2] // LANES)
@@ -126,9 +139,12 @@
     to_messages(dot(place_ref[...], total, ((0,), (0,))), out_ref)
 
 
-def receive_slots(pick_ref, arrived_ref, out_ref):
-    rows = from_messages(arrived_ref, out_ref.shape[1] // LANES)
-    out_ref[...] = dot(pick_ref[...], rows, ((1,), (0,))).astype(BF16)
+def receive_slots(fetch_ref, arrived_ref, grad_ref, mixed_ref):
+    n_own = grad_ref.shape[0]
+    rows = from_messages(arrived_ref, grad_ref.shape[1] // LANES)
+    found = dot(fetch_ref[...], rows, ((1,), (0,))).astype(BF16)
+    grad_ref[...] = found[:n_own]
+    mixed_ref[...] = found[n_own:]
 
 
 def on_device(tokens, cotangent, slot_token, slot_gate, w_gate, w_up, w_down):
@@ -144,11 +160,16 @@
 
     slots = slot_token.reshape(1, -1)
     pairs = from_cores(jnp.concatenate([tokens, cotangent], axis=1))
-    sent, pick = on_vmem(send_tokens, ((blocks, F32), ((2 * n_own, n_chips), BF16)), slots, pairs)
+    sent, _ = on_vmem(send_tokens, ((blocks, F32), ((2 * n_own, n_chips), BF16)), slots, pairs)
     arrived = lax.all_to_all(sent, CHIPS, 0, 0, tiled=True)
-    place, my_gates = on_vmem(
+    place, to_owner, fetch, my_gates = on_vmem(
         functools.partial(find_slots, 2 * n_own),
-        (((per_chip, n_chips), BF16), ((per_chip, 1), F32)),
+        (
+            ((per_chip, n_chips), BF16),
+            ((per_chip, 2 * n_chips), BF16),
+            ((2 * n_own, 2 * n_chips), BF16),
+            ((per_chip, 1), F32),
+        ),
         slots,
         slot_gate.reshape(1, -1),
     )
@@ -192,17 +213,15 @@
     summands = exchange(total, CHIPS)
     other = lax.ppermute(jnp.concatenate([rows, factors[:, :n_ff]], axis=1), "core", [(0, 1), (1, 0)])
     factors, rows, other = lax.optimization_barrier((factors, rows, other))
-    (back,) = on_vmem(send_slots, ((blocks, F32),), place, my_gates, summands)
-    returned = lax.all_to_all(back, CHIPS, 0, 0, tiled=True)
-    (chip_out,) = on_vmem(receive_slots, (((2 * n_own, width), BF16),), pick, returned)
-    done = from_cores(chip_out)
-    grad_tokens = lax.dynamic_slice_in_dim(done[0], core * n_own, n_own, 0)
-    mixed = lax.dynamic_slice_in_dim(done[1], core * n_own, n_own, 0)
+    messages = (2 * n_chips, SEGMENTS, LANES)
+    (back,) = on_vmem(send_slots, ((messages, F32),), to_owner, my_gates, summands)
+    returned = lax.all_to_all(back.astype(BF16), DP, 0, 0, tiled=True).astype(F32)
+    grad_tokens, mixed = on_vmem(receive_slots, (((n_own, width), BF16),) * 2, fetch, returned)
 
     inputs = jnp.where(first, rows, other[:, :width])
     scaled = jnp.where(first, other[:, :width], rows)
     hidden = jnp.where(first, other[:, width:], factors[:, n_ff : 2 * n_ff])
-    grad_pre = lax.dynamic_slice_in_dim(factors, core * 2 * n_ff, 2 * n_ff, 1)
+    grad_pre = jnp.where(first, factors[:, : 2 * n_ff], factors[:, 2 * n_ff :])
     grad_down = dot(hidden, scaled, ((0,), (0,))).astype(BF16)
     grad_gate = dot(inputs, grad_pre[:, :n_ff], ((0,), (0,))).astype(BF16)
     grad_up = dot(inputs, grad_pre[:, n_ff:], ((0,), (0,))).astype(BF16)

time: 132 us -> 137 us (1.038)
  waiting for transfers between devices: 40.6 us -> 49.7 us
  blocking collectives: 33.7 us -> 30.1 us
    all_to_all x1, waiting for transfers between devices: 5.59 us -> 14.4 us  [exchange(): return lax.all_to_all(blocks, axes, 0, 0, tiled=True)]
    all_gather x3 -> x2, blocking collectives: 11.3 us -> 7.68 us  [from_cores(): return lax.all_gather(rows, 'core', axis=0, tiled=False)]
    all_to_all x1, waiting for transfers between devices: 9.14 us -> 10.9 us  [on_device(): lax.all_to_all(back.astype(BF16), DP, 0, 0, tiled=True).astype(F32)]
    ppermute x1, waiting for transfers between devices: 1.51 us -> 0.01 us  [on_device(): lax.ppermute(jnp.concatenate([rows, factors[:, :n_ff]], axis=1), 'core',...]
  transfers between devices with their start and end apart: 6 -> 6, of which waited for: 5 -> 4; matrix products, arithmetic and copies ran while one was open for 4% -> 3% of each run, Pallas kernels for 2% -> 2%
where the time goes in v7:
time: 137 us; the launch traced here: 136 us
  waiting for transfers between devices  49.7 us (36%)
  starting transfers between devices  42 us (31%)
  blocking collectives  30.1 us (22%)
  matrix products  5.15 us (4%)
  Pallas kernels  3.36 us (2%)
  local copies, waits for them, and re-layouts  2.53 us (2%)
  other arithmetic  2.52 us (2%)
    all_to_all x1, waiting for transfers between devices, exchange(): return lax.all_to_all(blocks, axes, 0, 0, tiled=True)  14.4 us
    all_to_all x1, waiting for transfers between devices, on_device(): rows = lax.all_to_all(copies, CHIPS, 0, 0, tiled=True)  13.4 us
    all_to_all x1, blocking collectives, exchange(): return lax.all_to_all(blocks, axes, 0, 0, tiled=True)  11.3 us
    all_to_all x1, blocking collectives, spread(): out = lax.all_to_all(blocks, axes, 0, 0, tiled=True)  11.1 us
    all_to_all x1, waiting for transfers between devices, on_device(): arrived = lax.all_to_all(sent, CHIPS, 0, 0, tiled=True)  11 us
    all_to_all x1, waiting for transfers between devices, on_device(): lax.all_to_all(back.astype(BF16), DP, 0, 0, tiled=True).astype(F32)  10.9 us
    all_to_all x1, starting transfers between devices, on_device(): arrived = lax.all_to_all(sent, CHIPS, 0, 0, tiled=True)  10.3 us
    ppermute x1, starting transfers between devices, on_device(): theirs = lax.ppermute(theirs, 'core', [(0, 1), (1, 0)])  8.75 us
  transfers between devices with their start and end apart: 6, of which 4 were waited for; matrix products, arithmetic and copies ran while one was open for 3% of the time, Pallas kernels for 2%

profile of v7, /device:TPU:1, one launch (start us, length us, event | category | flops | bytes accessed | tf_op | source)
XLA Modules:
  0.0 136.2 jit_solution(973191155683112512)
XLA Ops:
  0.6 0.0 copy-start.2
  0.6 1.2 copy.12
  1.9 0.0 copy-start.3
  1.9 0.0 copy-start.4
  1.9 0.0 copy-start
  1.9 0.0 copy-start.1
  1.9 1.2 copy.13
  3.1 0.0 copy-done.2
  3.1 0.2 maximum_select_fusion.1
  3.3 8.7 %collective-permute-start = (bf16[768,512]{0,1:T(8,128)(2,1)S(1)}, bf16[768,512]{0,1:T(8,128)(2,1)S(1)}, u32[]{:S(2)}, u32[]{:S(2)}) collective-permute-start(bf16[768,512]{0,1:T(8,128)(2,1)S(1)} %maximum_select_fusion.1), channel_id=1, source_target_pairs={{0,8},{8,0},{1,9},{9,1},{2,10},{10,2},{3,11},{11,3},{4,12},{12,4},... | collective-permute-start | bytes 2359304 | tf_op jit(solution)/shard_map/ppermute | solution.py:180
  12.0 0.0 copy-done.3
  12.1 0.0 copy-done.4
  12.1 1.9 %all-gather = bf16[32,1536]{1,0:T(8,128)(2,1)S(1)} all-gather(bf16[16,1536]{1,0:T(8,128)(2,1)S(1)} %pad_maximum_fusion.2), channel_id=2, replica_groups=mesh['z'=8,'yh'=4,'core'=2,'yl'=2,'x'=4] {'core'}, dimensions={0}, use_global_device_ids=true | all-gather | bytes 147456 | tf_op jit(solution)/shard_map/all_gather | solution.py:34
  14.0 0.0 copy-done
  14.0 1.0 shard_map.111
  15.0 10.3 %all-to-all-start = ((f32[32,8,128]{2,1,0:T(8,128)}), f32[32,8,128]{2,1,0:T(8,128)S(1)}, u32[]{:S(2)}, u32[]{:S(2)}) async-start(f32[32,8,128]{2,1,0:T(8,128)} %get-tuple-element.24), calls=%async_computation | async-start | bytes 262144 | tf_op jit(solution)/shard_map/all_to_all | solution.py:164
  25.3 0.0 copy-done.1
  25.4 0.3 shard_map.110
  25.6 11.0 %all-to-all-done.arrived_ref = f32[32,8,128]{2,1,0:T(8,128)S(1)} async-done(((f32[32,8,128]{2,1,0:T(8,128)}), f32[32,8,128]{2,1,0:T(8,128)S(1)}, u32[]{:S(2)}, u32[]{:S(2)}) %all-to-all-start) | async-done | bytes 131104 | tf_op jit(solution)/shard_map/all_to_all | solution.py:164
  36.7 0.9 shard_map.112
  37.6 4.5 %all-to-all-start.1 = ((bf16[32,8,768]{2,1,0:T(8,128)(2,1)}), bf16[32,8,768]{2,1,0:T(8,128)(2,1)S(1)}, u32[]{:S(2)}, u32[]{:S(2)}) async-start(bf16[32,8,768]{2,1,0:T(8,128)(2,1)} %shard_map.112), calls=%async_computation.1 | async-start | bytes 786432 | tf_op jit(solution)/shard_map/all_to_all | solution.py:187
  42.1 0.0 collective-permute-done
  42.1 1.4 %maximum_select_fusion = bf16[768,1024]{0,1:T(8,128)(2,1)S(1)} fusion(bf16[768,512]{0,1:T(8,128)(2,1)S(1)} %collective-permute-done, bf16[768,256]{0,1:T(8,128)(2,1)S(1)} %bitcast.88, bf16[768,256]{0,1:T(8,128)(2,1)S(1)} %bitcast.86, bf16[768,256]{0,1:T(8,128)(2,1)} %bitcast.94, bf16[768,256]{0,1:T(8,128)(2,1)S(1)} %slice.61, pred[]{:T(512)S(6)} %eq.3, ...), kind=kLoop, calls=%fused_computation | loop fusion | flops 10223616 | bytes 3934209 | tf_op jit(solution)/shard_map/jit(_where)/select_n | solution.py:181
  43.6 13.4 %all-to-all-done.1 = bf16[32,8,768]{2,1,0:T(8,128)(2,1)S(1)} async-done(((bf16[32,8,768]{2,1,0:T(8,128)(2,1)}), bf16[32,8,768]{2,1,0:T(8,128)(2,1)S(1)}, u32[]{:S(2)}, u32[]{:S(2)}) %all-to-all-start.1) | async-done | bytes 393248 | tf_op jit(solution)/shard_map/all_to_all | solution.py:187
  56.9 0.6 convolution_convert_fusion
  57.5 11.3 %all_to_all.30 = bf16[8,32,1024]{2,1,0:T(8,128)(2,1)S(1)} all-to-all(bf16[8,32,1024]{2,1,0:T(8,128)(2,1)S(1)} %bitcast.93), channel_id=1, replica_groups=mesh['z'=8,'yh'=4,'core'=2,'yl'=2,'x'=4] {'yl','x'}, dimensions={0} | all-to-all | bytes 1048576 | tf_op jit(solution)/shard_map/all_to_all | solution.py:23
  68.8 0.1 convert_reduce_fusion
  68.9 5.8 %all-gather.1 = f32[64,1024]{1,0:T(8,128)S(1)} all-gather(f32[32,1024]{1,0:T(8,128)S(1)} %convert_reduce_fusion), channel_id=3, replica_groups=mesh['z'=8,'yh'=4,'core'=2,'yl'=2,'x'=4] {'core'}, dimensions={0}, use_global_device_ids=true | all-gather | bytes 393216 | tf_op jit(solution)/shard_map/all_gather | solution.py:34
  74.8 0.1 broadcast_in_dim.16
  74.8 11.1 %all_to_all.31 = bf16[8,32,1024]{2,1,0:T(8,128)(2,1)S(1)} all-to-all(bf16[8,32,1024]{2,1,0:T(8,128)(2,1)S(1)} %broadcast_in_dim.16), channel_id=1, replica_groups=mesh['z'=8,'yh'=4,'core'=2,'yl'=2,'x'=4] {'yl','x'}, dimensions={0} | all-to-all | bytes 1048576 | tf_op jit(solution)/shard_map/all_to_all | solution.py:29
  85.9 1.3 convolution_convert_fusion.4
  87.3 0.1 pad_maximum_fusion
  87.3 4.2 %collective-permute-start.1 = (bf16[256,1024]{1,0:T(8,128)(2,1)S(1)}, bf16[256,1024]{1,0:T(8,128)(2,1)S(1)}, u32[]{:S(2)}, u32[]{:S(2)}) collective-permute-start(bf16[256,1024]{1,0:T(8,128)(2,1)S(1)} %pad_maximum_fusion), channel_id=1, source_target_pairs={{0,8},{8,0},{1,9},{9,1},{2,10},{10,2},{3,11},{11,3},{4,12},{12,4},... | collective-permute-start | bytes 1572872 | tf_op jit(solution)/shard_map/ppermute | solution.py:214
  91.5 6.3 %all-to-all-start.4 = ((bf16[32,8,768]{2,1,0:T(8,128)(2,1)}), bf16[32,8,768]{2,1,0:T(8,128)(2,1)S(1)}, u32[]{:S(2)}, u32[]{:S(2)}) async-start(bf16[32,8,768]{2,1,0:T(8,128)(2,1)} %bitcast.98), calls=%async_computation.4 | async-start | bytes 786432 | tf_op jit(solution)/shard_map/all_to_all | solution.py:23
  97.8 0.0 collective-permute-done.1
  97.9 1.1 fusion.1
  98.9 14.4 %all-to-all-done.4.blocks_ref = bf16[32,8,768]{2,1,0:T(8,128)(2,1)S(1)} async-done(((bf16[32,8,768]{2,1,0:T(8,128)(2,1)}), bf16[32,8,768]{2,1,0:T(8,128)(2,1)S(1)}, u32[]{:S(2)}, u32[]{:S(2)}) %all-to-all-start.4) | async-done | bytes 393248 | tf_op jit(solution)/shard_map/all_to_all | solution.py:23
  113.3 0.3 shard_map.113
  113.7 0.7 convert_element_type.51
  114.3 8.0 %all-to-all-start.5 = ((bf16[64,8,128]{2,1,0:T(8,128)(2,1)}), bf16[64,8,128]{2,1,0:T(8,128)(2,1)S(1)}, u32[]{:S(2)}, u32[]{:S(2)}) async-start(bf16[64,8,128]{2,1,0:T(8,128)(2,1)} %convert_element_type.51), calls=%async_computation.5 | async-start | bytes 262144 | tf_op jit(solution)/shard_map/all_to_all | solution.py:218
  122.3 1.1 fusion
  123.4 1.1 fusion.2
  124.5 10.9 %all-to-all-done.5 = bf16[64,8,128]{2,1,0:T(8,128)(2,1)S(1)} async-done(((bf16[64,8,128]{2,1,0:T(8,128)(2,1)}), bf16[64,8,128]{2,1,0:T(8,128)(2,1)S(1)}, u32[]{:S(2)}, u32[]{:S(2)}) %all-to-all-start.5) | async-done | bytes 131104 | tf_op jit(solution)/shard_map/all_to_all | solution.py:218
  135.4 0.8 shard_map.114
  (10 shorter events, 0.2 us)
Async XLA Ops:
  0.6 2.5 %copy-start.2 = (bf16[1,256,768]{2,1,0:T(8,128)(2,1)S(1)}, bf16[1,256,768]{2,1,0:T(8,128)(2,1)}, u32[]{:S(2)}) copy-start(bf16[1,256,768]{2,1,0:T(8,128)(2,1)} %param.13) | copy-start | bytes 1179652
  1.9 10.2 %copy-start.3 = (bf16[16,768]{1,0:T(8,128)(2,1)S(1)}, bf16[16,768]{1,0:T(8,128)(2,1)}, u32[]{:S(2)}) copy-start(bf16[16,768]{1,0:T(8,128)(2,1)} %param.8) | copy-start | bytes 73732
  1.9 10.2 %copy-start.4 = (bf16[16,768]{1,0:T(8,128)(2,1)S(1)}, bf16[16,768]{1,0:T(8,128)(2,1)}, u32[]{:S(2)}) copy-start(bf16[16,768]{1,0:T(8,128)(2,1)} %param.7) | copy-start | bytes 73732
  1.9 12.1 %copy-start = (s32[1,256]{1,0:T(1,128)S(1)}, s32[1,256]{1,0:T(1,128)}, u32[]{:S(2)}) copy-start(s32[1,256]{1,0:T(1,128)} %slots_ref.3) | copy-start | bytes 3076
  1.9 23.4 %copy-start.1 = (f32[1,256]{1,0:T(1,128)S(1)}, f32[1,256]{1,0:T(1,128)}, u32[]{:S(2)}) copy-start(f32[1,256]{1,0:T(1,128)} %gates_ref.1) | copy-start | bytes 3076
  3.3 38.8 %collective-permute-start = (bf16[768,512]{0,1:T(8,128)(2,1)S(1)}, bf16[768,512]{0,1:T(8,128)(2,1)S(1)}, u32[]{:S(2)}, u32[]{:S(2)}) collective-permute-start(bf16[768,512]{0,1:T(8,128)(2,1)S(1)} %maximum_select_fusion.1), channel_id=1, source_target_pairs={{0,8},{8,0},{1,9},{9,1},{2,10},{10,2},{3,11},{11,3},{4,12},{12,4},... | collective-permute-start | bytes 2359304 | tf_op jit(solution)/shard_map/ppermute | solution.py:180
  15.0 21.7 %all-to-all-start = ((f32[32,8,128]{2,1,0:T(8,128)}), f32[32,8,128]{2,1,0:T(8,128)S(1)}, u32[]{:S(2)}, u32[]{:S(2)}) async-start(f32[32,8,128]{2,1,0:T(8,128)} %get-tuple-element.24), calls=%async_computation | async-start | bytes 262144 | tf_op jit(solution)/shard_map/all_to_all | solution.py:164
  37.6 19.3 %all-to-all-start.1 = ((bf16[32,8,768]{2,1,0:T(8,128)(2,1)}), bf16[32,8,768]{2,1,0:T(8,128)(2,1)S(1)}, u32[]{:S(2)}, u32[]{:S(2)}) async-start(bf16[32,8,768]{2,1,0:T(8,128)(2,1)} %shard_map.112), calls=%async_computation.1 | async-start | bytes 786432 | tf_op jit(solution)/shard_map/all_to_all | solution.py:187
  87.3 10.5 %collective-permute-start.1 = (bf16[256,1024]{1,0:T(8,128)(2,1)S(1)}, bf16[256,1024]{1,0:T(8,128)(2,1)S(1)}, u32[]{:S(2)}, u32[]{:S(2)}) collective-permute-start(bf16[256,1024]{1,0:T(8,128)(2,1)S(1)} %pad_maximum_fusion), channel_id=1, source_target_pairs={{0,8},{8,0},{1,9},{9,1},{2,10},{10,2},{3,11},{11,3},{4,12},{12,4},... | collective-permute-start | bytes 1572872 | tf_op jit(solution)/shard_map/ppermute | solution.py:214
  91.5 21.8 %all-to-all-start.4 = ((bf16[32,8,768]{2,1,0:T(8,128)(2,1)}), bf16[32,8,768]{2,1,0:T(8,128)(2,1)S(1)}, u32[]{:S(2)}, u32[]{:S(2)}) async-start(bf16[32,8,768]{2,1,0:T(8,128)(2,1)} %bitcast.98), calls=%async_computation.4 | async-start | bytes 786432 | tf_op jit(solution)/shard_map/all_to_all | solution.py:23
  114.3 21.0 %all-to-all-start.5 = ((bf16[64,8,128]{2,1,0:T(8,128)(2,1)}), bf16[64,8,128]{2,1,0:T(8,128)(2,1)S(1)}, u32[]{:S(2)}, u32[]{:S(2)}) async-start(bf16[64,8,128]{2,1,0:T(8,128)(2,1)} %convert_element_type.51), calls=%async_computation.5 | async-start | bytes 262144 | tf_op jit(solution)/shard_map/all_to_all | solution.py:218

commit v8 on v6

--- a/solution.py
+++ b/solution.py
@@ -193,16 +193,16 @@
     other = lax.ppermute(jnp.concatenate([rows, factors[:, :n_ff]], axis=1), "core", [(0, 1), (1, 0)])
     factors, rows, other = lax.optimization_barrier((factors, rows, other))
     (back,) = on_vmem(send_slots, ((blocks, F32),), place, my_gates, summands)
-    returned = lax.all_to_all(back, CHIPS, 0, 0, tiled=True)
+    returned = lax.all_to_all(back.astype(BF16), CHIPS, 0, 0, tiled=True).astype(F32)
     (chip_out,) = on_vmem(receive_slots, (((2 * n_own, width), BF16),), pick, returned)
     done = from_cores(chip_out)
-    grad_tokens = lax.dynamic_slice_in_dim(done[0], core * n_own, n_own, 0)
-    mixed = lax.dynamic_slice_in_dim(done[1], core * n_own, n_own, 0)
+    grad_tokens = jnp.where(first, done[0, :n_own], done[0, n_own:])
+    mixed = jnp.where(first, done[1, :n_own], done[1, n_own:])
 
     inputs = jnp.where(first, rows, other[:, :width])
     scaled = jnp.where(first, other[:, :width], rows)
     hidden = jnp.where(first, other[:, width:], factors[:, n_ff : 2 * n_ff])
-    grad_pre = lax.dynamic_slice_in_dim(factors, core * 2 * n_ff, 2 * n_ff, 1)
+    grad_pre = jnp.where(first, factors[:, : 2 * n_ff], factors[:, 2 * n_ff :])
     grad_down = dot(hidden, scaled, ((0,), (0,))).astype(BF16)
     grad_gate = dot(inputs, grad_pre[:, :n_ff], ((0,), (0,))).astype(BF16)
     grad_up = dot(inputs, grad_pre[:, n_ff:], ((0,), (0,))).astype(BF16)

time: 132 us -> 137 us (1.038)
  waiting for transfers between devices: 40.6 us -> 47.9 us
  starting transfers between devices: 43.1 us -> 40.5 us
    all_to_all x1, waiting for transfers between devices: 5.59 us -> 13.3 us  [exchange(): return lax.all_to_all(blocks, axes, 0, 0, tiled=True)]
    all_to_all x1, starting transfers between devices: 8.84 us -> 6.48 us  [on_device(): lax.all_to_all(back.astype(BF16), CHIPS, 0, 0, tiled=True).astype(F32)]
    ppermute x1, waiting for transfers between devices: 1.51 us -> 0.01 us  [on_device(): lax.ppermute(jnp.concatenate([rows, factors[:, :n_ff]], axis=1), 'core',...]
  transfers between devices with their start and end apart: 6 -> 6, of which waited for: 5 -> 4; matrix products, arithmetic and copies ran while one was open for 4% -> 3% of each run, Pallas kernels for 2% -> 2%
where the time goes in v8:
time: 137 us
  waiting for transfers between devices  47.9 us (35%)
  starting transfers between devices  40.5 us (30%)
  blocking collectives  33.9 us (25%)
  matrix products  5.15 us (4%)
  other arithmetic  3.1 us (2%)
  Pallas kernels  2.6 us (2%)
  local copies, waits for them, and re-layouts  2.53 us (2%)
    all_to_all x1, waiting for transfers between devices, on_device(): rows = lax.all_to_all(copies, CHIPS, 0, 0, tiled=True)  13.4 us
    all_to_all x1, waiting for transfers between devices, exchange(): return lax.all_to_all(blocks, axes, 0, 0, tiled=True)  13.3 us
    all_gather x3, blocking collectives, from_cores(): return lax.all_gather(rows, 'core', axis=0, tiled=False)  11.5 us
    all_to_all x1, blocking collectives, exchange(): return lax.all_to_all(blocks, axes, 0, 0, tiled=True)  11.3 us
    all_to_all x1, blocking collectives, spread(): out = lax.all_to_all(blocks, axes, 0, 0, tiled=True)  11.1 us
    all_to_all x1, waiting for transfers between devices, on_device(): arrived = lax.all_to_all(sent, CHIPS, 0, 0, tiled=True)  11 us
    all_to_all x1, starting transfers between devices, on_device(): arrived = lax.all_to_all(sent, CHIPS, 0, 0, tiled=True)  10.3 us
    all_to_all x1, waiting for transfers between devices, on_device(): lax.all_to_all(back.astype(BF16), CHIPS, 0, 0, tiled=True).astype(F32)  10.2 us
  transfers between devices with their start and end apart: 6, of which 4 were waited for; matrix products, arithmetic and copies ran while one was open for 3% of the time, Pallas kernels for 2%

profile of v8, /device:TPU:1, one launch (start us, length us, event | category | flops | bytes accessed | tf_op | source)
XLA Modules:
  0.0 136.7 jit_solution(2087237485318583558)
XLA Ops:
  0.6 0.0 copy-start.2
  0.6 1.2 copy.12
  1.9 0.0 copy-start.3
  1.9 0.0 copy-start.4
  1.9 0.0 copy-start
  1.9 0.0 copy-start.1
  1.9 1.2 copy.13
  3.1 0.0 copy-done.2
  3.1 0.2 maximum_select_fusion.1
  3.3 8.7 %collective-permute-start = (bf16[768,512]{0,1:T(8,128)(2,1)S(1)}, bf16[768,512]{0,1:T(8,128)(2,1)S(1)}, u32[]{:S(2)}, u32[]{:S(2)}) collective-permute-start(bf16[768,512]{0,1:T(8,128)(2,1)S(1)} %maximum_select_fusion.1), channel_id=1, source_target_pairs={{0,8},{8,0},{1,9},{9,1},{2,10},{10,2},{3,11},{11,3},{4,12},{12,4},... | collective-permute-start | bytes 2359304 | tf_op jit(solution)/shard_map/ppermute | solution.py:159
  12.0 0.0 copy-done.3
  12.1 0.0 copy-done.4
  12.1 1.9 %all-gather = bf16[32,1536]{1,0:T(8,128)(2,1)S(1)} all-gather(bf16[16,1536]{1,0:T(8,128)(2,1)S(1)} %pad_maximum_fusion.2), channel_id=2, replica_groups=mesh['z'=8,'yh'=4,'core'=2,'yl'=2,'x'=4] {'core'}, dimensions={0}, use_global_device_ids=true | all-gather | bytes 147456 | tf_op jit(solution)/shard_map/all_gather | solution.py:34
  14.0 0.0 copy-done
  14.0 1.0 shard_map.110
  15.0 10.3 %all-to-all-start = ((f32[32,8,128]{2,1,0:T(8,128)}), f32[32,8,128]{2,1,0:T(8,128)S(1)}, u32[]{:S(2)}, u32[]{:S(2)}) async-start(f32[32,8,128]{2,1,0:T(8,128)} %get-tuple-element.20), calls=%async_computation | async-start | bytes 262144 | tf_op jit(solution)/shard_map/all_to_all | solution.py:148
  25.3 0.0 copy-done.1
  25.3 0.3 shard_map.111
  25.6 11.0 %all-to-all-done.arrived_ref = f32[32,8,128]{2,1,0:T(8,128)S(1)} async-done(((f32[32,8,128]{2,1,0:T(8,128)}), f32[32,8,128]{2,1,0:T(8,128)S(1)}, u32[]{:S(2)}, u32[]{:S(2)}) %all-to-all-start) | async-done | bytes 131104 | tf_op jit(solution)/shard_map/all_to_all | solution.py:148
  36.7 0.9 shard_map.112
  37.6 4.5 %all-to-all-start.1 = ((bf16[32,8,768]{2,1,0:T(8,128)(2,1)}), bf16[32,8,768]{2,1,0:T(8,128)(2,1)S(1)}, u32[]{:S(2)}, u32[]{:S(2)}) async-start(bf16[32,8,768]{2,1,0:T(8,128)(2,1)} %shard_map.112), calls=%async_computation.1 | async-start | bytes 786432 | tf_op jit(solution)/shard_map/all_to_all | solution.py:166
  42.1 0.0 collective-permute-done
  42.1 1.4 %maximum_select_fusion = bf16[768,1024]{0,1:T(8,128)(2,1)S(1)} fusion(bf16[768,512]{0,1:T(8,128)(2,1)S(1)} %collective-permute-done, bf16[768,256]{0,1:T(8,128)(2,1)S(1)} %bitcast.93, bf16[768,256]{0,1:T(8,128)(2,1)S(1)} %bitcast.91, bf16[768,256]{0,1:T(8,128)(2,1)} %bitcast.99, bf16[768,256]{0,1:T(8,128)(2,1)S(1)} %slice.77, pred[]{:T(512)S(6)} %eq.3, ...), kind=kLoop, calls=%fused_computation | loop fusion | flops 10223616 | bytes 3934209 | tf_op jit(solution)/shard_map/jit(_where)/select_n | solution.py:160
  43.6 13.4 %all-to-all-done.1 = bf16[32,8,768]{2,1,0:T(8,128)(2,1)S(1)} async-done(((bf16[32,8,768]{2,1,0:T(8,128)(2,1)}), bf16[32,8,768]{2,1,0:T(8,128)(2,1)S(1)}, u32[]{:S(2)}, u32[]{:S(2)}) %all-to-all-start.1) | async-done | bytes 393248 | tf_op jit(solution)/shard_map/all_to_all | solution.py:166
  56.9 0.6 convolution_convert_fusion
  57.5 11.3 %all_to_all.30 = bf16[8,32,1024]{2,1,0:T(8,128)(2,1)S(1)} all-to-all(bf16[8,32,1024]{2,1,0:T(8,128)(2,1)S(1)} %bitcast.98), channel_id=1, replica_groups=mesh['z'=8,'yh'=4,'core'=2,'yl'=2,'x'=4] {'yl','x'}, dimensions={0} | all-to-all | bytes 1048576 | tf_op jit(solution)/shard_map/all_to_all | solution.py:23
  68.8 0.1 convert_reduce_fusion
  68.9 5.8 %all-gather.1 = f32[64,1024]{1,0:T(8,128)S(1)} all-gather(f32[32,1024]{1,0:T(8,128)S(1)} %convert_reduce_fusion), channel_id=3, replica_groups=mesh['z'=8,'yh'=4,'core'=2,'yl'=2,'x'=4] {'core'}, dimensions={0}, use_global_device_ids=true | all-gather | bytes 393216 | tf_op jit(solution)/shard_map/all_gather | solution.py:34
  74.7 0.1 broadcast_in_dim.16
  74.8 11.1 %all_to_all.31 = bf16[8,32,1024]{2,1,0:T(8,128)(2,1)S(1)} all-to-all(bf16[8,32,1024]{2,1,0:T(8,128)(2,1)S(1)} %broadcast_in_dim.16), channel_id=1, replica_groups=mesh['z'=8,'yh'=4,'core'=2,'yl'=2,'x'=4] {'yl','x'}, dimensions={0} | all-to-all | bytes 1048576 | tf_op jit(solution)/shard_map/all_to_all | solution.py:29
  85.9 1.3 convolution_convert_fusion.4
  87.3 0.1 pad_maximum_fusion
  87.3 4.2 %collective-permute-start.1 = (bf16[256,1024]{1,0:T(8,128)(2,1)S(1)}, bf16[256,1024]{1,0:T(8,128)(2,1)S(1)}, u32[]{:S(2)}, u32[]{:S(2)}) collective-permute-start(bf16[256,1024]{1,0:T(8,128)(2,1)S(1)} %pad_maximum_fusion), channel_id=1, source_target_pairs={{0,8},{8,0},{1,9},{9,1},{2,10},{10,2},{3,11},{11,3},{4,12},{12,4},... | collective-permute-start | bytes 1572872 | tf_op jit(solution)/shard_map/ppermute | solution.py:193
  91.5 6.3 %all-to-all-start.4 = ((bf16[32,8,768]{2,1,0:T(8,128)(2,1)}), bf16[32,8,768]{2,1,0:T(8,128)(2,1)S(1)}, u32[]{:S(2)}, u32[]{:S(2)}) async-start(bf16[32,8,768]{2,1,0:T(8,128)(2,1)} %bitcast.103), calls=%async_computation.4 | async-start | bytes 786432 | tf_op jit(solution)/shard_map/all_to_all | solution.py:23
  97.8 0.0 collective-permute-done.1
  97.8 1.1 fusion.1
  98.9 1.1 fusion.2
  100.0 13.3 %all-to-all-done.4.blocks_ref = bf16[32,8,768]{2,1,0:T(8,128)(2,1)S(1)} async-done(((bf16[32,8,768]{2,1,0:T(8,128)(2,1)}), bf16[32,8,768]{2,1,0:T(8,128)(2,1)S(1)}, u32[]{:S(2)}, u32[]{:S(2)}) %all-to-all-start.4) | async-done | bytes 393248 | tf_op jit(solution)/shard_map/all_to_all | solution.py:23
  113.3 0.2 shard_map.113
  113.6 0.6 convert_element_type.51
  114.2 6.5 %all-to-all-start.5 = ((bf16[32,8,128]{2,1,0:T(8,128)(2,1)}), bf16[32,8,128]{2,1,0:T(8,128)(2,1)S(1)}, u32[]{:S(2)}, u32[]{:S(2)}) async-start(bf16[32,8,128]{2,1,0:T(8,128)(2,1)} %convert_element_type.51), calls=%async_computation.5 | async-start | bytes 131072 | tf_op jit(solution)/shard_map/all_to_all | solution.py:196
  120.7 1.1 fusion
  121.8 10.2 %all-to-all-done.5 = bf16[32,8,128]{2,1,0:T(8,128)(2,1)S(1)} async-done(((bf16[32,8,128]{2,1,0:T(8,128)(2,1)}), bf16[32,8,128]{2,1,0:T(8,128)(2,1)S(1)}, u32[]{:S(2)}, u32[]{:S(2)}) %all-to-all-start.5) | async-done | bytes 65568 | tf_op jit(solution)/shard_map/all_to_all | solution.py:196
  132.0 0.2 shard_map.114
  132.2 3.8 %all-gather.2 = bf16[64,768]{1,0:T(8,128)(2,1)S(1)} all-gather(bf16[32,768]{1,0:T(8,128)(2,1)S(1)} %shard_map.114), channel_id=4, replica_groups=mesh['z'=8,'yh'=4,'core'=2,'yl'=2,'x'=4] {'core'}, dimensions={0}, use_global_device_ids=true | all-gather | bytes 147456 | tf_op jit(solution)/shard_map/all_gather | solution.py:34
  136.0 0.6 fusion.12
  (10 shorter events, 0.2 us)
Async XLA Ops:
  0.6 2.5 %copy-start.2 = (bf16[1,256,768]{2,1,0:T(8,128)(2,1)S(1)}, bf16[1,256,768]{2,1,0:T(8,128)(2,1)}, u32[]{:S(2)}) copy-start(bf16[1,256,768]{2,1,0:T(8,128)(2,1)} %param.13) | copy-start | bytes 1179652
  1.9 10.2 %copy-start.3 = (bf16[16,768]{1,0:T(8,128)(2,1)S(1)}, bf16[16,768]{1,0:T(8,128)(2,1)}, u32[]{:S(2)}) copy-start(bf16[16,768]{1,0:T(8,128)(2,1)} %param.8) | copy-start | bytes 73732
  1.9 10.2 %copy-start.4 = (bf16[16,768]{1,0:T(8,128)(2,1)S(1)}, bf16[16,768]{1,0:T(8,128)(2,1)}, u32[]{:S(2)}) copy-start(bf16[16,768]{1,0:T(8,128)(2,1)} %param.7) | copy-start | bytes 73732
  1.9 12.1 %copy-start = (s32[1,256]{1,0:T(1,128)S(1)}, s32[1,256]{1,0:T(1,128)}, u32[]{:S(2)}) copy-start(s32[1,256]{1,0:T(1,128)} %slots_ref.3) | copy-start | bytes 3076
  1.9 23.4 %copy-start.1 = (f32[1,256]{1,0:T(1,128)S(1)}, f32[1,256]{1,0:T(1,128)}, u32[]{:S(2)}) copy-start(f32[1,256]{1,0:T(1,128)} %gates_ref.1) | copy-start | bytes 3076
  3.3 38.8 %collective-permute-start = (bf16[768,512]{0,1:T(8,128)(2,1)S(1)}, bf16[768,512]{0,1:T(8,128)(2,1)S(1)}, u32[]{:S(2)}, u32[]{:S(2)}) collective-permute-start(bf16[768,512]{0,1:T(8,128)(2,1)S(1)} %maximum_select_fusion.1), channel_id=1, source_target_pairs={{0,8},{8,0},{1,9},{9,1},{2,10},{10,2},{3,11},{11,3},{4,12},{12,4},... | collective-permute-start | bytes 2359304 | tf_op jit(solution)/shard_map/ppermute | solution.py:159
  15.0 21.7 %all-to-all-start = ((f32[32,8,128]{2,1,0:T(8,128)}), f32[32,8,128]{2,1,0:T(8,128)S(1)}, u32[]{:S(2)}, u32[]{:S(2)}) async-start(f32[32,8,128]{2,1,0:T(8,128)} %get-tuple-element.20), calls=%async_computation | async-start | bytes 262144 | tf_op jit(solution)/shard_map/all_to_all | solution.py:148
  37.6 19.3 %all-to-all-start.1 = ((bf16[32,8,768]{2,1,0:T(8,128)(2,1)}), bf16[32,8,768]{2,1,0:T(8,128)(2,1)S(1)}, u32[]{:S(2)}, u32[]{:S(2)}) async-start(bf16[32,8,768]{2,1,0:T(8,128)(2,1)} %shard_map.112), calls=%async_computation.1 | async-start | bytes 786432 | tf_op jit(solution)/shard_map/all_to_all | solution.py:166
  87.3 10.5 %collective-permute-start.1 = (bf16[256,1024]{1,0:T(8,128)(2,1)S(1)}, bf16[256,1024]{1,0:T(8,128)(2,1)S(1)}, u32[]{:S(2)}, u32[]{:S(2)}) collective-permute-start(bf16[256,1024]{1,0:T(8,128)(2,1)S(1)} %pad_maximum_fusion), channel_id=1, source_target_pairs={{0,8},{8,0},{1,9},{9,1},{2,10},{10,2},{3,11},{11,3},{4,12},{12,4},... | collective-permute-start | bytes 1572872 | tf_op jit(solution)/shard_map/ppermute | solution.py:193
  91.5 21.8 %all-to-all-start.4 = ((bf16[32,8,768]{2,1,0:T(8,128)(2,1)}), bf16[32,8,768]{2,1,0:T(8,128)(2,1)S(1)}, u32[]{:S(2)}, u32[]{:S(2)}) async-start(bf16[32,8,768]{2,1,0:T(8,128)(2,1)} %bitcast.103), calls=%async_computation.4 | async-start | bytes 786432 | tf_op jit(solution)/shard_map/all_to_all | solution.py:23
  114.2 17.8 %all-to-all-start.5 = ((bf16[32,8,128]{2,1,0:T(8,128)(2,1)}), bf16[32,8,128]{2,1,0:T(8,128)(2,1)S(1)}, u32[]{:S(2)}, u32[]{:S(2)}) async-start(bf16[32,8,128]{2,1,0:T(8,128)(2,1)} %convert_element_type.51), calls=%async_computation.5 | async-start | bytes 131072 | tf_op jit(solution)/shard_map/all_to_all | solution.py:196
